TPU v7x, 32 devices: a whole 2x2x4 slice. The times are simulated.
32 devices in a mesh: section: 2 (over core), gx: 4 (over z), gy: 4 (over y, x).
Axes of the slice: x: 2, y: 2, z: 4, core: 2. Of those that a mesh axis runs over, the one named last changes fastest.
Arguments:
- ends: bfloat16 [2, 32, 64, 64, 128], P('section', None, 'gx', 'gy'), may hold values from -9 to 9, as said below
- spectral_weight: bfloat16 [2, 32, 16, 32, 32, 32], P('section', 'gy', 'gx'), may hold values from -1 to 1
- point_weight: bfloat16 [2, 32, 32], P('section'), may hold values from -1 to 1
- point_bias: bfloat16 [2, 32], P('section'), may hold values from -3 to 3
Outputs:
- spectral_grad: float32 [2, 32, 16, 32, 32, 32], P('section', 'gy', 'gx')
- point_grad: float32 [2, 32, 32], P('section')
- bias_grad: float32 [2, 32], P('section')
Inputs may be any that keep to these rules, and one draw needn't show every extreme that they name: `ends`: both slots are fields of order one with a smooth part made of low modes inside the retained range and a rough part that varies from cell to cell.
All inputs are finite; a program needn't handle non-finite values.
Results may differ from a plain program's by a relative error of at most 0.014.
Values may be sent and summed in bfloat16 or wider, within the bound.
No kernel may reach another device: no remote copies, remote signals or barrier semaphores. Data moves between devices by JAX's collectives and lax.ppermute only.
A program may use at most 128 MiB of HBM per device.

v0:
```python
import math

import jax
import jax.numpy as jnp
import ml_dtypes
import numpy as np
from jax import lax
from jax.experimental import pallas as pl
from jax.experimental.pallas import tpu as pltpu
from jax.sharding import PartitionSpec as P

gelu_coef = 0.7978845608028654
f32 = jnp.float32
bf16 = jnp.bfloat16
AXES = ("section", "gx", "gy")


def table(length, count):
    half = count // 2
    modes = np.arange(count)
    is_cos = modes < half
    wave = np.where(is_cos, modes, modes - half + 1)
    phase = wave[:, None] * np.arange(length)[None, :] % length
    angle = phase.astype(np.float32) * np.float32(2.0 * math.pi / length)
    values = np.where(is_cos[:, None], np.cos(angle), np.sin(angle)).astype(np.float32)
    scale = np.where(is_cos & (wave == 0), math.sqrt(1.0 / length), math.sqrt(2.0 / length))
    return (values * scale.astype(np.float32)[:, None]).astype(ml_dtypes.bfloat16).astype(np.float32)


def nn(a, b):
    return lax.dot_general(a, b, (((1,), (0,)), ((), ())), preferred_element_type=f32)


def nt(a, b):
    return lax.dot_general(a, b, (((1,), (1,)), ((), ())), preferred_element_type=f32)


def tn(a, b):
    return lax.dot_general(a, b, (((0,), (0,)), ((), ())), preferred_element_type=f32)


def iota(shape, dim):
    return lax.broadcasted_iota(jnp.int32, shape, dim)


def vmem(n):
    return [pl.BlockSpec(memory_space=pltpu.VMEM)] * n


params = pltpu.CompilerParams(vmem_limit_bytes=56 * 1024 * 1024)
smem = pl.BlockSpec(memory_space=pltpu.SMEM)
hbm = pl.BlockSpec(memory_space=pl.ANY)


class Sizes:
    def __init__(self, ends, weight):
        self.n_gx = lax.axis_size("gx")
        self.n_gy = lax.axis_size("gy")
        _, self.chans, self.len_x, full, self.depth = ends.shape
        self.len_y = full // 2
        _, self.blk_j, self.blk_k, self.modes_y, _, _ = weight.shape
        self.half_j = self.blk_j // 2
        self.jk = self.half_j * self.blk_k
        self.places = 2 * self.n_gx * self.n_gy
        self.modes = self.places * self.jk
        self.rows = self.chans * self.len_y
        self.cells = self.len_x * self.depth
        self.lines = 2 * self.n_gy
        self.cpl = 128 // self.len_y
        self.groups = self.rows // 128
        self.lgs = self.modes_y // 8
        self.full_x = self.len_x * self.n_gx
        self.full_y = full * self.n_gy


def mode_tables(sz):
    bx = table(sz.full_x, sz.blk_j * sz.n_gy)
    bz = table(sz.depth, sz.blk_k * sz.n_gx)
    by = table(sz.full_y, sz.modes_y)
    sec, gx, gy, jj, kk = np.meshgrid(
        np.arange(2), np.arange(sz.n_gx), np.arange(sz.n_gy), np.arange(sz.half_j), np.arange(sz.blk_k), indexing="ij"
    )
    row_j = (gy * sz.blk_j + sec * sz.half_j + jj).reshape(-1)
    row_k = (gx * sz.blk_k + kk).reshape(-1)
    sec, gy, yy = np.meshgrid(np.arange(2), np.arange(sz.n_gy), np.arange(sz.len_y), indexing="ij")
    row_y = (gy * 2 * sz.len_y + sec * sz.len_y + yy).reshape(-1)
    return bx[row_j], bz[row_k], np.repeat(by[:, row_y].T, sz.cpl, axis=1)


def activate(pre):
    inner = gelu_coef * (pre + 0.044715 * pre * pre * pre)
    tanh_val = jnp.tanh(inner)
    value = 0.5 * pre * (1.0 + tanh_val)
    slope = 0.5 * (1.0 + tanh_val) + 0.5 * pre * (1.0 - tanh_val * tanh_val) * gelu_coef * (
        1.0 + 3.0 * 0.044715 * pre * pre
    )
    return value, slope


def spread(sz):
    shape = (sz.rows, sz.chans)
    return (iota(shape, 0) // sz.len_y == iota(shape, 1)).astype(bf16)


def same_y(sz):
    shape = (sz.rows, sz.rows)
    return iota(shape, 0) % sz.len_y == iota(shape, 1) % sz.len_y


def point_matrix(sz, weight, forward):
    one = spread(sz)
    part = nt(one, weight) if forward else nn(one, weight)
    full = nt(part.astype(bf16), one)
    return jnp.where(same_y(sz), full, 0.0).astype(bf16)


def swapped(rows, half):
    return jnp.concatenate([rows[half:], rows[:half]], axis=0)


def send_analysis(sz, bb_ref, field, out_ref, layer):
    out = nt(bb_ref[...], field).astype(bf16)
    out_ref[...] = swapped(out, sz.modes // 2) if layer == 1 else out


def first_kernel(sz, s_ref, keep_ref, recv_ref, bx_ref, bz_ref, by_ref, bb_ref, ya_ref, out_ref):
    depth = sz.depth
    for x in range(sz.len_x):
        bb_ref[:, x * depth : (x + 1) * depth] = (bx_ref[:, x : x + 1] * bz_ref[...]).astype(bf16)
    wide = sz.modes_y * sz.cpl
    lane_c = iota((sz.len_y, wide), 1) % sz.cpl
    for g in range(sz.lines):
        part = by_ref[g * sz.len_y : (g + 1) * sz.len_y, :]
        block = jnp.concatenate([jnp.where(lane_c == c, part, 0.0) for c in range(sz.cpl)], axis=0)
        ya_ref[g * 128 : (g + 1) * 128, :] = block.astype(bf16)
    field = jnp.where(s_ref[0] == 0, keep_ref[...], recv_ref[...])
    send_analysis(sz, bb_ref, field, out_ref, 0)


def first_call(sz, s, keep, recv, bx, bz, by):
    return pl.pallas_call(
        lambda *refs: first_kernel(sz, *refs),
        out_shape=(
            jax.ShapeDtypeStruct((sz.modes, sz.cells), bf16),
            jax.ShapeDtypeStruct((sz.lines * 128, sz.modes_y * sz.cpl), bf16),
            jax.ShapeDtypeStruct((sz.modes, sz.rows), bf16),
        ),
        in_specs=[smem] + vmem(5),
        out_specs=tuple(vmem(3)),
        compiler_params=params,
        name="first",
    )(s, keep, recv, bx, bz, by)


def line_analysis(sz, r_ref, ya_ref):
    jk = sz.jk
    lines = []
    for sec in range(2):
        for gy in range(sz.n_gy):
            total = None
            for gx in range(sz.n_gx):
                at = ((sec * sz.n_gx + gx) * sz.n_gy + gy) * jk
                part = r_ref[at : at + jk, :].astype(f32)
                total = part if total is None else total + part
            lines.append(total.astype(bf16))
    halves = [
        jnp.concatenate([line[:, h * 128 : (h + 1) * 128] for line in lines], axis=1) for h in range(sz.groups)
    ]
    return nn(jnp.concatenate(halves, axis=0), ya_ref[...]).astype(bf16)


def diagonal(sz, count):
    shape = (count, sz.groups * 128)
    return iota(shape, 0) % 8 == (iota(shape, 1) % 128) // sz.cpl


def row_spread(sz):
    shape = (sz.jk * 8, sz.jk)
    return (iota(shape, 0) // 8 == iota(shape, 1)).astype(bf16)


def row_gather(sz):
    shape = (sz.jk, sz.jk * 8)
    return (iota(shape, 1) // 8 == iota(shape, 0)).astype(bf16)


def chan_lanes(sz):
    shape = (sz.groups * 128, sz.chans)
    lane = iota(shape, 0)
    return ((lane // 128) * sz.cpl + lane % sz.cpl == iota(shape, 1)).astype(bf16)


def to_blocks(sz, rows, lg):
    jk = sz.jk
    wide = jnp.concatenate(
        [rows[h * jk : (h + 1) * jk, lg * 128 : (lg + 1) * 128] for h in range(sz.groups)], axis=1
    )
    return jnp.where(diagonal(sz, jk * 8), nn(row_spread(sz), wide), 0.0)


def from_blocks(sz, blocks):
    jk = sz.jk
    pieces = []
    for block in blocks:
        kept = jnp.where(diagonal(sz, jk * 8), block, 0.0).astype(bf16)
        pieces.append(nn(row_gather(sz), kept).astype(bf16))
    return jnp.concatenate(
        [
            jnp.concatenate([piece[:, h * 128 : (h + 1) * 128] for piece in pieces], axis=1)
            for h in range(sz.groups)
        ],
        axis=0,
    )


def send_lines(sz, rows, ya_ref, out_ref):
    jk = sz.jk
    lines = nt(rows, ya_ref[...]).astype(bf16)
    for sec in range(2):
        for gy in range(sz.n_gy):
            line = sec * sz.n_gy + gy
            block = jnp.concatenate(
                [lines[h * jk : (h + 1) * jk, line * 128 : (line + 1) * 128] for h in range(sz.groups)], axis=1
            )
            for gx in range(sz.n_gx):
                at = ((sec * sz.n_gx + gx) * sz.n_gy + gy) * jk
                out_ref[at : at + jk, :] = block


def weight_block(sz, w_ref, jk, lg, h):
    jj, kk = jk // sz.blk_k, jk % sz.blk_k
    part = w_ref[jj, kk, lg * 8 : (lg + 1) * 8, h * sz.cpl : (h + 1) * sz.cpl, :]
    return part.reshape(128, sz.chans)


def mix_kernel(sz, layer, turn, s_ref, r_ref, ya_ref, own_ref, other_ref, spec_ref, out_ref, w_ref, blk_ref, mix_ref, sem):
    own = pltpu.make_async_copy(own_ref.at[0, pl.ds(0, sz.half_j)], w_ref, sem)
    other = pltpu.make_async_copy(other_ref, w_ref, sem)

    @pl.when(s_ref[0] == layer)
    def _():
        own.start()

    @pl.when(s_ref[0] != layer)
    def _():
        other.start()

    spec = line_analysis(sz, r_ref, ya_ref)
    spec_ref[...] = spec
    count = sz.jk * 8
    for lg in range(sz.lgs):
        blk_ref[lg * count : (lg + 1) * count, :] = to_blocks(sz, spec, lg)
    if turn:
        flat = nn(blk_ref[...].astype(bf16), chan_lanes(sz))
        blk_ref[:, : sz.chans] = flat
    other.wait()
    for lg in range(sz.lgs):
        for jk in range(sz.jk):
            at = (lg * sz.jk + jk) * 8
            if turn:
                left = blk_ref[at : at + 8, : sz.chans].astype(bf16)
                for h in range(sz.groups):
                    mix_ref[at : at + 8, h * 128 : (h + 1) * 128] = nt(left, weight_block(sz, w_ref, jk, lg, h))
            else:
                left = blk_ref[at : at + 8, :].astype(bf16)
                total = None
                for h in range(sz.groups):
                    part = nn(left[:, h * 128 : (h + 1) * 128], weight_block(sz, w_ref, jk, lg, h))
                    total = part if total is None else total + part
                mix_ref[at : at + 8, : sz.chans] = total
    blocks = []
    for lg in range(sz.lgs):
        if turn:
            blocks.append(mix_ref[lg * count : (lg + 1) * count, :])
        else:
            blocks.append(nt(mix_ref[lg * count : (lg + 1) * count, : sz.chans].astype(bf16), chan_lanes(sz)))
    send_lines(sz, from_blocks(sz, blocks), ya_ref, out_ref)


def mix_call(sz, layer, turn, s, r, ya, own, other):
    count = sz.jk * 8 * sz.lgs
    return pl.pallas_call(
        lambda *refs: mix_kernel(sz, layer, turn, *refs),
        out_shape=(
            jax.ShapeDtypeStruct((sz.groups * sz.jk, sz.modes_y * sz.cpl), bf16),
            jax.ShapeDtypeStruct((sz.modes, sz.rows), bf16),
        ),
        in_specs=[smem] + vmem(2) + [hbm, hbm],
        out_specs=tuple(vmem(2)),
        scratch_shapes=[
            pltpu.VMEM((sz.half_j, sz.blk_k, sz.modes_y, sz.chans, sz.chans), bf16),
            pltpu.VMEM((count, sz.groups * 128), f32),
            pltpu.VMEM((count, sz.groups * 128), f32),
            pltpu.SemaphoreType.DMA,
        ],
        compiler_params=params,
        name="mix",
    )(s, r, ya, own, other)


def spec_kernel(sz, r_ref, ya_ref, out_ref):
    out_ref[...] = line_analysis(sz, r_ref, ya_ref)


def spec_call(sz, r, ya):
    return pl.pallas_call(
        lambda *refs: spec_kernel(sz, *refs),
        out_shape=jax.ShapeDtypeStruct((sz.groups * sz.jk, sz.modes_y * sz.cpl), bf16),
        in_specs=vmem(2),
        out_specs=vmem(1)[0],
        compiler_params=params,
        name="spec",
    )(r, ya)


def turned_modes(sz, u_ref, layer):
    left = jnp.transpose(u_ref[...])
    half = sz.modes // 2
    if layer == 1:
        left = jnp.concatenate([left[:, half:], left[:, :half]], axis=1)
    return left


CHUNK = 256


def small_parts(sz, s_ref, own_ref, other_ref, layer):
    chosen = jnp.where(s_ref[0] == layer, own_ref[...].astype(f32), other_ref[...].astype(f32)).astype(bf16)
    return chosen[: sz.chans], chosen[sz.chans :]


def forward_kernel(sz, s_ref, keep_ref, recv_ref, u_ref, bb_ref, own_ref, other_ref, v_ref, slope_ref, out_ref):
    weight, bias = small_parts(sz, s_ref, own_ref, other_ref, 0)
    matrix = point_matrix(sz, weight, True)
    column = nt(spread(sz), bias)[:, :1]
    left = turned_modes(sz, u_ref, 0)
    for at in range(0, sz.cells, CHUNK):
        cut = slice(at, at + CHUNK)
        field = jnp.where(s_ref[0] == 0, keep_ref[:, cut], recv_ref[:, cut])
        pre = nn(left, bb_ref[:, cut]) + nn(matrix, field) + column
        value, slope = activate(pre)
        v_ref[:, cut] = value.astype(bf16)
        slope_ref[:, cut] = slope
    send_analysis(sz, bb_ref, v_ref[...], out_ref, 1)


def forward_call(sz, s, keep, recv, u, bb, own, other):
    return pl.pallas_call(
        lambda *refs: forward_kernel(sz, *refs),
        out_shape=(
            jax.ShapeDtypeStruct((sz.rows, sz.cells), bf16),
            jax.ShapeDtypeStruct((sz.rows, sz.cells), f32),
            jax.ShapeDtypeStruct((sz.modes, sz.rows), bf16),
        ),
        in_specs=[smem] + vmem(6),
        out_specs=tuple(vmem(3)),
        compiler_params=params,
        name="forward",
    )(s, keep, recv, u, bb, own, other)


def turn_kernel(sz, s_ref, keep_ref, recv_ref, v_ref, u_ref, bb_ref, own_ref, other_ref, d_ref, out_ref):
    weight, bias = small_parts(sz, s_ref, own_ref, other_ref, 1)
    matrix = point_matrix(sz, weight, True)
    column = nt(spread(sz), bias)[:, :1]
    left = turned_modes(sz, u_ref, 1)
    for at in range(0, sz.cells, CHUNK):
        cut = slice(at, at + CHUNK)
        grad = jnp.where(s_ref[0] == 0, recv_ref[:, cut], keep_ref[:, cut]).astype(f32)
        pre = nn(left, bb_ref[:, cut]) + nn(matrix, v_ref[:, cut]) + column
        _, slope = activate(pre)
        d_ref[:, cut] = (grad * slope).astype(bf16)
    send_analysis(sz, bb_ref, d_ref[...], out_ref, 1)


def turn_call(sz, s, keep, recv, v, u, bb, own, other):
    return pl.pallas_call(
        lambda *refs: turn_kernel(sz, *refs),
        out_shape=(
            jax.ShapeDtypeStruct((sz.rows, sz.cells), bf16),
            jax.ShapeDtypeStruct((sz.modes, sz.rows), bf16),
        ),
        in_specs=[smem] + vmem(7),
        out_specs=tuple(vmem(2)),
        compiler_params=params,
        name="turn",
    )(s, keep, recv, v, u, bb, own, other)


def back_kernel(sz, s_ref, d_ref, slope_ref, u_ref, bb_ref, own_ref, other_ref, new_ref, out_ref):
    weight, _ = small_parts(sz, s_ref, own_ref, other_ref, 1)
    matrix = point_matrix(sz, weight, False)
    left = turned_modes(sz, u_ref, 1)
    for at in range(0, sz.cells, CHUNK):
        cut = slice(at, at + CHUNK)
        grad = (nn(left, bb_ref[:, cut]) + nn(matrix, d_ref[:, cut])).astype(bf16).astype(f32)
        new_ref[:, cut] = (grad * slope_ref[:, cut]).astype(bf16)
    send_analysis(sz, bb_ref, new_ref[...], out_ref, 0)


def back_call(sz, s, d, slope, u, bb, own, other):
    return pl.pallas_call(
        lambda *refs: back_kernel(sz, *refs),
        out_shape=(
            jax.ShapeDtypeStruct((sz.rows, sz.cells), bf16),
            jax.ShapeDtypeStruct((sz.modes, sz.rows), bf16),
        ),
        in_specs=[smem] + vmem(6),
        out_specs=tuple(vmem(2)),
        compiler_params=params,
        name="back",
    )(s, d, slope, u, bb, own, other)


def point_kernel(sz, field, d_ref, out_ref):
    d = d_ref[...]
    pairs = jnp.where(same_y(sz), nt(field, d), 0.0)
    pairs = jnp.sum(pairs.reshape(sz.chans, sz.len_y, sz.rows), axis=1)
    ones = jnp.ones((8, sz.cells), bf16)
    bias = nt(ones, d)
    part = sz.chans // 4
    total = None
    for t in range(4):
        shape = (sz.rows, 128)
        place = (iota(shape, 0) // sz.len_y + t * sz.chans == iota(shape, 1)).astype(f32)
        both = pairs[t * part : (t + 1) * part]
        if t == 0:
            both = jnp.concatenate([both, bias], axis=0)
        else:
            both = jnp.concatenate([both, jnp.zeros_like(bias)], axis=0)
        term = lax.dot_general(
            both, place, (((1,), (0,)), ((), ())), precision=lax.Precision.HIGHEST, preferred_element_type=f32
        )
        total = term if total is None else total + term
    out_ref[...] = total


def point0_kernel(sz, s_ref, keep_ref, recv_ref, d_ref, out_ref):
    field = jnp.where(s_ref[0] == 0, keep_ref[...], recv_ref[...])
    point_kernel(sz, field, d_ref, out_ref)


def point1_kernel(sz, v_ref, d_ref, out_ref):
    point_kernel(sz, v_ref[...], d_ref, out_ref)


def point_call(sz, kernel, specs, *args):
    return pl.pallas_call(
        lambda *refs: kernel(sz, *refs),
        out_shape=jax.ShapeDtypeStruct((sz.chans // 4 + 8, 128), f32),
        in_specs=specs,
        out_specs=vmem(1)[0],
        compiler_params=params,
        name="point",
    )(*args)


def outer_kernel(sz, sv_ref, su_ref, out_ref):
    jk, groups, kk_count = sz.jk, sz.groups, sz.blk_k
    sv = sv_ref[0]
    su = su_ref[0]
    shape = (kk_count * 8, kk_count)
    one = (iota(shape, 0) // 8 == iota(shape, 1)).astype(bf16)
    diag = diagonal(sz, kk_count * 8)
    for lg in range(sz.lgs):
        cut = slice(lg * 128, (lg + 1) * 128)

        def block(rows):
            wide = jnp.concatenate([rows[h * kk_count : (h + 1) * kk_count, cut] for h in range(groups)], axis=1)
            return jnp.where(diag, nn(one, wide), 0.0)

        left = block(sv)
        right = nn(block(su).astype(bf16), chan_lanes(sz))
        for kk in range(kk_count):
            res = tn(left[kk * 8 : (kk + 1) * 8].astype(bf16), right[kk * 8 : (kk + 1) * 8].astype(bf16))
            for h in range(groups):
                out_ref[0, 0, kk, lg * 8 : (lg + 1) * 8, h * sz.cpl : (h + 1) * sz.cpl, :] = res[
                    h * 128 : (h + 1) * 128
                ].reshape(8, sz.cpl, sz.chans)


def outer_call(sz, sv, su):
    wide = sz.modes_y * sz.cpl
    rows = sz.groups * sz.blk_k
    return pl.pallas_call(
        lambda *refs: outer_kernel(sz, *refs),
        grid=(sz.blk_j,),
        out_shape=jax.ShapeDtypeStruct(
            (1, sz.blk_j, sz.blk_k, sz.modes_y, sz.chans, sz.chans), f32
        ),
        in_specs=[pl.BlockSpec((1, rows, wide), lambda i: (i, 0, 0))] * 2,
        out_specs=pl.BlockSpec(
            (1, 1, sz.blk_k, sz.modes_y, sz.chans, sz.chans), lambda i: (0, i, 0, 0, 0, 0)
        ),
        compiler_params=params,
        name="outer",
    )(sv, su)


def exchange(block):
    return lax.all_to_all(block, AXES, split_axis=0, concat_axis=0, tiled=True)


def swap(block):
    return lax.ppermute(block, "section", [(0, 1), (1, 0)])


def local(ends, spectral_weight, point_weight, point_bias):
    sz = Sizes(ends, spectral_weight)
    section = lax.axis_index("section")
    first = section == 0
    s = section.astype(jnp.int32).reshape(1)
    bx, bz, by = mode_tables(sz)
    bx = lax.dynamic_slice_in_dim(jnp.asarray(bx), lax.axis_index("gx") * sz.len_x, sz.len_x, axis=1)

    def half(which):
        part = lax.dynamic_slice_in_dim(ends[0], which * sz.len_y, sz.len_y, axis=2)
        return jnp.swapaxes(part, 1, 2).reshape(sz.rows, sz.cells)

    recv = swap(half(1 - section))
    keep = half(section)
    own_small = jnp.concatenate(
        [point_weight[0], jnp.broadcast_to(point_bias, (16, sz.chans))], axis=0
    )
    other_small = swap(own_small)
    other_weight = swap(spectral_weight[0, sz.half_j :])

    bb, ya, out = first_call(sz, s, keep, recv, bx, jnp.asarray(bz), jnp.asarray(by))
    sv0, out = mix_call(sz, 0, False, s, exchange(out), ya, spectral_weight, other_weight)
    v1, slope0, out = forward_call(sz, s, keep, recv, exchange(out), bb, own_small, other_small)
    sv1, out = mix_call(sz, 1, False, s, exchange(out), ya, spectral_weight, other_weight)
    d1, out = turn_call(sz, s, keep, recv, v1, exchange(out), bb, own_small, other_small)
    su1, out = mix_call(sz, 1, True, s, exchange(out), ya, spectral_weight, other_weight)
    d0, out = back_call(sz, s, d1, slope0, exchange(out), bb, own_small, other_small)
    su0 = spec_call(sz, exchange(out), ya)
    pg1 = point_call(sz, point1_kernel, vmem(2), v1, d1)
    pg0 = point_call(sz, point0_kernel, [smem] + vmem(3), s, keep, recv, d0)

    half_places = sz.places // 2
    sums = jnp.concatenate(
        [jnp.broadcast_to(pg0, (half_places,) + pg0.shape), jnp.broadcast_to(pg1, (half_places,) + pg1.shape)]
    )
    sums = jnp.sum(lax.all_to_all(sums, AXES, split_axis=0, concat_axis=0, tiled=True), axis=0)
    part = sz.chans // 4
    point_grad = jnp.swapaxes(sums[:part].reshape(part, 4, sz.chans), 0, 1).reshape(1, sz.chans, sz.chans)
    bias_grad = sums[part : part + 1, : sz.chans]

    def both(own, other):
        mine = jnp.where(first, own, other)
        theirs = swap(jnp.where(first, other, own))
        full = jnp.stack([mine, theirs]).reshape(2, sz.groups, sz.half_j, sz.blk_k, -1)
        return jnp.swapaxes(full, 1, 2).reshape(sz.blk_j, sz.groups * sz.blk_k, -1)

    spectral_grad = outer_call(sz, both(sv0, sv1), both(su0, su1))
    return (spectral_grad, point_grad, bias_grad)


def solution(mesh):
    return jax.shard_map(
        local,
        mesh=mesh,
        in_specs=(
            P("section", None, "gx", "gy", None),
            P("section", "gy", "gx", None, None, None),
            P("section", None, None),
            P("section", None),
        ),
        out_specs=(
            P("section", "gy", "gx", None, None, None),
            P("section", None, None),
            P("section", None),
        ),
        check_vma=False,
    )
```

profile of v0, /device:TPU:0, one launch (start us, length us, event | category | flops | bytes accessed | tf_op | source)
XLA Modules:
  0.0 188.3 jit_solution(9748903826557027214)
XLA Ops:
  0.6 2.8 %dynamic-slice_bitcast_fusion = (bf16[256,2048]{1,0:T(8,128)(2,1)S(1)}, bf16[256,2048]{1,0:T(8,128)(2,1)}) fusion(bf16[1,32,16,16,128]{4,3,2,1,0:T(8,128)(2,1)} %param.7, s32[]{:T(128)S(6)} %select_n.31, s32[]{:T(128)S(6)} %select_n.30), kind=kLoop, calls=%fused_computation.1 | loop fusion | bytes 4194312 | tf_op jit(solution)/shard_map/reshape | solution.py:518
  3.9 5.1 %slice_bitcast_fusion = bf16[4,4,32,32,32]{4,3,2,1,0:T(8,128)(2,1)} fusion(bf16[1,8,4,32,32,32]{5,4,3,2,1,0:T(8,128)(2,1)} %refs_3_.5), kind=kLoop, calls=%fused_computation | loop fusion | bytes 2097152 | tf_op jit(solution)/shard_map/squeeze | solution.py:526
  9.1 0.8 constant_dynamic-slice_fusion.refs_3_
  10.0 1.0 copy-done
  11.0 4.8 %first.1 = (bf16[512,2048]{1,0:T(8,128)(2,1)}, bf16[1024,512]{1,0:T(8,128)(2,1)}, bf16[512,256]{1,0:T(8,128)(2,1)}) custom-call(s32[1]{0:T(128)} %bitcast.refs_0_, bf16[256,2048]{1,0:T(8,128)(2,1)} %get-tuple-element.36.refs_1_, bf16[256,2048]{1,0:T(8,128)(2,1)} %copy-done, f32[512,16]{1,0:T(8,128)} %constant_dynamic-slice_fusion.refs_3_, ...), custom_call_target="tpu_custom_call" | custom-call | tf_op jit(solution)/shard_map/first/pallas_call | solution.py:141
  15.8 7.3 %all-to-all-start = ((bf16[32,16,256]{2,1,0:T(8,128)(2,1)}), bf16[32,16,256]{2,1,0:T(8,128)(2,1)S(1)}, u32[]{:S(2)}, u32[]{:S(2)}) async-start(bf16[32,16,256]{2,1,0:T(8,128)(2,1)} %bitcast.48), calls=%async_computation | async-start | bytes 524288 | tf_op jit(solution)/shard_map/all_to_all | solution.py:501
  23.0 11.2 %all-to-all-done = bf16[32,16,256]{2,1,0:T(8,128)(2,1)S(1)} async-done(((bf16[32,16,256]{2,1,0:T(8,128)(2,1)}), bf16[32,16,256]{2,1,0:T(8,128)(2,1)S(1)}, u32[]{:S(2)}, u32[]{:S(2)}) %all-to-all-start) | async-done | bytes 262176 | tf_op jit(solution)/shard_map/all_to_all | solution.py:501
  34.9 6.0 %mix.3 = (bf16[32,512]{1,0:T(8,128)(2,1)}, bf16[512,256]{1,0:T(8,128)(2,1)}) custom-call(s32[1]{0:T(128)} %bitcast.refs_0_, bf16[512,256]{1,0:T(8,128)(2,1)} %bitcast.40, bf16[1024,512]{1,0:T(8,128)(2,1)} %get-tuple-element.20.refs_2_.refs_1_, bf16[1,8,4,32,32,32]{5,4,3,2,1,0:T(8,128)(2,1)} %refs_3_.5, bf16[4,4,32,32,32]{4,3,2,1,0:T(8,128)(2,1)} %collective-permute-done.1.refs_4_), custom_call_target="tpu_custom_call" | custom-call | tf_op jit(solution)/shard_map/mix/pallas_call | solution.py:282
  41.0 2.6 %all-to-all-start.1 = ((bf16[32,16,256]{2,1,0:T(8,128)(2,1)}), bf16[32,16,256]{2,1,0:T(8,128)(2,1)S(1)}, u32[]{:S(2)}, u32[]{:S(2)}) async-start(bf16[32,16,256]{2,1,0:T(8,128)(2,1)} %bitcast.47), calls=%async_computation.1 | async-start | bytes 524288 | tf_op jit(solution)/shard_map/all_to_all | solution.py:501
  43.8 1.1 collective-permute-done.2.refs_6_.refs_7_
  44.9 9.9 %all-to-all-done.1 = bf16[32,16,256]{2,1,0:T(8,128)(2,1)S(1)} async-done(((bf16[32,16,256]{2,1,0:T(8,128)(2,1)}), bf16[32,16,256]{2,1,0:T(8,128)(2,1)S(1)}, u32[]{:S(2)}, u32[]{:S(2)}) %all-to-all-start.1) | async-done | bytes 262176 | tf_op jit(solution)/shard_map/all_to_all | solution.py:501
  55.5 6.4 %forward.1 = (bf16[256,2048]{1,0:T(8,128)(2,1)}, f32[256,2048]{1,0:T(8,128)}, bf16[512,256]{1,0:T(8,128)(2,1)}) custom-call(s32[1]{0:T(128)} %bitcast.refs_0_, bf16[256,2048]{1,0:T(8,128)(2,1)} %get-tuple-element.36.refs_1_, bf16[256,2048]{1,0:T(8,128)(2,1)} %copy-done, bf16[512,256]{1,0:T(8,128)(2,1)} %bitcast.39, ...), custom_call_target="tpu_custom_call" | custom-call | tf_op jit(solution)/shard_map/forward/pallas_call | solution.py:348
  61.9 14.5 %all_to_all.82 = bf16[32,16,256]{2,1,0:T(8,128)(2,1)} all-to-all(bf16[32,16,256]{2,1,0:T(8,128)(2,1)} %bitcast.49), channel_id=1, replica_groups=mesh['section'=2,'gx'=4,'gy'=4] {'section','gx','gy'}, dimensions={0} | all-to-all | bytes 524288 | tf_op jit(solution)/shard_map/all_to_all | solution.py:501
  76.4 6.0 %mix.4 = (bf16[32,512]{1,0:T(8,128)(2,1)}, bf16[512,256]{1,0:T(8,128)(2,1)}) custom-call(s32[1]{0:T(128)} %bitcast.refs_0_, bf16[512,256]{1,0:T(8,128)(2,1)} %bitcast.43, bf16[1024,512]{1,0:T(8,128)(2,1)} %get-tuple-element.20.refs_2_.refs_1_, bf16[1,8,4,32,32,32]{5,4,3,2,1,0:T(8,128)(2,1)} %refs_3_.5, bf16[4,4,32,32,32]{4,3,2,1,0:T(8,128)(2,1)} %collective-permute-done.1.refs_4_), custom_call_target="tpu_custom_call" | custom-call | tf_op jit(solution)/shard_map/mix/pallas_call | solution.py:282
  82.4 14.5 %all_to_all.83 = bf16[32,16,256]{2,1,0:T(8,128)(2,1)} all-to-all(bf16[32,16,256]{2,1,0:T(8,128)(2,1)} %bitcast.51), channel_id=1, replica_groups=mesh['section'=2,'gx'=4,'gy'=4] {'section','gx','gy'}, dimensions={0} | all-to-all | bytes 524288 | tf_op jit(solution)/shard_map/all_to_all | solution.py:501
  96.9 6.3 %turn.1 = (bf16[256,2048]{1,0:T(8,128)(2,1)}, bf16[512,256]{1,0:T(8,128)(2,1)}) custom-call(s32[1]{0:T(128)} %bitcast.refs_0_, bf16[256,2048]{1,0:T(8,128)(2,1)} %get-tuple-element.36.refs_1_, bf16[256,2048]{1,0:T(8,128)(2,1)} %copy-done, bf16[256,2048]{1,0:T(8,128)(2,1)} %get-tuple-element.26.refs_3_.refs_0_, bf16[512,256]{1,0:T(8,128)(2,1)} %bitcast.44, ...), custom_call_target="tpu_custom_call" | custom-call | tf_op jit(solution)/shard_map/turn/pallas_call | solution.py:377
  103.2 14.5 %all_to_all.84 = bf16[32,16,256]{2,1,0:T(8,128)(2,1)} all-to-all(bf16[32,16,256]{2,1,0:T(8,128)(2,1)} %bitcast.52), channel_id=1, replica_groups=mesh['section'=2,'gx'=4,'gy'=4] {'section','gx','gy'}, dimensions={0} | all-to-all | bytes 524288 | tf_op jit(solution)/shard_map/all_to_all | solution.py:501
  117.7 7.0 %mix.5 = (bf16[32,512]{1,0:T(8,128)(2,1)}, bf16[512,256]{1,0:T(8,128)(2,1)}) custom-call(s32[1]{0:T(128)} %bitcast.refs_0_, bf16[512,256]{1,0:T(8,128)(2,1)} %bitcast.42, bf16[1024,512]{1,0:T(8,128)(2,1)} %get-tuple-element.20.refs_2_.refs_1_, bf16[1,8,4,32,32,32]{5,4,3,2,1,0:T(8,128)(2,1)} %refs_3_.5, bf16[4,4,32,32,32]{4,3,2,1,0:T(8,128)(2,1)} %collective-permute-done.1.refs_4_), custom_call_target="tpu_custom_call" | custom-call | tf_op jit(solution)/shard_map/mix/pallas_call | solution.py:282
  124.7 14.5 %all_to_all.85 = bf16[32,16,256]{2,1,0:T(8,128)(2,1)} all-to-all(bf16[32,16,256]{2,1,0:T(8,128)(2,1)} %bitcast.50), channel_id=1, replica_groups=mesh['section'=2,'gx'=4,'gy'=4] {'section','gx','gy'}, dimensions={0} | all-to-all | bytes 524288 | tf_op jit(solution)/shard_map/all_to_all | solution.py:501
  139.2 5.0 %back.1 = (bf16[256,2048]{1,0:T(8,128)(2,1)}, bf16[512,256]{1,0:T(8,128)(2,1)}) custom-call(s32[1]{0:T(128)} %bitcast.refs_0_, bf16[256,2048]{1,0:T(8,128)(2,1)} %get-tuple-element.28.refs_1_, f32[256,2048]{1,0:T(8,128)} %get-tuple-element.29.refs_2_, bf16[512,256]{1,0:T(8,128)(2,1)} %bitcast.41, bf16[512,2048]{1,0:T(8,128)(2,1)} %get-tuple-element.23.refs_4_.refs_5_, ...), custom_call_target="tpu_custom_call" | custom-call | tf_op jit(solution)/shard_map/back/pallas_call | solution.py:402
  144.2 2.7 %all-to-all-start.6 = ((bf16[32,16,256]{2,1,0:T(8,128)(2,1)}), bf16[32,16,256]{2,1,0:T(8,128)(2,1)S(1)}, u32[]{:S(2)}, u32[]{:S(2)}) async-start(bf16[32,16,256]{2,1,0:T(8,128)(2,1)} %bitcast.46), calls=%async_computation.6 | async-start | bytes 524288 | tf_op jit(solution)/shard_map/all_to_all | solution.py:501
  146.9 3.2 %point.3 = f32[16,128]{1,0:T(8,128)} custom-call(bf16[256,2048]{1,0:T(8,128)(2,1)} %get-tuple-element.26.refs_3_.refs_0_, bf16[256,2048]{1,0:T(8,128)(2,1)} %get-tuple-element.28.refs_1_), custom_call_target="tpu_custom_call" | custom-call | tf_op jit(solution)/shard_map/point/pallas_call | solution.py:448
  150.2 3.5 %point.2 = f32[16,128]{1,0:T(8,128)} custom-call(s32[1]{0:T(128)} %bitcast.refs_0_, bf16[256,2048]{1,0:T(8,128)(2,1)} %get-tuple-element.36.refs_1_, bf16[256,2048]{1,0:T(8,128)(2,1)} %copy-done, bf16[256,2048]{1,0:T(8,128)(2,1)} %get-tuple-element.34.refs_3_), custom_call_target="tpu_custom_call" | custom-call | tf_op jit(solution)/shard_map/point/pallas_call | solution.py:448
  154.4 0.7 broadcast_in_dim.16
  155.2 0.7 pad_maximum_fusion
  155.9 2.3 %all-to-all-done.6 = bf16[32,16,256]{2,1,0:T(8,128)(2,1)S(1)} async-done(((bf16[32,16,256]{2,1,0:T(8,128)(2,1)}), bf16[32,16,256]{2,1,0:T(8,128)(2,1)S(1)}, u32[]{:S(2)}, u32[]{:S(2)}) %all-to-all-start.6) | async-done | bytes 262176 | tf_op jit(solution)/shard_map/all_to_all | solution.py:501
  158.1 3.6 %all-to-all-start.7 = ((f32[32,16,128]{2,1,0:T(8,128)}), f32[32,16,128]{2,1,0:T(8,128)S(1)}, u32[]{:S(2)}, u32[]{:S(2)}) async-start(f32[32,16,128]{2,1,0:T(8,128)} %pad_maximum_fusion), calls=%async_computation.7 | async-start | bytes 524288 | tf_op jit(solution)/shard_map/all_to_all | solution.py:543
  162.1 0.9 collective-permute-done.3
  163.0 2.2 %spec.1 = bf16[32,512]{1,0:T(8,128)(2,1)} custom-call(bf16[512,256]{1,0:T(8,128)(2,1)} %bitcast.45, bf16[1024,512]{1,0:T(8,128)(2,1)} %get-tuple-element.20.refs_2_.refs_1_), custom_call_target="tpu_custom_call" | custom-call | tf_op jit(solution)/shard_map/spec/pallas_call | solution.py:306
  165.3 0.8 broadcast_select_fusion.1
  167.0 6.0 %all-to-all-done.7 = f32[32,16,128]{2,1,0:T(8,128)S(1)} async-done(((f32[32,16,128]{2,1,0:T(8,128)}), f32[32,16,128]{2,1,0:T(8,128)S(1)}, u32[]{:S(2)}, u32[]{:S(2)}) %all-to-all-start.7) | async-done | bytes 262176 | tf_op jit(solution)/shard_map/all_to_all | solution.py:543
  174.9 13.4 %outer.1 = f32[1,8,4,32,32,32]{5,4,3,2,1,0:T(8,128)} custom-call(bf16[8,8,512]{2,1,0:T(8,128)(2,1)} %reshape.56.refs_0_, bf16[8,8,512]{2,1,0:T(8,128)(2,1)} %reshape.57.refs_1_), custom_call_target="tpu_custom_call" | custom-call | tf_op jit(solution)/shard_map/outer/pallas_call | solution.py:485
  (48 shorter events, 6.1 us)
Async XLA Ops:
  3.4 5.7 %copy-start.4 = (f32[512,64]{1,0:T(8,128)S(1)}, f32[512,64]{1,0:T(8,128)}, u32[]{:S(2)}) copy-start(f32[512,64]{1,0:T(8,128)} %constant.31.clone) | copy-start | bytes 393220
  3.4 6.5 %collective-permute-start = (bf16[256,2048]{1,0:T(8,128)(2,1)S(1)}, bf16[256,2048]{1,0:T(8,128)(2,1)S(1)}, u32[]{:S(2)}, u32[]{:S(2)}) collective-permute-start(bf16[256,2048]{1,0:T(8,128)(2,1)S(1)} %get-tuple-element.35), channel_id=1, source_target_pairs={{0,16},{16,0},{1,17},{17,1},{2,18},{18,2},{3,19},{19,3},{4,20},{20... | collective-permute-start | bytes 3145736 | tf_op jit(solution)/shard_map/ppermute | solution.py:505
  9.0 14.0 %collective-permute-start.1 = (bf16[4,4,32,32,32]{4,3,2,1,0:T(8,128)(2,1)}, bf16[4,4,32,32,32]{4,3,2,1,0:T(8,128)(2,1)}, u32[]{:S(2)}, u32[]{:S(2)}) collective-permute-start(bf16[4,4,32,32,32]{4,3,2,1,0:T(8,128)(2,1)} %slice_bitcast_fusion), channel_id=1, source_target_pairs={{0,16},{16,0},{1,17},{17,1},{2,18},{18,2},{3,19},{19,3},{4,20},{20... | collective-permute-start | bytes 3145736 | tf_op jit(solution)/shard_map/ppermute | solution.py:505
  10.0 1.0 copy-start
  15.8 18.5 %all-to-all-start = ((bf16[32,16,256]{2,1,0:T(8,128)(2,1)}), bf16[32,16,256]{2,1,0:T(8,128)(2,1)S(1)}, u32[]{:S(2)}, u32[]{:S(2)}) async-start(bf16[32,16,256]{2,1,0:T(8,128)(2,1)} %bitcast.48), calls=%async_computation | async-start | bytes 524288 | tf_op jit(solution)/shard_map/all_to_all | solution.py:501
  34.2 0.7 copy-start.2
  34.9 8.6 %copy-start.11 = (bf16[1,32]{1,0:T(2,128)(2,1)S(1)}, bf16[1,32]{1,0:T(2,128)(2,1)}, u32[]{:S(2)}) copy-start(bf16[1,32]{1,0:T(2,128)(2,1)} %param.10) | copy-start | bytes 196
  34.9 8.6 %copy-start.10 = (bf16[1,32,32]{2,1,0:T(8,128)(2,1)S(1)}, bf16[1,32,32]{2,1,0:T(8,128)(2,1)}, u32[]{:S(2)}) copy-start(bf16[1,32,32]{2,1,0:T(8,128)(2,1)} %param.9) | copy-start | bytes 6148
  41.0 13.8 %all-to-all-start.1 = ((bf16[32,16,256]{2,1,0:T(8,128)(2,1)}), bf16[32,16,256]{2,1,0:T(8,128)(2,1)S(1)}, u32[]{:S(2)}, u32[]{:S(2)}) async-start(bf16[32,16,256]{2,1,0:T(8,128)(2,1)} %bitcast.47), calls=%async_computation.1 | async-start | bytes 524288 | tf_op jit(solution)/shard_map/all_to_all | solution.py:501
  43.6 11.2 %copy-start.5 = (bf16[48,32]{1,0:T(8,128)(2,1)}, bf16[48,32]{1,0:T(8,128)(2,1)S(1)}, u32[]{:S(2)}) copy-start(bf16[48,32]{1,0:T(8,128)(2,1)S(1)} %pad_maximum_fusion.3.refs_5_.refs_6_) | copy-start | bytes 9220
  43.6 1.2 collective-permute-start.2
  44.9 9.9 %copy-start.6 = (bf16[48,32]{1,0:T(8,128)(2,1)}, bf16[48,32]{1,0:T(8,128)(2,1)S(1)}, u32[]{:S(2)}) copy-start(bf16[48,32]{1,0:T(8,128)(2,1)S(1)} %collective-permute-done.2.refs_6_.refs_7_) | copy-start | bytes 9220
  54.8 0.7 copy-start.1
  144.2 17.5 %copy-start.7 = (bf16[32,512]{1,0:T(8,128)(2,1)S(1)}, bf16[32,512]{1,0:T(8,128)(2,1)}, u32[]{:S(2)}) copy-start(bf16[32,512]{1,0:T(8,128)(2,1)} %get-tuple-element.21) | copy-start | bytes 98308
  144.2 17.5 %copy-start.9 = (bf16[32,512]{1,0:T(8,128)(2,1)S(1)}, bf16[32,512]{1,0:T(8,128)(2,1)}, u32[]{:S(2)}) copy-start(bf16[32,512]{1,0:T(8,128)(2,1)} %get-tuple-element.25) | copy-start | bytes 98308
  144.2 13.9 %all-to-all-start.6 = ((bf16[32,16,256]{2,1,0:T(8,128)(2,1)}), bf16[32,16,256]{2,1,0:T(8,128)(2,1)S(1)}, u32[]{:S(2)}, u32[]{:S(2)}) async-start(bf16[32,16,256]{2,1,0:T(8,128)(2,1)} %bitcast.46), calls=%async_computation.6 | async-start | bytes 524288 | tf_op jit(solution)/shard_map/all_to_all | solution.py:501
  146.9 18.3 %copy-start.8 = (bf16[32,512]{1,0:T(8,128)(2,1)S(1)}, bf16[32,512]{1,0:T(8,128)(2,1)}, u32[]{:S(2)}) copy-start(bf16[32,512]{1,0:T(8,128)(2,1)} %get-tuple-element.33) | copy-start | bytes 98308
  158.1 4.9 %copy-start.3 = (bf16[32,16,256]{2,1,0:T(8,128)(2,1)}, bf16[32,16,256]{2,1,0:T(8,128)(2,1)S(1)}, u32[]{:S(2)}) copy-start(bf16[32,16,256]{2,1,0:T(8,128)(2,1)S(1)} %all-to-all-done.6) | copy-start | bytes 786436
  158.1 14.8 %all-to-all-start.7 = ((f32[32,16,128]{2,1,0:T(8,128)}), f32[32,16,128]{2,1,0:T(8,128)S(1)}, u32[]{:S(2)}, u32[]{:S(2)}) async-start(f32[32,16,128]{2,1,0:T(8,128)} %pad_maximum_fusion), calls=%async_computation.7 | async-start | bytes 524288 | tf_op jit(solution)/shard_map/all_to_all | solution.py:543
  161.8 1.3 collective-permute-start.3
  166.0 8.2 %collective-permute-start.4 = (bf16[32,512]{1,0:T(8,128)(2,1)S(1)}, bf16[32,512]{1,0:T(8,128)(2,1)S(1)}, u32[]{:S(2)}, u32[]{:S(2)}) collective-permute-start(bf16[32,512]{1,0:T(8,128)(2,1)S(1)} %get-tuple-element.38), channel_id=1, source_target_pairs={{0,16},{16,0},{1,17},{17,1},{2,18},{18,2},{3,19},{19,3},{4,20},{20... | collective-permute-start | bytes 98312 | tf_op jit(solution)/shard_map/ppermute | solution.py:505
where the time goes:
time: 189 us; the launch traced here: 188 us
  Pallas kernels  63.8 us (34%)
  blocking collectives  58 us (31%)
  waiting for transfers between devices  31.4 us (17%)
  starting transfers between devices  17.4 us (9%)
  local copies, waits for them, and re-layouts  15.2 us (8%)
    all_to_all x4, blocking collectives, exchange(): return lax.all_to_all(block, AXES, split_axis=0, concat_axis=0, tiled=True)  58 us
    all_to_all x3, waiting for transfers between devices, exchange(): return lax.all_to_all(block, AXES, split_axis=0, concat_axis=0, tiled=True)  23.4 us
    pallas_call x3, Pallas kernels, mix_call(): pl.pallas_call(lambda *refs: mix_kernel(sz, layer, turn, *refs), out_shap...  19 us
    pallas_call x1, Pallas kernels, outer_call(): pl.pallas_call(lambda *refs: outer_kernel(sz, *refs), grid=(sz.blk_j,), o...  13.4 us
    all_to_all x3, starting transfers between devices, exchange(): return lax.all_to_all(block, AXES, split_axis=0, concat_axis=0, tiled=True)  12.6 us
    pallas_call x2, Pallas kernels, point_call(): pl.pallas_call(lambda *refs: kernel(sz, *refs), out_shape=jax.ShapeDtypeS...  6.78 us
    pallas_call x1, Pallas kernels, forward_call(): pl.pallas_call(lambda *refs: forward_kernel(sz, *refs), out_shape=(jax.Sh...  6.41 us
    pallas_call x1, Pallas kernels, turn_call(): pl.pallas_call(lambda *refs: turn_kernel(sz, *refs), out_shape=(jax.Shape...  6.29 us
  transfers between devices with their start and end apart: 9, of which 6 were waited for; matrix products, arithmetic and copies ran while one was open for 6% of the time, Pallas kernels for 7%

commit v1 on v0

v1 whole, which is shorter than its diff:
```python
import math

import jax
import jax.numpy as jnp
import ml_dtypes
import numpy as np
from jax import lax
from jax.experimental import pallas as pl
from jax.experimental.pallas import tpu as pltpu
from jax.sharding import PartitionSpec as P

gelu_coef = 0.7978845608028654
f32 = jnp.float32
bf16 = jnp.bfloat16
AXES = ("section", "gx", "gy")


def table(length, count):
    half = count // 2
    modes = np.arange(count)
    is_cos = modes < half
    wave = np.where(is_cos, modes, modes - half + 1)
    phase = wave[:, None] * np.arange(length)[None, :] % length
    angle = phase.astype(np.float32) * np.float32(2.0 * math.pi / length)
    values = np.where(is_cos[:, None], np.cos(angle), np.sin(angle)).astype(np.float32)
    scale = np.where(is_cos & (wave == 0), math.sqrt(1.0 / length), math.sqrt(2.0 / length))
    return (values * scale.astype(np.float32)[:, None]).astype(ml_dtypes.bfloat16).astype(np.float32)


def nn(a, b):
    return lax.dot_general(a, b, (((1,), (0,)), ((), ())), preferred_element_type=f32)


def nt(a, b):
    return lax.dot_general(a, b, (((1,), (1,)), ((), ())), preferred_element_type=f32)


def tn(a, b):
    return lax.dot_general(a, b, (((0,), (0,)), ((), ())), preferred_element_type=f32)


def iota(shape, dim):
    return lax.broadcasted_iota(jnp.int32, shape, dim)


limit = 24 * 1024 * 1024
smem = pl.BlockSpec(memory_space=pltpu.SMEM)
hbm = pl.BlockSpec(memory_space=pltpu.HBM)
vmem = pl.BlockSpec(memory_space=pltpu.VMEM)


def shape(dims, dtype=bf16):
    return jax.ShapeDtypeStruct(dims, dtype)


def kept(dims, dtype=bf16):
    return pltpu.VMEM(dims, dtype)


def near(value):
    return pltpu.with_memory_space_constraint(value, pltpu.VMEM)


def far(value):
    return pltpu.with_memory_space_constraint(value, pltpu.HBM)


def run(name, kernel, outs, specs, args, scratch=(), copies=0, micros=1):
    return pl.pallas_call(
        kernel,
        out_shape=tuple(pltpu.HBM(o.shape, o.dtype) if away else o for o, away in outs),
        in_specs=list(specs),
        out_specs=tuple(hbm if away else vmem for _, away in outs),
        scratch_shapes=list(scratch) + ([pltpu.SemaphoreType.DMA((copies,))] if copies else []),
        compiler_params=pltpu.CompilerParams(vmem_limit_bytes=limit),
        cost_estimate=pl.CostEstimate(flops=0, transcendentals=0, bytes_accessed=micros * 3000000),
        name=name,
    )(*[far(a) if spec is hbm else a for a, spec in zip(args, specs)])


class Copies:
    def __init__(self, sems):
        self.sems = sems
        self.used = 0
        self.open = []

    def make(self, src, dst):
        copy = pltpu.make_async_copy(src, dst, self.sems.at[self.used])
        self.used += 1
        return copy

    def start(self, src, dst):
        copy = self.make(src, dst)
        copy.start()
        return copy

    def choose(self, pick, triples):
        firsts, others = [], []
        for src, other, dst in triples:
            firsts.append(pltpu.make_async_copy(src, dst, self.sems.at[self.used]))
            others.append(self.make(other, dst))

        @pl.when(pick)
        def _():
            for copy in firsts:
                copy.start()

        @pl.when(jnp.logical_not(pick))
        def _():
            for copy in others:
                copy.start()

        return others

    def send(self, src, dst):
        self.open.append(self.start(src, dst))

    def finish(self):
        for copy in self.open:
            copy.wait()


class Sizes:
    def __init__(self, ends, weight):
        self.n_gx = lax.axis_size("gx")
        self.n_gy = lax.axis_size("gy")
        _, self.chans, self.len_x, full, self.depth = ends.shape
        self.len_y = full // 2
        _, self.blk_j, self.blk_k, self.modes_y, _, _ = weight.shape
        self.half_j = self.blk_j // 2
        self.jk = self.half_j * self.blk_k
        self.places = 2 * self.n_gx * self.n_gy
        self.modes = self.places * self.jk
        self.rows = self.chans * self.len_y
        self.cells = self.len_x * self.depth
        self.lines = 2 * self.n_gy
        self.cpl = 128 // self.len_y
        self.groups = self.rows // 128
        self.lgs = self.modes_y // 8
        self.full_x = self.len_x * self.n_gx
        self.full_y = full * self.n_gy


def mode_tables(sz):
    bx = table(sz.full_x, sz.blk_j * sz.n_gy)
    bz = table(sz.depth, sz.blk_k * sz.n_gx)
    by = table(sz.full_y, sz.modes_y)
    sec, gx, gy, jj, kk = np.meshgrid(
        np.arange(2), np.arange(sz.n_gx), np.arange(sz.n_gy), np.arange(sz.half_j), np.arange(sz.blk_k), indexing="ij"
    )
    row_j = (gy * sz.blk_j + sec * sz.half_j + jj).reshape(-1)
    row_k = (gx * sz.blk_k + kk).reshape(-1)
    sec, gy, yy = np.meshgrid(np.arange(2), np.arange(sz.n_gy), np.arange(sz.len_y), indexing="ij")
    row_y = (gy * 2 * sz.len_y + sec * sz.len_y + yy).reshape(-1)
    bx = np.moveaxis(bx[row_j].reshape(sz.modes, sz.n_gx, sz.len_x), 1, 0)
    return bx, bz[row_k], np.repeat(by[:, row_y].T, sz.cpl, axis=1)


def activate(pre):
    inner = gelu_coef * (pre + 0.044715 * pre * pre * pre)
    tanh_val = jnp.tanh(inner)
    value = 0.5 * pre * (1.0 + tanh_val)
    slope = 0.5 * (1.0 + tanh_val) + 0.5 * pre * (1.0 - tanh_val * tanh_val) * gelu_coef * (
        1.0 + 3.0 * 0.044715 * pre * pre
    )
    return value, slope


def spread(sz):
    shape = (sz.rows, sz.chans)
    return (iota(shape, 0) // sz.len_y == iota(shape, 1)).astype(bf16)


def same_y(sz):
    shape = (sz.rows, sz.rows)
    return iota(shape, 0) % sz.len_y == iota(shape, 1) % sz.len_y


def point_matrix(sz, weight, forward):
    one = spread(sz)
    part = nt(one, weight) if forward else nn(one, weight)
    full = nt(part.astype(bf16), one)
    return jnp.where(same_y(sz), full, 0.0).astype(bf16)


def swapped(rows, half):
    return jnp.concatenate([rows[half:], rows[:half]], axis=0)


def send_analysis(sz, bb_ref, field, out_ref, layer):
    out = nt(bb_ref[...], field).astype(bf16)
    out_ref[...] = swapped(out, sz.modes // 2) if layer == 1 else out


def fill_table(sz, bx, bz, bb):
    depth = sz.depth
    for x in range(sz.len_x):
        bb[:, x * depth : (x + 1) * depth] = (bx[:, x : x + 1] * bz[...]).astype(bf16)


def tables_kernel(sz, gx_ref, bx_hbm, bz_hbm, bb, bx, bz, sems):
    copies = Copies(sems)
    get_bx = copies.start(bx_hbm.at[gx_ref[0]], bx)
    get_bz = copies.start(bz_hbm, bz)
    get_bx.wait()
    get_bz.wait()
    fill_table(sz, bx, bz, bb)


def tables_call(sz, gx, bx, bz):
    (bb,) = run(
        "tables",
        lambda *refs: tables_kernel(sz, *refs),
        [(kept((sz.modes, sz.cells)), False)],
        [smem, hbm, hbm],
        (gx, bx, bz),
        [pltpu.VMEM(bx.shape[1:], f32), pltpu.VMEM(bz.shape, f32)],
        2,
    )
    return bb


def first_kernel(sz, s_ref, keep_hbm, recv_hbm, small_ref, bb, out_hbm, v, out, sems):
    copies = Copies(sems)
    (get_v,) = copies.choose(s_ref[0] == 0, [(keep_hbm, recv_hbm, v)])
    get_v.wait()
    send_analysis(sz, bb, v[...], out, 0)
    copies.send(out, out_hbm)
    copies.finish()


def first_call(sz, s, keep, recv, small, bb):
    line = (sz.modes, sz.rows)
    (out,) = run(
        "first",
        lambda *refs: first_kernel(sz, *refs),
        [(shape(line), True)],
        [smem, hbm, hbm, vmem, vmem],
        (s, keep, recv, small, near(bb)),
        [pltpu.VMEM((sz.rows, sz.cells), bf16), pltpu.VMEM(line, bf16)],
        2,
    )
    return out


def pack_kernel(sz, tables, w_ref, *rest):
    if tables:
        by_ref, out_ref, ya_ref = rest

        @pl.when(pl.program_id(0) == 0)
        def _():
            wide = sz.modes_y * sz.cpl
            lane_c = iota((sz.len_y, wide), 1) % sz.cpl
            for g in range(sz.lines):
                part = by_ref[g * sz.len_y : (g + 1) * sz.len_y, :]
                block = jnp.concatenate([jnp.where(lane_c == c, part, 0.0) for c in range(sz.cpl)], axis=0)
                ya_ref[g * 128 : (g + 1) * 128, :] = block.astype(bf16)

    else:
        (out_ref,) = rest
    width = sz.lgs * sz.chans
    dims = (sz.chans, width)
    places = [(iota(dims, 0) + lg * sz.chans == iota(dims, 1)).astype(bf16) for lg in range(sz.lgs)]
    for kk in range(sz.blk_k):
        total = None
        for lg in range(sz.lgs):
            rows = jnp.concatenate(
                [
                    w_ref[0, 0, kk, lg * 8 : (lg + 1) * 8, h * sz.cpl : (h + 1) * sz.cpl, :].reshape(128, sz.chans)
                    for h in range(sz.groups)
                ],
                axis=0,
            )
            part = nn(rows, places[lg])
            total = part if total is None else total + part
        out_ref[0, kk] = total.astype(bf16)


def pack_call(sz, weight, start, micros, by=None):
    rows, width, half = sz.groups * 128, sz.lgs * sz.chans, sz.half_j
    block = (1, sz.blk_k, rows, width)
    lines = (sz.lines * 128, sz.modes_y * sz.cpl)
    packed = pltpu.HBM((half, sz.blk_k, rows, width), bf16)
    tables = by is not None
    weight_spec = pl.BlockSpec((1, 1) + weight.shape[2:], lambda i: (0, i + start, 0, 0, 0, 0))
    packed_spec = pl.BlockSpec(block, lambda i: (i, 0, 0, 0))
    return pl.pallas_call(
        lambda *refs: pack_kernel(sz, tables, *refs),
        grid=(half,),
        out_shape=(packed, pltpu.HBM(lines, bf16)) if tables else packed,
        in_specs=[weight_spec, pl.BlockSpec(by.shape, lambda i: (0, 0))] if tables else [weight_spec],
        out_specs=(packed_spec, pl.BlockSpec(lines, lambda i: (0, 0))) if tables else packed_spec,
        compiler_params=pltpu.CompilerParams(vmem_limit_bytes=limit),
        cost_estimate=pl.CostEstimate(flops=0, transcendentals=0, bytes_accessed=micros * 3000000),
        name="pack",
    )(*([far(weight), far(by)] if tables else [far(weight)]))


def line_analysis(sz, r_ref, ya_ref, get_ya):
    jk = sz.jk
    lines = []
    for sec in range(2):
        for gy in range(sz.n_gy):
            total = None
            for gx in range(sz.n_gx):
                at = ((sec * sz.n_gx + gx) * sz.n_gy + gy) * jk
                part = r_ref[at : at + jk, :].astype(f32)
                total = part if total is None else total + part
            lines.append(total.astype(bf16))
    halves = [
        jnp.concatenate([line[:, h * 128 : (h + 1) * 128] for line in lines], axis=1) for h in range(sz.groups)
    ]
    if get_ya is not None:
        get_ya.wait()
    return nn(jnp.concatenate(halves, axis=0), ya_ref[...]).astype(bf16)


def diagonal(sz, count):
    shape = (count, sz.groups * 128)
    return iota(shape, 0) % 8 == (iota(shape, 1) % 128) // sz.cpl


def row_spread(sz):
    shape = (sz.jk * 8, sz.jk)
    return (iota(shape, 0) // 8 == iota(shape, 1)).astype(bf16)


def row_gather(sz):
    shape = (sz.jk, sz.jk * 8)
    return (iota(shape, 1) // 8 == iota(shape, 0)).astype(bf16)


def chan_lanes(sz):
    shape = (sz.groups * 128, sz.chans)
    lane = iota(shape, 0)
    return ((lane // 128) * sz.cpl + lane % sz.cpl == iota(shape, 1)).astype(bf16)


def to_blocks(sz, rows, lg):
    jk = sz.jk
    wide = jnp.concatenate(
        [rows[h * jk : (h + 1) * jk, lg * 128 : (lg + 1) * 128] for h in range(sz.groups)], axis=1
    )
    return jnp.where(diagonal(sz, jk * 8), nn(row_spread(sz), wide), 0.0)


def from_blocks(sz, blocks):
    jk = sz.jk
    pieces = []
    for block in blocks:
        kept = jnp.where(diagonal(sz, jk * 8), block, 0.0).astype(bf16)
        pieces.append(nn(row_gather(sz), kept).astype(bf16))
    return jnp.concatenate(
        [
            jnp.concatenate([piece[:, h * 128 : (h + 1) * 128] for piece in pieces], axis=1)
            for h in range(sz.groups)
        ],
        axis=0,
    )


def send_lines(sz, rows, ya_ref, out_ref):
    jk = sz.jk
    lines = nt(rows, ya_ref[...]).astype(bf16)
    for sec in range(2):
        for gy in range(sz.n_gy):
            line = sec * sz.n_gy + gy
            block = jnp.concatenate(
                [lines[h * jk : (h + 1) * jk, line * 128 : (line + 1) * 128] for h in range(sz.groups)], axis=1
            )
            for gx in range(sz.n_gx):
                at = ((sec * sz.n_gx + gx) * sz.n_gy + gy) * jk
                out_ref[at : at + jk, :] = block


def lane_group(sz):
    dims = (sz.lgs * sz.jk * 8, sz.lgs * sz.chans)
    return iota(dims, 0) // (sz.jk * 8) == iota(dims, 1) // sz.chans


def mix_kernel(sz, layer, turn, s_ref, r, ya_in, low_hbm, high_hbm, spec_hbm, out, *rest):
    if layer == 0:
        ya, w, spec_b, blk, mix, sems = rest
    else:
        ya = ya_in
        w, spec_b, blk, mix, sems = rest
    copies = Copies(sems)
    get_ya = copies.start(ya_in, ya) if layer == 0 else None
    get_w = copies.choose(s_ref[0] == layer, [(low_hbm.at[jj], high_hbm.at[jj], w.at[jj]) for jj in range(sz.half_j)])
    spec = line_analysis(sz, r, ya, get_ya)
    spec_b[...] = spec
    copies.send(spec_b, spec_hbm)
    count = sz.jk * 8
    width = sz.lgs * sz.chans
    rep = jnp.concatenate([chan_lanes(sz)] * sz.lgs, axis=1)
    blocks = [to_blocks(sz, spec, lg) for lg in range(sz.lgs)]
    if turn:
        flat = nn(jnp.concatenate(blocks, axis=0).astype(bf16), rep)
        mix[:, :width] = jnp.where(lane_group(sz), flat, 0.0)
        left_ref, right_ref, left_width = mix, blk, width
    else:
        for lg in range(sz.lgs):
            blk[lg * count : (lg + 1) * count, :] = blocks[lg]
        left_ref, right_ref, left_width = blk, mix, blk.shape[1]
    for jk in range(sz.jk):
        jj, kk = jk // sz.blk_k, jk % sz.blk_k
        if kk == 0:
            get_w[jj].wait()
        at = [slice((lg * sz.jk + jk) * 8, (lg * sz.jk + jk + 1) * 8) for lg in range(sz.lgs)]
        left = jnp.concatenate([left_ref[a, :left_width] for a in at], axis=0).astype(bf16)
        part = nt(left, w[jj, kk]) if turn else nn(left, w[jj, kk])
        for lg, a in enumerate(at):
            right_ref[a, : part.shape[1]] = part[lg * 8 : (lg + 1) * 8]
    if not turn:
        kept_mix = jnp.where(lane_group(sz), mix[:, :width], 0.0).astype(bf16)
        full = nt(kept_mix, rep)
    else:
        full = blk[...]
    blocks = [full[lg * count : (lg + 1) * count] for lg in range(sz.lgs)]
    send_lines(sz, from_blocks(sz, blocks), ya, out)
    copies.finish()


def mix_call(sz, layer, turn, s, r, ya, low, high):
    count = sz.jk * 8 * sz.lgs
    spec = (sz.groups * sz.jk, sz.modes_y * sz.cpl)
    line = (sz.modes, sz.rows)
    outs = [(shape(spec), True), (kept(line), False)]
    if layer == 0:
        outs.append((kept(ya.shape), False))
    else:
        ya = near(ya)
    return run(
        "mix",
        lambda *refs: mix_kernel(sz, layer, turn, *refs),
        outs,
        [smem, vmem, hbm if layer == 0 else vmem, hbm, hbm],
        (s, r, ya, low, high),
        [
            pltpu.VMEM(low.shape, bf16),
            pltpu.VMEM(spec, bf16),
            pltpu.VMEM((count, sz.groups * 128), f32),
            pltpu.VMEM((count, sz.groups * 128), f32),
        ],
        sz.half_j + 2,
    )


def spec_kernel(sz, s_ref, r, sv0, sv1, su1, ya, out_hbm, send_hbm, out, sends, sems):
    copies = Copies(sems)
    first = s_ref[0] == 0
    spec = line_analysis(sz, r, ya, None)
    out[...] = spec
    sends[0] = jnp.where(first, sv1[...], sv0[...])
    sends[1] = jnp.where(first, su1[...], spec)
    copies.send(sends, send_hbm)
    copies.send(out, out_hbm)
    copies.finish()


def spec_call(sz, s, r, sv0, sv1, su1, ya):
    spec = (sz.groups * sz.jk, sz.modes_y * sz.cpl)
    return run(
        "spec",
        lambda *refs: spec_kernel(sz, *refs),
        [(shape(spec), True), (shape((2,) + spec), True)],
        [smem] + [vmem] * 5,
        (s, r, sv0, sv1, su1, near(ya)),
        [pltpu.VMEM(spec, bf16), pltpu.VMEM((2,) + spec, bf16)],
        2,
    )


def turned_modes(sz, u_ref, layer):
    left = jnp.transpose(u_ref[...])
    half = sz.modes // 2
    if layer == 1:
        left = jnp.concatenate([left[:, half:], left[:, :half]], axis=1)
    return left


CHUNK = 512


def cuts(sz):
    return [slice(at, at + CHUNK) for at in range(0, sz.cells, CHUNK)]


def buffers(sz, kinds):
    dims = {"m": (sz.modes, sz.cells), "u": (sz.modes, sz.rows), "f": (sz.rows, sz.cells), "w": (sz.rows, sz.cells)}
    return [pltpu.VMEM(dims[kind], f32 if kind == "w" else bf16) for kind in kinds]


def small_parts(sz, s_ref, own_ref, other_ref, layer):
    chosen = jnp.where(s_ref[0] == layer, own_ref[...].astype(f32), other_ref[...].astype(f32)).astype(bf16)
    return chosen[: sz.chans], chosen[sz.chans :]


def point_sums(sz, v, d):
    pairs = jnp.where(same_y(sz), nt(v, d), 0.0)
    pairs = jnp.sum(pairs.reshape(sz.chans, sz.len_y, sz.rows), axis=1)
    bias = nt(jnp.ones((8, sz.cells), bf16), d)
    part = sz.chans // 4
    total = None
    for t in range(4):
        dims = (sz.rows, 128)
        place = (iota(dims, 0) // sz.len_y + t * sz.chans == iota(dims, 1)).astype(f32)
        both = pairs[t * part : (t + 1) * part]
        both = jnp.concatenate([both, bias if t == 0 else jnp.zeros_like(bias)], axis=0)
        term = lax.dot_general(
            both, place, (((1,), (0,)), ((), ())), precision=lax.Precision.HIGHEST, preferred_element_type=f32
        )
        total = term if total is None else total + term
    return total


def forward_kernel(
    sz, s_ref, gx_ref, own_ref, other_ref, u, keep_hbm, recv_hbm, bx_hbm, bz_hbm, v, slope, bb, out, field, bx, bz, sems
):
    copies = Copies(sems)
    get_bx = copies.start(bx_hbm.at[gx_ref[0]], bx)
    get_bz = copies.start(bz_hbm, bz)
    (get_v,) = copies.choose(s_ref[0] == 0, [(keep_hbm, recv_hbm, field)])
    weight, bias = small_parts(sz, s_ref, own_ref, other_ref, 0)
    matrix = point_matrix(sz, weight, True)
    column = nt(spread(sz), bias)[:, :1]
    left = turned_modes(sz, u, 0)
    get_bx.wait()
    get_bz.wait()
    fill_table(sz, bx, bz, bb)
    get_v.wait()
    for cut in cuts(sz):
        pre = nn(left, bb[:, cut]) + nn(matrix, field[:, cut]) + column
        value, rate = activate(pre)
        v[:, cut] = value.astype(bf16)
        slope[:, cut] = rate
    send_analysis(sz, bb, v[...], out, 1)


def forward_call(sz, s, gx, keep, recv, u, bx, bz, own, other):
    field, line = (sz.rows, sz.cells), (sz.modes, sz.rows)
    return run(
        "forward",
        lambda *refs: forward_kernel(sz, *refs),
        [(kept(field), False), (kept(field, f32), False), (kept((sz.modes, sz.cells)), False), (kept(line), False)],
        [smem, smem, vmem, vmem, vmem, hbm, hbm, hbm, hbm],
        (s, gx, own, other, u, keep, recv, bx, bz),
        buffers(sz, "f") + [pltpu.VMEM(bx.shape[1:], f32), pltpu.VMEM(bz.shape, f32)],
        3,
    )


def turn_kernel(sz, s_ref, own_ref, other_ref, u, v, bb, keep_hbm, recv_hbm, d, sums, out, grad, sems):
    copies = Copies(sems)
    (get_g,) = copies.choose(s_ref[0] == 0, [(recv_hbm, keep_hbm, grad)])
    weight, bias = small_parts(sz, s_ref, own_ref, other_ref, 1)
    matrix = point_matrix(sz, weight, True)
    column = nt(spread(sz), bias)[:, :1]
    left = turned_modes(sz, u, 1)
    for at, cut in enumerate(cuts(sz)):
        pre = nn(left, bb[:, cut]) + nn(matrix, v[:, cut]) + column
        _, rate = activate(pre)
        if at == 0:
            get_g.wait()
        d[:, cut] = (grad[:, cut].astype(f32) * rate).astype(bf16)
    send_analysis(sz, bb, d[...], out, 1)
    sums[...] = point_sums(sz, v[...], d[...])


def turn_call(sz, s, keep, recv, v, u, bb, own, other):
    field, line = (sz.rows, sz.cells), (sz.modes, sz.rows)
    return run(
        "turn",
        lambda *refs: turn_kernel(sz, *refs),
        [(kept(field), False), (kept((sz.chans // 4 + 8, 128), f32), False), (kept(line), False)],
        [smem, vmem, vmem, vmem, vmem, vmem, hbm, hbm],
        (s, own, other, u, near(v), near(bb), keep, recv),
        buffers(sz, "f"),
        1,
    )


def back_kernel(sz, s_ref, own_ref, other_ref, u, d, slope, bb, sums, keep_hbm, recv_hbm, parts_hbm, out, new, field, parts, sems):
    copies = Copies(sems)
    (get_v,) = copies.choose(s_ref[0] == 0, [(keep_hbm, recv_hbm, field)])
    weight, _ = small_parts(sz, s_ref, own_ref, other_ref, 1)
    matrix = point_matrix(sz, weight, False)
    left = turned_modes(sz, u, 1)
    for cut in cuts(sz):
        grad = (nn(left, bb[:, cut]) + nn(matrix, d[:, cut])).astype(bf16).astype(f32)
        new[:, cut] = (grad * slope[:, cut]).astype(bf16)
    send_analysis(sz, bb, new[...], out, 0)
    get_v.wait()
    first = point_sums(sz, field[...], new[...])
    half = sz.places // 2
    for place in range(half):
        parts[place] = first
        parts[half + place] = sums[...]
    copies.send(parts, parts_hbm)
    copies.finish()


def back_call(sz, s, keep, recv, d, slope, u, bb, sums, own, other):
    parts, line = (sz.places, sz.chans // 4 + 8, 128), (sz.modes, sz.rows)
    return run(
        "back",
        lambda *refs: back_kernel(sz, *refs),
        [(shape(parts, f32), True), (kept(line), False)],
        [smem] + [vmem] * 7 + [hbm, hbm],
        (s, own, other, u, near(d), near(slope), near(bb), near(sums), keep, recv),
        buffers(sz, "ff") + [pltpu.VMEM(parts, f32)],
        2,
    )


def finish_kernel(sz, parts_ref, after_ref, point_ref, bias_ref):
    total = jnp.sum(parts_ref[...], axis=0)
    part = sz.chans // 4
    for t in range(4):
        point_ref[0, t * part : (t + 1) * part, :] = total[:part, t * sz.chans : (t + 1) * sz.chans]
    bias_ref[...] = total[part : part + 1, : sz.chans]


def finish_call(sz, parts, after):
    return pl.pallas_call(
        lambda *refs: finish_kernel(sz, *refs),
        out_shape=(shape((1, sz.chans, sz.chans), f32), shape((1, sz.chans), f32)),
        in_specs=[vmem, hbm],
        out_specs=(vmem, vmem),
        compiler_params=pltpu.CompilerParams(vmem_limit_bytes=limit),
        name="finish",
    )(parts, far(after))


def outer_kernel(sz, s_ref, sv0_ref, sv1_ref, su0_ref, su1_ref, theirs_ref, out_ref, left_ref, right_ref):
    jk, groups, kk_count = sz.jk, sz.groups, sz.blk_k
    step = pl.program_id(0)

    def prepare(side, sv, su):
        sv = sv.astype(f32)
        for jj in range(sz.half_j):
            place = side * sz.half_j + jj
            rows = jnp.concatenate(
                [sv[h * jk + jj * kk_count : h * jk + (jj + 1) * kk_count] for h in range(groups)], axis=0
            )
            left_ref[place] = jnp.transpose(rows)
        for lg in range(sz.lgs):
            flat = nn(to_blocks(sz, su, lg).astype(bf16), chan_lanes(sz))
            for at in range(jk):
                place = side * sz.half_j + at // kk_count
                right_ref[place, at % kk_count, lg * 8 : (lg + 1) * 8, :] = flat[at * 8 : (at + 1) * 8]

    @pl.when(step == 0)
    def _():
        first = s_ref[0] == 0
        prepare(
            0, jnp.where(first, sv0_ref[...], sv1_ref[...]), jnp.where(first, su0_ref[...], su1_ref[...])
        )

    @pl.when(step == 1)
    def _():
        prepare(1, theirs_ref[0], theirs_ref[1])

    for kk in range(kk_count):
        for h in range(groups):
            column = left_ref[step, :, h * kk_count + kk : h * kk_count + kk + 1]
            for ll in range(sz.modes_y):
                row = right_ref[step, kk, ll : ll + 1, :]
                part = column[ll * sz.cpl : (ll + 1) * sz.cpl] * row
                out_ref[0, 0, kk, ll, h * sz.cpl : (h + 1) * sz.cpl, :] = part


def outer_call(sz, s, sv0, sv1, su0, su1, theirs):
    wide = sz.modes_y * sz.cpl
    return pl.pallas_call(
        lambda *refs: outer_kernel(sz, *refs),
        grid=(sz.blk_j,),
        out_shape=pltpu.HBM((1, sz.blk_j, sz.blk_k, sz.modes_y, sz.chans, sz.chans), f32),
        in_specs=[smem] + [vmem] * 5,
        out_specs=pl.BlockSpec((1, 1, sz.blk_k, sz.modes_y, sz.chans, sz.chans), lambda i: (0, i, 0, 0, 0, 0)),
        scratch_shapes=[
            pltpu.VMEM((sz.blk_j, wide, sz.groups * sz.blk_k), f32),
            pltpu.VMEM((sz.blk_j, sz.blk_k, sz.modes_y, sz.chans), f32),
        ],
        compiler_params=pltpu.CompilerParams(vmem_limit_bytes=limit),
        cost_estimate=pl.CostEstimate(flops=0, transcendentals=0, bytes_accessed=20000000),
        name="outer",
    )(s, sv0, sv1, su0, su1, theirs)


def exchange(block):
    return lax.all_to_all(block, AXES, split_axis=0, concat_axis=0, tiled=True)


def swap(block):
    return lax.ppermute(block, "section", [(0, 1), (1, 0)])


def local(ends, spectral_weight, point_weight, point_bias):
    sz = Sizes(ends, spectral_weight)
    section = lax.axis_index("section")
    first = section == 0
    s = section.astype(jnp.int32).reshape(1)

    def half(field, which):
        part = lax.dynamic_slice_in_dim(field, which * sz.len_y, sz.len_y, axis=2)
        return jnp.swapaxes(part, 1, 2).reshape(sz.rows, sz.cells)

    bx, bz, by = [jnp.asarray(t) for t in mode_tables(sz)]
    send = half(ends[0], 1 - section)
    send, later = lax.optimization_barrier((send, ends[0]))
    recv = swap(send)
    keep = half(later, section)
    gx = lax.axis_index("gx").astype(jnp.int32).reshape(1)
    bb = tables_call(sz, gx, bx, bz)
    own_small = jnp.concatenate([point_weight[0], jnp.broadcast_to(point_bias, (16, sz.chans))], axis=0)
    other_small = swap(own_small)

    out = first_call(sz, s, keep, recv, other_small, bb)
    out, weight = lax.optimization_barrier((out, spectral_weight))
    r = exchange(out)
    high = swap(pack_call(sz, weight, sz.half_j, 2))
    low, ya = pack_call(sz, weight, 0, 6, by)
    sv0, out, ya = mix_call(sz, 0, False, s, r, ya, low, high)
    v1, slope0, bb, out = forward_call(sz, s, gx, keep, recv, exchange(out), bx, bz, own_small, other_small)
    sv1, out = mix_call(sz, 1, False, s, exchange(out), ya, low, high)
    d1, sums, out = turn_call(sz, s, keep, recv, v1, exchange(out), bb, own_small, other_small)
    su1, out = mix_call(sz, 1, True, s, exchange(out), ya, low, high)
    parts, out = back_call(sz, s, keep, recv, d1, slope0, exchange(out), bb, sums, own_small, other_small)
    r, parts = lax.optimization_barrier((exchange(out), parts))
    su0, send = spec_call(sz, s, r, sv0, sv1, su1, ya)
    theirs = swap(send)
    parts = lax.all_to_all(parts, AXES, split_axis=0, concat_axis=0, tiled=True)
    spectral_grad = outer_call(sz, s, sv0, sv1, su0, su1, theirs)
    point_grad, bias_grad = finish_call(sz, parts, spectral_grad)
    return (spectral_grad, point_grad, bias_grad)


def solution(mesh):
    return jax.shard_map(
        local,
        mesh=mesh,
        in_specs=(
            P("section", None, "gx", "gy", None),
            P("section", "gy", "gx", None, None, None),
            P("section", None, None),
            P("section", None),
        ),
        out_specs=(
            P("section", "gy", "gx", None, None, None),
            P("section", None, None),
            P("section", None),
        ),
        check_vma=False,
    )
```

time: 189 us -> 154 us (0.81)
  waiting for transfers between devices: 31.4 us -> 7.64 us
  blocking collectives: 58 us -> 78.2 us
  Pallas kernels: 63.8 us -> 47.9 us
  local copies, waits for them, and re-layouts: 15.2 us -> 7.44 us
  starting transfers between devices: 17.4 us -> 10.7 us
    all_to_all x4 -> x6, blocking collectives: 58 us -> 78.2 us  [exchange(): return lax.all_to_all(block, AXES, split_axis=0, concat_axis=0, tiled=True)]
    all_to_all x3 -> x1, waiting for transfers between devices: 23.4 us -> 6.28 us  [exchange(): return lax.all_to_all(block, AXES, split_axis=0, concat_axis=0, tiled=True)]
    pallas_call x10 -> x12, Pallas kernels: 50.5 us -> 38.6 us  [the longest x9 28.2 us: run(): pl.pallas_call(kernel, out_shape=tuple((pltpu.HBM(o.shape, o.dtype) if aw...]
    all_to_all x1, waiting for transfers between devices: 5.95 us -> 0.01 us  [local(): parts = lax.all_to_all(parts, AXES, split_axis=0, concat_axis=0, tiled=True)]
    all_to_all x3 -> x1, starting transfers between devices: 12.6 us -> 6.96 us  [exchange(): return lax.all_to_all(block, AXES, split_axis=0, concat_axis=0, tiled=True)]
    squeeze x1 -> x0, local copies, waits for them, and re-layouts: 5.12 us -> none  [local(): other_weight = swap(spectral_weight[0, sz.half_j:])]
    pallas_call x1, Pallas kernels: 13.4 us -> 9.31 us  [outer_call(): pl.pallas_call(lambda *refs: outer_kernel(sz, *refs), grid=(sz.blk_j,), o...]
    unnamed x24 -> x20, local copies, waits for them, and re-layouts: 2.46 us -> 5.27 us
  transfers between devices with their start and end apart: 9 -> 6, of which waited for: 6 -> 2; matrix products, arithmetic and copies ran while one was open for 6% -> 1% of each run, Pallas kernels for 7% -> 11%
where the time goes in v1:
time: 154 us; the launch traced here: 153 us
  blocking collectives  78.2 us (51%)
  Pallas kernels  47.9 us (31%)
  starting transfers between devices  10.7 us (7%)
  waiting for transfers between devices  7.64 us (5%)
  local copies, waits for them, and re-layouts  7.44 us (5%)
    all_to_all x6, blocking collectives, exchange(): return lax.all_to_all(block, AXES, split_axis=0, concat_axis=0, tiled=True)  78.2 us
    pallas_call x9, Pallas kernels, run(): pl.pallas_call(kernel, out_shape=tuple((pltpu.HBM(o.shape, o.dtype) if aw...  28.2 us
    pallas_call x2, Pallas kernels, pack_call(): pl.pallas_call(lambda *refs: pack_kernel(sz, tables, *refs), grid=(half,)...  9.7 us
    pallas_call x1, Pallas kernels, outer_call(): pl.pallas_call(lambda *refs: outer_kernel(sz, *refs), grid=(sz.blk_j,), o...  9.31 us
    all_to_all x1, starting transfers between devices, exchange(): return lax.all_to_all(block, AXES, split_axis=0, concat_axis=0, tiled=True)  6.96 us
    all_to_all x1, waiting for transfers between devices, exchange(): return lax.all_to_all(block, AXES, split_axis=0, concat_axis=0, tiled=True)  6.28 us
    unnamed x20, local copies, waits for them, and re-layouts  5.27 us
  transfers between devices with their start and end apart: 6, of which 2 were waited for; matrix products, arithmetic and copies ran while one was open for 1% of the time, Pallas kernels for 11%

profile of v1, /device:TPU:0, one launch (start us, length us, event | category | flops | bytes accessed | tf_op | source)
XLA Modules:
  0.0 152.8 jit_solution(3400928411002143168)
XLA Ops:
  0.7 1.6 %copy-done = bf16[1,32,16,16,128]{4,3,2,1,0:T(8,128)(2,1)S(1)} copy-done((bf16[1,32,16,16,128]{4,3,2,1,0:T(8,128)(2,1)S(1)}, bf16[1,32,16,16,128]{4,3,2,1,0:T(8,128)(2,1)}, u32[]{:S(2)}) %copy-start) | copy-done | bytes 2097176
  2.2 1.1 dynamic-slice_bitcast_fusion.1
  3.4 0.5 collective-permute-start
  4.0 1.1 dynamic-slice_bitcast_fusion.refs_1_.refs_5_.refs_6_.refs_8_
  5.0 2.2 %tables.1.refs_4_ = bf16[512,2048]{1,0:T(8,128)(2,1)S(1)} custom-call(s32[1]{0:T(128)} %bitcast.9.refs_0_.refs_1_, f32[4,512,16]{2,1,0:T(8,128)} %constant.26.clone.refs_1_.refs_7_, f32[512,128]{1,0:T(8,128)} %constant.27.clone.refs_2_.refs_8_), custom_call_target="tpu_custom_call" | custom-call | bytes 3000000 | tf_op jit(solution)/shard_map/tables/pallas_call | solution.py:69
  7.3 1.0 copy-done.6
  8.3 2.7 %first.1 = bf16[512,256]{1,0:T(8,128)(2,1)} custom-call(s32[1]{0:T(128)} %bitcast.refs_0_, bf16[256,2048]{1,0:T(8,128)(2,1)} %dynamic-slice_bitcast_fusion.refs_1_.refs_5_.refs_6_.refs_8_, bf16[256,2048]{1,0:T(8,128)(2,1)} %copy-done.6, bf16[48,32]{1,0:T(8,128)(2,1)S(1)} %collective-permute-done.1.refs_3_.refs_2_, bf16[512,2048]{1,0:T(8,128)(2,1)S(1)} %tables.1.refs_4_), custom_call_target="tpu_custom_call" | custom-call | bytes 3000000 | tf_op jit(solution)/shard_map/first/pallas_call | solution.py:69
  11.0 4.8 %pack.3 = bf16[4,4,256,128]{3,2,1,0:T(8,128)(2,1)} custom-call(bf16[1,8,4,32,32,32]{5,4,3,2,1,0:T(8,128)(2,1)} %refs_0_.1), custom_call_target="tpu_custom_call" | custom-call | bytes 6000000 | tf_op jit(solution)/shard_map/pack/pallas_call | solution.py:287
  15.7 0.4 collective-permute-start.2
  16.2 7.0 %all-to-all-start = ((bf16[32,16,256]{2,1,0:T(8,128)(2,1)}), bf16[32,16,256]{2,1,0:T(8,128)(2,1)S(1)}, u32[]{:S(2)}, u32[]{:S(2)}) async-start(bf16[32,16,256]{2,1,0:T(8,128)(2,1)} %bitcast.43), calls=%async_computation | async-start | bytes 524288 | tf_op jit(solution)/shard_map/all_to_all | solution.py:692
  23.1 4.9 %pack.2 = (bf16[4,4,256,128]{3,2,1,0:T(8,128)(2,1)}, bf16[1024,512]{1,0:T(8,128)(2,1)}) custom-call(bf16[1,8,4,32,32,32]{5,4,3,2,1,0:T(8,128)(2,1)} %refs_0_.1, f32[64,512]{1,0:T(8,128)} %constant.28.clone.refs_1_), custom_call_target="tpu_custom_call" | custom-call | bytes 18000000 | tf_op jit(solution)/shard_map/pack/pallas_call | solution.py:287
  28.1 6.3 %all-to-all-done = bf16[32,16,256]{2,1,0:T(8,128)(2,1)S(1)} async-done(((bf16[32,16,256]{2,1,0:T(8,128)(2,1)}), bf16[32,16,256]{2,1,0:T(8,128)(2,1)S(1)}, u32[]{:S(2)}, u32[]{:S(2)}) %all-to-all-start) | async-done | bytes 262176 | tf_op jit(solution)/shard_map/all_to_all | solution.py:692
  34.4 1.0 copy-done.7
  35.3 3.1 %mix.3 = (bf16[32,512]{1,0:T(8,128)(2,1)}, bf16[512,256]{1,0:T(8,128)(2,1)S(1)}, bf16[1024,512]{1,0:T(8,128)(2,1)S(1)}) custom-call(s32[1]{0:T(128)} %bitcast.refs_0_, bf16[512,256]{1,0:T(8,128)(2,1)S(1)} %bitcast.30, bf16[1024,512]{1,0:T(8,128)(2,1)} %get-tuple-element.35.refs_2_, bf16[4,4,256,128]{3,2,1,0:T(8,128)(2,1)} %get-tuple-element.36.refs_3_, ...), custom_call_target="tpu_custom_call" | custom-call | bytes 3000000 | tf_op jit(solution)/shard_map/mix/pallas_call | solution.py:69
  38.4 12.9 %all_to_all.83 = bf16[32,16,256]{2,1,0:T(8,128)(2,1)S(1)} all-to-all(bf16[32,16,256]{2,1,0:T(8,128)(2,1)S(1)} %bitcast.39), channel_id=1, replica_groups=mesh['section'=2,'gx'=4,'gy'=4] {'section','gx','gy'}, dimensions={0} | all-to-all | bytes 524288 | tf_op jit(solution)/shard_map/all_to_all | solution.py:692
  51.3 5.0 %forward.1 = (bf16[256,2048]{1,0:T(8,128)(2,1)S(1)}, f32[256,2048]{1,0:T(8,128)S(1)}, bf16[512,2048]{1,0:T(8,128)(2,1)S(1)}, bf16[512,256]{1,0:T(8,128)(2,1)S(1)}) custom-call(s32[1]{0:T(128)} %bitcast.refs_0_, s32[1]{0:T(128)} %bitcast.9.refs_0_.refs_1_, bf16[48,32]{1,0:T(8,128)(2,1)S(1)} %pad_maximum_fusion.refs_2_.refs_1_, ...), custom_call_target="tpu_custom_call" | custom-call | bytes 3000000 | tf_op jit(solution)/shard_map/forward/pallas_call | solution.py:69
  56.4 12.9 %all_to_all.84 = bf16[32,16,256]{2,1,0:T(8,128)(2,1)S(1)} all-to-all(bf16[32,16,256]{2,1,0:T(8,128)(2,1)S(1)} %bitcast.38), channel_id=1, replica_groups=mesh['section'=2,'gx'=4,'gy'=4] {'section','gx','gy'}, dimensions={0} | all-to-all | bytes 524288 | tf_op jit(solution)/shard_map/all_to_all | solution.py:692
  69.3 2.7 %mix.4 = (bf16[32,512]{1,0:T(8,128)(2,1)}, bf16[512,256]{1,0:T(8,128)(2,1)S(1)}) custom-call(s32[1]{0:T(128)} %bitcast.refs_0_, bf16[512,256]{1,0:T(8,128)(2,1)S(1)} %bitcast.36, bf16[1024,512]{1,0:T(8,128)(2,1)S(1)} %get-tuple-element.40.refs_2_.refs_5_, bf16[4,4,256,128]{3,2,1,0:T(8,128)(2,1)} %get-tuple-element.36.refs_3_, bf16[4,4,256,128]{3,2,1,0:T(8,128)(2,1)} %copy-done.7), custom_call_target="tpu_custom_call" | custom-call | bytes 3000000 | tf_op jit(solution)/shard_map/mix/pallas_call | solution.py:69
  71.9 12.9 %all_to_all.85 = bf16[32,16,256]{2,1,0:T(8,128)(2,1)S(1)} all-to-all(bf16[32,16,256]{2,1,0:T(8,128)(2,1)S(1)} %bitcast.42), channel_id=1, replica_groups=mesh['section'=2,'gx'=4,'gy'=4] {'section','gx','gy'}, dimensions={0} | all-to-all | bytes 524288 | tf_op jit(solution)/shard_map/all_to_all | solution.py:692
  84.9 4.5 %turn.1 = (bf16[256,2048]{1,0:T(8,128)(2,1)S(1)}, f32[16,128]{1,0:T(8,128)S(1)}, bf16[512,256]{1,0:T(8,128)(2,1)S(1)}) custom-call(s32[1]{0:T(128)} %bitcast.refs_0_, bf16[48,32]{1,0:T(8,128)(2,1)S(1)} %pad_maximum_fusion.refs_2_.refs_1_, bf16[48,32]{1,0:T(8,128)(2,1)S(1)} %collective-permute-done.1.refs_3_.refs_2_, bf16[512,256]{1,0:T(8,128)(2,1)S(1)} %bitcast.34, ...), custom_call_target="tpu_custom_call" | custom-call | bytes 3000000 | tf_op jit(solution)/shard_map/turn/pallas_call | solution.py:69
  89.4 12.9 %all_to_all.86 = bf16[32,16,256]{2,1,0:T(8,128)(2,1)S(1)} all-to-all(bf16[32,16,256]{2,1,0:T(8,128)(2,1)S(1)} %bitcast.40), channel_id=1, replica_groups=mesh['section'=2,'gx'=4,'gy'=4] {'section','gx','gy'}, dimensions={0} | all-to-all | bytes 524288 | tf_op jit(solution)/shard_map/all_to_all | solution.py:692
  102.3 2.6 %mix.5 = (bf16[32,512]{1,0:T(8,128)(2,1)}, bf16[512,256]{1,0:T(8,128)(2,1)S(1)}) custom-call(s32[1]{0:T(128)} %bitcast.refs_0_, bf16[512,256]{1,0:T(8,128)(2,1)S(1)} %bitcast.35, bf16[1024,512]{1,0:T(8,128)(2,1)S(1)} %get-tuple-element.40.refs_2_.refs_5_, bf16[4,4,256,128]{3,2,1,0:T(8,128)(2,1)} %get-tuple-element.36.refs_3_, bf16[4,4,256,128]{3,2,1,0:T(8,128)(2,1)} %copy-done.7), custom_call_target="tpu_custom_call" | custom-call | bytes 3000000 | tf_op jit(solution)/shard_map/mix/pallas_call | solution.py:69
  104.9 12.9 %all_to_all.87 = bf16[32,16,256]{2,1,0:T(8,128)(2,1)S(1)} all-to-all(bf16[32,16,256]{2,1,0:T(8,128)(2,1)S(1)} %bitcast.41), channel_id=1, replica_groups=mesh['section'=2,'gx'=4,'gy'=4] {'section','gx','gy'}, dimensions={0} | all-to-all | bytes 524288 | tf_op jit(solution)/shard_map/all_to_all | solution.py:692
  117.8 4.5 %back.1 = (f32[32,16,128]{2,1,0:T(8,128)}, bf16[512,256]{1,0:T(8,128)(2,1)S(1)}) custom-call(s32[1]{0:T(128)} %bitcast.refs_0_, bf16[48,32]{1,0:T(8,128)(2,1)S(1)} %pad_maximum_fusion.refs_2_.refs_1_, bf16[48,32]{1,0:T(8,128)(2,1)S(1)} %collective-permute-done.1.refs_3_.refs_2_, bf16[512,256]{1,0:T(8,128)(2,1)S(1)} %bitcast.31, ...), custom_call_target="tpu_custom_call" | custom-call | bytes 3000000 | tf_op jit(solution)/shard_map/back/pallas_call | solution.py:69
  122.3 13.6 %all_to_all.88 = bf16[32,16,256]{2,1,0:T(8,128)(2,1)} all-to-all(bf16[32,16,256]{2,1,0:T(8,128)(2,1)S(1)} %bitcast.37), channel_id=1, replica_groups=mesh['section'=2,'gx'=4,'gy'=4] {'section','gx','gy'}, dimensions={0} | all-to-all | bytes 524288 | tf_op jit(solution)/shard_map/all_to_all | solution.py:692
  136.0 2.6 %all-to-all-start.7 = ((f32[32,16,128]{2,1,0:T(8,128)}), f32[32,16,128]{2,1,0:T(8,128)S(1)}, u32[]{:S(2)}, u32[]{:S(2)}) async-start(f32[32,16,128]{2,1,0:T(8,128)} %get-tuple-element.56), calls=%async_computation.7 | async-start | bytes 524288 | tf_op jit(solution)/shard_map/all_to_all | solution.py:733
  138.6 0.9 copy-done.1
  139.5 0.9 spec.1
  140.7 1.4 collective-permute-done.3.refs_5_
  142.0 0.8 copy-done.5
  142.8 9.3 %outer.1.refs_1_ = f32[1,8,4,32,32,32]{5,4,3,2,1,0:T(8,128)} custom-call(s32[1]{0:T(128)} %bitcast.refs_0_, bf16[32,512]{1,0:T(8,128)(2,1)S(1)} %copy-done.2, bf16[32,512]{1,0:T(8,128)(2,1)S(1)} %copy-done.3, bf16[32,512]{1,0:T(8,128)(2,1)S(1)} %copy-done.5, bf16[32,512]{1,0:T(8,128)(2,1)S(1)} %copy-done.4, ...), custom_call_target="tpu_custom_call" | custom-call | bytes 20000000 | tf_op jit(solution)/shard_map/outer/pallas_call | solution.py:675
  152.1 0.7 finish.1
  (23 shorter events, 0.4 us)
Async XLA Ops:
  0.6 1.6 %copy-start = (bf16[1,32,16,16,128]{4,3,2,1,0:T(8,128)(2,1)S(1)}, bf16[1,32,16,16,128]{4,3,2,1,0:T(8,128)(2,1)}, u32[]{:S(2)}) copy-start(bf16[1,32,16,16,128]{4,3,2,1,0:T(8,128)(2,1)} %param.7) | copy-start | bytes 6291460
  0.6 3.2 %copy-start.8 = (bf16[1,32,32]{2,1,0:T(8,128)(2,1)S(1)}, bf16[1,32,32]{2,1,0:T(8,128)(2,1)}, u32[]{:S(2)}) copy-start(bf16[1,32,32]{2,1,0:T(8,128)(2,1)} %param.9) | copy-start | bytes 6148
  0.7 3.2 %copy-start.9 = (bf16[1,32]{1,0:T(2,128)(2,1)S(1)}, bf16[1,32]{1,0:T(2,128)(2,1)}, u32[]{:S(2)}) copy-start(bf16[1,32]{1,0:T(2,128)(2,1)} %param.10) | copy-start | bytes 196
  3.4 3.9 %collective-permute-start = (bf16[256,2048]{1,0:T(8,128)(2,1)}, bf16[256,2048]{1,0:T(8,128)(2,1)S(1)}, u32[]{:S(2)}, u32[]{:S(2)}) collective-permute-start(bf16[256,2048]{1,0:T(8,128)(2,1)} %dynamic-slice_bitcast_fusion.1), channel_id=1, source_target_pairs={{0,16},{16,0},{1,17},{17,1},{2,18},{18,2},{3,19},{19,3},{4,20},{20... | collective-permute-start | bytes 3145736 | tf_op jit(solution)/shard_map/ppermute | solution.py:696
  3.8 3.4 %collective-permute-start.1 = (bf16[48,32]{1,0:T(8,128)(2,1)S(1)}, bf16[48,32]{1,0:T(8,128)(2,1)S(1)}, u32[]{:S(2)}, u32[]{:S(2)}) collective-permute-start(bf16[48,32]{1,0:T(8,128)(2,1)S(1)} %pad_maximum_fusion.refs_2_.refs_1_), channel_id=1, source_target_pairs={{0,16},{16,0},{1,17},{17,1},{2,18},{18,2},{3,19},{19,3},{4,20},{20... | collective-permute-start | bytes 9224 | tf_op jit(solution)/shard_map/ppermute | solution.py:696
  7.3 1.0 copy-start.6
  15.7 18.6 %collective-permute-start.2 = (bf16[4,4,256,128]{3,2,1,0:T(8,128)(2,1)}, bf16[4,4,256,128]{3,2,1,0:T(8,128)(2,1)S(1)}, u32[]{:S(2)}, u32[]{:S(2)}) collective-permute-start(bf16[4,4,256,128]{3,2,1,0:T(8,128)(2,1)} %pack.3), channel_id=1, source_target_pairs={{0,16},{16,0},{1,17},{17,1},{2,18},{18,2},{3,19},{19,3},{4,20},{20... | collective-permute-start | bytes 3145736 | tf_op jit(solution)/shard_map/ppermute | solution.py:696
  16.2 18.2 %all-to-all-start = ((bf16[32,16,256]{2,1,0:T(8,128)(2,1)}), bf16[32,16,256]{2,1,0:T(8,128)(2,1)S(1)}, u32[]{:S(2)}, u32[]{:S(2)}) async-start(bf16[32,16,256]{2,1,0:T(8,128)(2,1)} %bitcast.43), calls=%async_computation | async-start | bytes 524288 | tf_op jit(solution)/shard_map/all_to_all | solution.py:692
  34.4 1.0 copy-start.7
  117.8 20.7 %copy-start.2 = (bf16[32,512]{1,0:T(8,128)(2,1)S(1)}, bf16[32,512]{1,0:T(8,128)(2,1)}, u32[]{:S(2)}) copy-start(bf16[32,512]{1,0:T(8,128)(2,1)} %get-tuple-element.37.refs_2_.refs_1_) | copy-start | bytes 98308
  117.8 20.7 %copy-start.3 = (bf16[32,512]{1,0:T(8,128)(2,1)S(1)}, bf16[32,512]{1,0:T(8,128)(2,1)}, u32[]{:S(2)}) copy-start(bf16[32,512]{1,0:T(8,128)(2,1)} %get-tuple-element.41.refs_3_.refs_2_) | copy-start | bytes 98308
  117.8 20.7 %copy-start.4 = (bf16[32,512]{1,0:T(8,128)(2,1)S(1)}, bf16[32,512]{1,0:T(8,128)(2,1)}, u32[]{:S(2)}) copy-start(bf16[32,512]{1,0:T(8,128)(2,1)} %get-tuple-element.53.refs_4_) | copy-start | bytes 98308
  136.0 16.1 %all-to-all-start.7 = ((f32[32,16,128]{2,1,0:T(8,128)}), f32[32,16,128]{2,1,0:T(8,128)S(1)}, u32[]{:S(2)}, u32[]{:S(2)}) async-start(f32[32,16,128]{2,1,0:T(8,128)} %get-tuple-element.56), calls=%async_computation.7 | async-start | bytes 524288 | tf_op jit(solution)/shard_map/all_to_all | solution.py:733
  138.6 1.0 copy-start.1
  140.5 1.5 %collective-permute-start.3 = (bf16[2,32,512]{2,1,0:T(8,128)(2,1)}, bf16[2,32,512]{2,1,0:T(8,128)(2,1)S(1)}, u32[]{:S(2)}, u32[]{:S(2)}) collective-permute-start(bf16[2,32,512]{2,1,0:T(8,128)(2,1)} %get-tuple-element.55), channel_id=1, source_target_pairs={{0,16},{16,0},{1,17},{17,1},{2,18},{18,2},{3,19},{19,3},{4,20},{20... | collective-permute-start | bytes 196616 | tf_op jit(solution)/shard_map/ppermute | solution.py:696
  142.0 0.8 copy-start.5

commit v2 on v1

--- a/solution.py
+++ b/solution.py
@@ -138,6 +138,9 @@
         self.groups = self.rows // 128
         self.lgs = self.modes_y // 8
         self.full_x = self.len_x * self.n_gx
+        self.fine = self.len_y // 2
+        self.thin = self.chans * self.fine
+        self.wide = 2 * self.cells
         self.full_y = full * self.n_gy
 
 
@@ -153,7 +156,9 @@
     sec, gy, yy = np.meshgrid(np.arange(2), np.arange(sz.n_gy), np.arange(sz.len_y), indexing="ij")
     row_y = (gy * 2 * sz.len_y + sec * sz.len_y + yy).reshape(-1)
     bx = np.moveaxis(bx[row_j].reshape(sz.modes, sz.n_gx, sz.len_x), 1, 0)
-    return bx, bz[row_k], np.repeat(by[:, row_y].T, sz.cpl, axis=1)
+    lines = by[:, row_y].T.reshape(sz.lines, 2, 1, sz.fine, sz.modes_y)
+    lines = np.broadcast_to(lines, (sz.lines, 2, 8 // sz.fine, sz.fine, sz.modes_y)).reshape(-1, sz.modes_y)
+    return bx, bz[row_k], np.repeat(lines, sz.cpl, axis=1)
 
 
 def activate(pre):
@@ -167,13 +172,13 @@
 
 
 def spread(sz):
-    shape = (sz.rows, sz.chans)
-    return (iota(shape, 0) // sz.len_y == iota(shape, 1)).astype(bf16)
+    shape = (sz.thin, sz.chans)
+    return (iota(shape, 0) // sz.fine == iota(shape, 1)).astype(bf16)
 
 
 def same_y(sz):
-    shape = (sz.rows, sz.rows)
-    return iota(shape, 0) % sz.len_y == iota(shape, 1) % sz.len_y
+    shape = (sz.thin, sz.thin)
+    return iota(shape, 0) % sz.fine == iota(shape, 1) % sz.fine
 
 
 def point_matrix(sz, weight, forward):
@@ -194,8 +199,9 @@
 
 def fill_table(sz, bx, bz, bb):
     depth = sz.depth
+    across, along = bx[...].astype(f32), bz[...].astype(f32)
     for x in range(sz.len_x):
-        bb[:, x * depth : (x + 1) * depth] = (bx[:, x : x + 1] * bz[...]).astype(bf16)
+        bb[:, x * depth : (x + 1) * depth] = (across[:, x : x + 1] * along).astype(bf16)
 
 
 def tables_kernel(sz, gx_ref, bx_hbm, bz_hbm, bb, bx, bz, sems):
@@ -214,105 +220,191 @@
         [(kept((sz.modes, sz.cells)), False)],
         [smem, hbm, hbm],
         (gx, bx, bz),
-        [pltpu.VMEM(bx.shape[1:], f32), pltpu.VMEM(bz.shape, f32)],
+        [pltpu.VMEM(bx.shape[1:], bf16), pltpu.VMEM(bz.shape, bf16)],
         2,
     )
     return bb
 
 
-def first_kernel(sz, s_ref, keep_hbm, recv_hbm, small_ref, bb, out_hbm, v, out, sems):
-    copies = Copies(sems)
-    (get_v,) = copies.choose(s_ref[0] == 0, [(keep_hbm, recv_hbm, v)])
-    get_v.wait()
+def reorder(sz):
+    dims = (sz.rows, sz.rows)
+    row = iota(dims, 0)
+    group, quarter = row // 128, row % 128 // 64
+    chan, y = group * sz.cpl + row % 64 // sz.fine, quarter * sz.fine + row % sz.fine
+    return (chan * sz.len_y + y == iota(dims, 1)).astype(bf16)
+
+
+def send_quarters(sz, gx_ref, field, mine_hbm, send_hbm, copies):
+    quarter = gx_ref[0] % 2
+    for h in range(sz.groups):
+        to = slice(h * 64, (h + 1) * 64)
+        copies.send(field.at[pl.ds(h * 128 + quarter * 64, 64)], mine_hbm.at[to])
+        copies.send(field.at[pl.ds(h * 128 + (1 - quarter) * 64, 64)], send_hbm.at[to])
+
+
+def wide_kernel(sz, gx_ref, bx_hbm, bz_hbm, after_hbm, bb_hbm, bx, bz, bb, sems):
+    copies = Copies(sems)
+    gets = [copies.start(bx_hbm.at[gx_ref[side]], bx.at[side]) for side in range(2)]
+    gets.append(copies.start(bz_hbm, bz))
+    for get in gets:
+        get.wait()
+    for side in range(2):
+        at = slice(side * sz.cells, (side + 1) * sz.cells)
+        fill_table(sz, bx.at[side], bz, bb.at[:, at])
+        copies.send(bb.at[:, at], bb_hbm.at[:, at])
+    copies.finish()
+
+
+def wide_call(sz, gx, bx, bz, after):
+    (bb,) = run(
+        "wide",
+        lambda *refs: wide_kernel(sz, *refs),
+        [(shape((sz.modes, sz.wide)), True)],
+        [smem, hbm, hbm, hbm],
+        (gx, bx, bz, after),
+        [pltpu.VMEM((2,) + bx.shape[1:], bf16), pltpu.VMEM(bz.shape, bf16), pltpu.VMEM((sz.modes, sz.wide), bf16)],
+        5,
+        0,
+    )
+    return bb
+
+
+def first_kernel(sz, s_ref, gx_ref, keep, recv, bb, mine_hbm, send_hbm, raw_hbm, out_hbm, v, out, sems):
+    copies = Copies(sems)
+    first = s_ref[0] == 0
+    (put_raw,) = copies.choose(first, [(recv, keep, raw_hbm)])
+    v[...] = nn(reorder(sz), jnp.where(first, keep[...], recv[...])).astype(bf16)
+    send_quarters(sz, gx_ref, v, mine_hbm, send_hbm, copies)
     send_analysis(sz, bb, v[...], out, 0)
     copies.send(out, out_hbm)
+    put_raw.wait()
     copies.finish()
 
 
-def first_call(sz, s, keep, recv, small, bb):
-    line = (sz.modes, sz.rows)
-    (out,) = run(
+def first_call(sz, s, gx, keep, recv, bb):
+    line, field, part = (sz.modes, sz.rows), (sz.rows, sz.cells), (sz.thin, sz.cells)
+    return run(
         "first",
         lambda *refs: first_kernel(sz, *refs),
-        [(shape(line), True)],
-        [smem, hbm, hbm, vmem, vmem],
-        (s, keep, recv, small, near(bb)),
-        [pltpu.VMEM((sz.rows, sz.cells), bf16), pltpu.VMEM(line, bf16)],
-        2,
-    )
-    return out
-
-
-def pack_kernel(sz, tables, w_ref, *rest):
+        [(shape(part), True), (shape(part), True), (shape(field), True), (shape(line), True)],
+        [smem, smem, vmem, vmem, vmem],
+        (s, gx, keep, recv, near(bb)),
+        [pltpu.VMEM(field, bf16), pltpu.VMEM(line, bf16)],
+        2 + 2 * sz.groups,
+    )
+
+
+def split_kernel(sz, gx_ref, raw_hbm, after_hbm, mine_hbm, send_hbm, raw, field, sems):
+    copies = Copies(sems)
+    copies.start(raw_hbm, raw).wait()
+    field[...] = nn(reorder(sz), raw[...]).astype(bf16)
+    send_quarters(sz, gx_ref, field, mine_hbm, send_hbm, copies)
+    copies.finish()
+
+
+def split_call(sz, gx, raw, after):
+    field, part = (sz.rows, sz.cells), (sz.thin, sz.cells)
+    return run(
+        "split",
+        lambda *refs: split_kernel(sz, *refs),
+        [(shape(part), True), (shape(part), True)],
+        [smem, hbm, hbm],
+        (gx, raw, after),
+        [pltpu.VMEM(field, bf16), pltpu.VMEM(field, bf16)],
+        1 + 2 * sz.groups,
+        0,
+    )
+
+
+def pack_kernel(sz, start, tables, *refs):
     if tables:
-        by_ref, out_ref, ya_ref = rest
-
-        @pl.when(pl.program_id(0) == 0)
-        def _():
-            wide = sz.modes_y * sz.cpl
-            lane_c = iota((sz.len_y, wide), 1) % sz.cpl
-            for g in range(sz.lines):
-                part = by_ref[g * sz.len_y : (g + 1) * sz.len_y, :]
-                block = jnp.concatenate([jnp.where(lane_c == c, part, 0.0) for c in range(sz.cpl)], axis=0)
-                ya_ref[g * 128 : (g + 1) * 128, :] = block.astype(bf16)
-
+        after_hbm, w_hbm, by_hbm, out_hbm, ya_hbm, w, out, by, ya, sems = refs
     else:
-        (out_ref,) = rest
-    width = sz.lgs * sz.chans
-    dims = (sz.chans, width)
-    places = [(iota(dims, 0) + lg * sz.chans == iota(dims, 1)).astype(bf16) for lg in range(sz.lgs)]
-    for kk in range(sz.blk_k):
-        total = None
-        for lg in range(sz.lgs):
-            rows = jnp.concatenate(
-                [
-                    w_ref[0, 0, kk, lg * 8 : (lg + 1) * 8, h * sz.cpl : (h + 1) * sz.cpl, :].reshape(128, sz.chans)
-                    for h in range(sz.groups)
-                ],
-                axis=0,
-            )
-            part = nn(rows, places[lg])
-            total = part if total is None else total + part
-        out_ref[0, kk] = total.astype(bf16)
-
-
-def pack_call(sz, weight, start, micros, by=None):
-    rows, width, half = sz.groups * 128, sz.lgs * sz.chans, sz.half_j
-    block = (1, sz.blk_k, rows, width)
+        after_hbm, w_hbm, out_hbm, w, out, sems = refs
+    copies = Copies(sems)
+    if tables:
+        get_by = copies.start(by_hbm, by)
+    gets = [copies.start(w_hbm.at[0, start + jj], w.at[jj]) for jj in range(sz.half_j)]
+    if tables:
+        get_by.wait()
+        table = by[...].astype(f32)
+        wide = sz.modes_y * sz.cpl
+        lane_c = iota((8, wide), 1) % sz.cpl
+        each = 8 // sz.fine
+        row_c = iota((8, wide), 0) // sz.fine
+        for g in range(sz.lines):
+            pieces = []
+            for quarter in range(2):
+                at = (g * 2 + quarter) * 8
+                part = table[at : at + 8, :]
+                pieces += [jnp.where(lane_c == c + row_c, part, 0.0) for c in range(0, sz.cpl, each)]
+            ya[g * 128 : (g + 1) * 128, :] = jnp.concatenate(pieces, axis=0).astype(bf16)
+        copies.send(ya, ya_hbm)
+    for jj in range(sz.half_j):
+        gets[jj].wait()
+        for kk in range(sz.blk_k):
+            for h in range(sz.groups):
+                lanes = [
+                    w[jj, kk, lg * 8 : (lg + 1) * 8, h * sz.cpl : (h + 1) * sz.cpl, :].reshape(128, sz.chans)
+                    for lg in range(sz.lgs)
+                ]
+                out[jj, kk, h * 128 : (h + 1) * 128, :] = jnp.concatenate(lanes, axis=1)
+        copies.send(out.at[jj], out_hbm.at[jj])
+    copies.finish()
+
+
+def pack_call(sz, after, weight, start, by=None):
+    half = sz.half_j
+    packed = (half, sz.blk_k, sz.groups * 128, sz.lgs * sz.chans)
     lines = (sz.lines * 128, sz.modes_y * sz.cpl)
-    packed = pltpu.HBM((half, sz.blk_k, rows, width), bf16)
+    outs = [(shape(packed), True)]
+    args = (after, weight)
+    scratch = [pltpu.VMEM((half,) + weight.shape[2:], bf16), pltpu.VMEM(packed, bf16)]
     tables = by is not None
-    weight_spec = pl.BlockSpec((1, 1) + weight.shape[2:], lambda i: (0, i + start, 0, 0, 0, 0))
-    packed_spec = pl.BlockSpec(block, lambda i: (i, 0, 0, 0))
-    return pl.pallas_call(
-        lambda *refs: pack_kernel(sz, tables, *refs),
-        grid=(half,),
-        out_shape=(packed, pltpu.HBM(lines, bf16)) if tables else packed,
-        in_specs=[weight_spec, pl.BlockSpec(by.shape, lambda i: (0, 0))] if tables else [weight_spec],
-        out_specs=(packed_spec, pl.BlockSpec(lines, lambda i: (0, 0))) if tables else packed_spec,
-        compiler_params=pltpu.CompilerParams(vmem_limit_bytes=limit),
-        cost_estimate=pl.CostEstimate(flops=0, transcendentals=0, bytes_accessed=micros * 3000000),
-        name="pack",
-    )(*([far(weight), far(by)] if tables else [far(weight)]))
-
-
-def line_analysis(sz, r_ref, ya_ref, get_ya):
+    if tables:
+        outs.append((shape(lines), True))
+        args += (by,)
+        scratch += [pltpu.VMEM(by.shape, bf16), pltpu.VMEM(lines, bf16)]
+    result = run(
+        "pack",
+        lambda *refs: pack_kernel(sz, start, tables, *refs),
+        outs,
+        [hbm] * len(args),
+        args,
+        scratch,
+        2 * half + 2 * tables,
+        0,
+    )
+    return result if tables else result[0]
+
+
+def line_analysis(sz, r_ref, ya_ref, get_ya, fine=True):
     jk = sz.jk
-    lines = []
+
+    def total(sec, gy, start, step):
+        result = None
+        for gx in range(start, sz.n_gx, step):
+            at = ((sec * sz.n_gx + gx) * sz.n_gy + gy) * jk
+            part = r_ref[at : at + jk, :].astype(f32)
+            result = part if result is None else result + part
+        return result
+
+    halves = [[], []]
+    low = iota((jk, 128), 1) < 64
     for sec in range(2):
         for gy in range(sz.n_gy):
-            total = None
-            for gx in range(sz.n_gx):
-                at = ((sec * sz.n_gx + gx) * sz.n_gy + gy) * jk
-                part = r_ref[at : at + jk, :].astype(f32)
-                total = part if total is None else total + part
-            lines.append(total.astype(bf16))
-    halves = [
-        jnp.concatenate([line[:, h * 128 : (h + 1) * 128] for line in lines], axis=1) for h in range(sz.groups)
-    ]
+            if fine:
+                a, b = total(sec, gy, 0, 2), total(sec, gy, 1, 2)
+                halves[0].append(jnp.where(low, a, pltpu.roll(b, 64, 1)).astype(bf16))
+                halves[1].append(jnp.where(low, pltpu.roll(a, 64, 1), b).astype(bf16))
+            else:
+                line = total(sec, gy, 0, 1).astype(bf16)
+                for h in range(sz.groups):
+                    halves[h].append(line[:, h * 128 : (h + 1) * 128])
+    rows = jnp.concatenate([jnp.concatenate(half, axis=1) for half in halves], axis=0)
     if get_ya is not None:
         get_ya.wait()
-    return nn(jnp.concatenate(halves, axis=0), ya_ref[...]).astype(bf16)
+    return nn(rows, ya_ref[...]).astype(bf16)
 
 
 def diagonal(sz, count):
@@ -361,16 +453,19 @@
 
 def send_lines(sz, rows, ya_ref, out_ref):
     jk = sz.jk
-    lines = nt(rows, ya_ref[...]).astype(bf16)
+    lines = nt(rows, ya_ref[...])
+    low = iota((jk, 128), 1) < 64
     for sec in range(2):
         for gy in range(sz.n_gy):
             line = sec * sz.n_gy + gy
-            block = jnp.concatenate(
-                [lines[h * jk : (h + 1) * jk, line * 128 : (line + 1) * 128] for h in range(sz.groups)], axis=1
-            )
+            a, b = [lines[h * jk : (h + 1) * jk, line * 128 : (line + 1) * 128] for h in range(2)]
+            quarters = [
+                jnp.where(low, a, pltpu.roll(b, 64, 1)).astype(bf16),
+                jnp.where(low, pltpu.roll(a, 64, 1), b).astype(bf16),
+            ]
             for gx in range(sz.n_gx):
                 at = ((sec * sz.n_gx + gx) * sz.n_gy + gy) * jk
-                out_ref[at : at + jk, :] = block
+                out_ref[at : at + jk, :] = quarters[gx % 2]
 
 
 def lane_group(sz):
@@ -378,7 +473,10 @@
     return iota(dims, 0) // (sz.jk * 8) == iota(dims, 1) // sz.chans
 
 
-def mix_kernel(sz, layer, turn, s_ref, r, ya_in, low_hbm, high_hbm, spec_hbm, out, *rest):
+def mix_kernel(sz, layer, turn, s_ref, r, ya_in, low_hbm, high_hbm, *rest):
+    if layer == 0:
+        rest = rest[3:]
+    spec_hbm, out, *rest = rest
     if layer == 0:
         ya, w, spec_b, blk, mix, sems = rest
     else:
@@ -387,7 +485,7 @@
     copies = Copies(sems)
     get_ya = copies.start(ya_in, ya) if layer == 0 else None
     get_w = copies.choose(s_ref[0] == layer, [(low_hbm.at[jj], high_hbm.at[jj], w.at[jj]) for jj in range(sz.half_j)])
-    spec = line_analysis(sz, r, ya, get_ya)
+    spec = line_analysis(sz, r, ya, get_ya, layer > 0)
     spec_b[...] = spec
     copies.send(spec_b, spec_hbm)
     count = sz.jk * 8
@@ -421,10 +519,10 @@
     copies.finish()
 
 
-def mix_call(sz, layer, turn, s, r, ya, low, high):
+def mix_call(sz, layer, turn, s, r, ya, low, high, after=()):
     count = sz.jk * 8 * sz.lgs
     spec = (sz.groups * sz.jk, sz.modes_y * sz.cpl)
-    line = (sz.modes, sz.rows)
+    line = (sz.modes, sz.thin)
     outs = [(shape(spec), True), (kept(line), False)]
     if layer == 0:
         outs.append((kept(ya.shape), False))
@@ -434,8 +532,8 @@
         "mix",
         lambda *refs: mix_kernel(sz, layer, turn, *refs),
         outs,
-        [smem, vmem, hbm if layer == 0 else vmem, hbm, hbm],
-        (s, r, ya, low, high),
+        [smem, vmem, hbm if layer == 0 else vmem, hbm, hbm] + [hbm] * len(after),
+        (s, r, ya, low, high) + after,
         [
             pltpu.VMEM(low.shape, bf16),
             pltpu.VMEM(spec, bf16),
@@ -446,15 +544,36 @@
     )
 
 
-def spec_kernel(sz, s_ref, r, sv0, sv1, su1, ya, out_hbm, send_hbm, out, sends, sems):
-    copies = Copies(sems)
+def gate_kernel(sz, in_ref, after_hbm, out_ref):
+    out_ref[...] = in_ref[...]
+
+
+def gate_call(sz, value, after):
+    (out,) = run(
+        "gate",
+        lambda *refs: gate_kernel(sz, *refs),
+        [(kept(value.shape), False)],
+        [vmem, hbm],
+        (near(value), after),
+        micros=0,
+    )
+    return out
+
+
+def spec_kernel(sz, s_ref, r, ya, sv0_hbm, sv1_hbm, su1_hbm, mine_hbm, send_hbm, before, mine, sends, sems):
+    copies = Copies(sems)
+    gets = [copies.start(src, before.at[at]) for at, src in enumerate((sv0_hbm, sv1_hbm, su1_hbm))]
     first = s_ref[0] == 0
     spec = line_analysis(sz, r, ya, None)
-    out[...] = spec
-    sends[0] = jnp.where(first, sv1[...], sv0[...])
-    sends[1] = jnp.where(first, su1[...], spec)
+    for get in gets:
+        get.wait()
+    sv0, sv1, su1 = [before[at] for at in range(3)]
+    sends[0] = jnp.where(first, sv1, sv0)
+    sends[1] = jnp.where(first, su1, spec)
     copies.send(sends, send_hbm)
-    copies.send(out, out_hbm)
+    mine[0] = jnp.where(first, sv0, sv1)
+    mine[1] = jnp.where(first, spec, su1)
+    copies.send(mine, mine_hbm)
     copies.finish()
 
 
@@ -463,11 +582,11 @@
     return run(
         "spec",
         lambda *refs: spec_kernel(sz, *refs),
-        [(shape(spec), True), (shape((2,) + spec), True)],
-        [smem] + [vmem] * 5,
-        (s, r, sv0, sv1, su1, near(ya)),
-        [pltpu.VMEM(spec, bf16), pltpu.VMEM((2,) + spec, bf16)],
-        2,
+        [(shape((2,) + spec), True), (shape((2,) + spec), True)],
+        [smem, vmem, vmem, hbm, hbm, hbm],
+        (s, r, near(ya), sv0, sv1, su1),
+        [pltpu.VMEM((3,) + spec, bf16), pltpu.VMEM((2,) + spec, bf16), pltpu.VMEM((2,) + spec, bf16)],
+        5,
     )
 
 
@@ -479,16 +598,11 @@
     return left
 
 
-CHUNK = 512
+CHUNK = 1024
 
 
 def cuts(sz):
-    return [slice(at, at + CHUNK) for at in range(0, sz.cells, CHUNK)]
-
-
-def buffers(sz, kinds):
-    dims = {"m": (sz.modes, sz.cells), "u": (sz.modes, sz.rows), "f": (sz.rows, sz.cells), "w": (sz.rows, sz.cells)}
-    return [pltpu.VMEM(dims[kind], f32 if kind == "w" else bf16) for kind in kinds]
+    return [slice(at, at + CHUNK) for at in range(0, sz.wide, CHUNK)]
 
 
 def small_parts(sz, s_ref, own_ref, other_ref, layer):
@@ -496,40 +610,57 @@
     return chosen[: sz.chans], chosen[sz.chans :]
 
 
+def field_copies(sz, copies, mine_hbm, other_hbm, field):
+    return [
+        copies.start(mine_hbm, field.at[:, : sz.cells]),
+        copies.start(other_hbm, field.at[:, sz.cells :]),
+    ]
+
+
+def thirds(value):
+    high = value.astype(bf16)
+    rest = value - high.astype(f32)
+    middle = rest.astype(bf16)
+    return [high, middle, (rest - middle.astype(f32)).astype(bf16)]
+
+
 def point_sums(sz, v, d):
     pairs = jnp.where(same_y(sz), nt(v, d), 0.0)
-    pairs = jnp.sum(pairs.reshape(sz.chans, sz.len_y, sz.rows), axis=1)
-    bias = nt(jnp.ones((8, sz.cells), bf16), d)
+    bias = nt(jnp.ones((8, sz.wide), bf16), d)
+    dims = (sz.chans, 3 * sz.thin)
+    fold = (iota(dims, 1) % sz.thin // sz.fine == iota(dims, 0)).astype(bf16)
+    pairs = nn(fold, jnp.concatenate(thirds(pairs), axis=0))
     part = sz.chans // 4
-    total = None
+    rows = []
     for t in range(4):
-        dims = (sz.rows, 128)
-        place = (iota(dims, 0) // sz.len_y + t * sz.chans == iota(dims, 1)).astype(f32)
-        both = pairs[t * part : (t + 1) * part]
-        both = jnp.concatenate([both, bias if t == 0 else jnp.zeros_like(bias)], axis=0)
-        term = lax.dot_general(
-            both, place, (((1,), (0,)), ((), ())), precision=lax.Precision.HIGHEST, preferred_element_type=f32
-        )
-        total = term if total is None else total + term
-    return total
+        below = bias if t == 0 else jnp.zeros_like(bias)
+        both = jnp.concatenate([pairs[t * part : (t + 1) * part], below], axis=0)
+        rows.append(jnp.concatenate(thirds(both), axis=0))
+    dims = (4 * sz.thin, 128)
+    row = iota(dims, 0)
+    place = (row // sz.thin * sz.chans + row % sz.thin // sz.fine == iota(dims, 1)).astype(bf16)
+    total = nn(jnp.concatenate(rows, axis=1), place)
+    count = part + 8
+    return total[:count] + total[count : 2 * count] + total[2 * count :]
 
 
 def forward_kernel(
-    sz, s_ref, gx_ref, own_ref, other_ref, u, keep_hbm, recv_hbm, bx_hbm, bz_hbm, v, slope, bb, out, field, bx, bz, sems
+    sz, s_ref, own_ref, other_ref, u, mine_hbm, next_hbm, bb_hbm, after_hbm, v, slope, bb, out, field, sems
 ):
     copies = Copies(sems)
-    get_bx = copies.start(bx_hbm.at[gx_ref[0]], bx)
-    get_bz = copies.start(bz_hbm, bz)
-    (get_v,) = copies.choose(s_ref[0] == 0, [(keep_hbm, recv_hbm, field)])
+    get_bb, get_v = [], []
+    for at, cut in enumerate(cuts(sz)):
+        get_bb.append(copies.start(bb_hbm.at[:, cut], bb.at[:, cut]))
+        if at == 0:
+            get_v = field_copies(sz, copies, mine_hbm, next_hbm, field)
     weight, bias = small_parts(sz, s_ref, own_ref, other_ref, 0)
     matrix = point_matrix(sz, weight, True)
     column = nt(spread(sz), bias)[:, :1]
     left = turned_modes(sz, u, 0)
-    get_bx.wait()
-    get_bz.wait()
-    fill_table(sz, bx, bz, bb)
-    get_v.wait()
-    for cut in cuts(sz):
+    for at, cut in enumerate(cuts(sz)):
+        get_bb[at].wait()
+        if cut.start % sz.cells == 0:
+            get_v[cut.start // sz.cells].wait()
         pre = nn(left, bb[:, cut]) + nn(matrix, field[:, cut]) + column
         value, rate = activate(pre)
         v[:, cut] = value.astype(bf16)
@@ -537,22 +668,22 @@
     send_analysis(sz, bb, v[...], out, 1)
 
 
-def forward_call(sz, s, gx, keep, recv, u, bx, bz, own, other):
-    field, line = (sz.rows, sz.cells), (sz.modes, sz.rows)
+def forward_call(sz, s, mine, other, u, bb, own_small, other_small, after):
+    field, line = (sz.thin, sz.wide), (sz.modes, sz.thin)
     return run(
         "forward",
         lambda *refs: forward_kernel(sz, *refs),
-        [(kept(field), False), (kept(field, f32), False), (kept((sz.modes, sz.cells)), False), (kept(line), False)],
-        [smem, smem, vmem, vmem, vmem, hbm, hbm, hbm, hbm],
-        (s, gx, own, other, u, keep, recv, bx, bz),
-        buffers(sz, "f") + [pltpu.VMEM(bx.shape[1:], f32), pltpu.VMEM(bz.shape, f32)],
-        3,
-    )
-
-
-def turn_kernel(sz, s_ref, own_ref, other_ref, u, v, bb, keep_hbm, recv_hbm, d, sums, out, grad, sems):
-    copies = Copies(sems)
-    (get_g,) = copies.choose(s_ref[0] == 0, [(recv_hbm, keep_hbm, grad)])
+        [(kept(field), False), (kept(field, f32), False), (kept((sz.modes, sz.wide)), False), (kept(line), False)],
+        [smem, vmem, vmem, vmem, hbm, hbm, hbm, hbm],
+        (s, own_small, other_small, u, mine, other, bb, after),
+        [pltpu.VMEM(field, bf16)],
+        2 + len(cuts(sz)),
+    )
+
+
+def turn_kernel(sz, s_ref, own_ref, other_ref, u, v, bb, mine_hbm, next_hbm, d, sums, out, grad, sems):
+    copies = Copies(sems)
+    get_g = field_copies(sz, copies, mine_hbm, next_hbm, grad)
     weight, bias = small_parts(sz, s_ref, own_ref, other_ref, 1)
     matrix = point_matrix(sz, weight, True)
     column = nt(spread(sz), bias)[:, :1]
@@ -561,28 +692,31 @@
         pre = nn(left, bb[:, cut]) + nn(matrix, v[:, cut]) + column
         _, rate = activate(pre)
         if at == 0:
-            get_g.wait()
+            for get in get_g:
+                get.wait()
         d[:, cut] = (grad[:, cut].astype(f32) * rate).astype(bf16)
     send_analysis(sz, bb, d[...], out, 1)
     sums[...] = point_sums(sz, v[...], d[...])
 
 
-def turn_call(sz, s, keep, recv, v, u, bb, own, other):
-    field, line = (sz.rows, sz.cells), (sz.modes, sz.rows)
+def turn_call(sz, s, mine, other, v, u, bb, own_small, other_small):
+    field, line = (sz.thin, sz.wide), (sz.modes, sz.thin)
     return run(
         "turn",
         lambda *refs: turn_kernel(sz, *refs),
         [(kept(field), False), (kept((sz.chans // 4 + 8, 128), f32), False), (kept(line), False)],
         [smem, vmem, vmem, vmem, vmem, vmem, hbm, hbm],
-        (s, own, other, u, near(v), near(bb), keep, recv),
-        buffers(sz, "f"),
-        1,
-    )
-
-
-def back_kernel(sz, s_ref, own_ref, other_ref, u, d, slope, bb, sums, keep_hbm, recv_hbm, parts_hbm, out, new, field, parts, sems):
-    copies = Copies(sems)
-    (get_v,) = copies.choose(s_ref[0] == 0, [(keep_hbm, recv_hbm, field)])
+        (s, own_small, other_small, u, near(v), near(bb), mine, other),
+        [pltpu.VMEM(field, bf16)],
+        2,
+    )
+
+
+def back_kernel(
+    sz, s_ref, own_ref, other_ref, u, d, slope, bb, sums, mine_hbm, next_hbm, parts, out, new, field, sems
+):
+    copies = Copies(sems)
+    get_v = field_copies(sz, copies, mine_hbm, next_hbm, field)
     weight, _ = small_parts(sz, s_ref, own_ref, other_ref, 1)
     matrix = point_matrix(sz, weight, False)
     left = turned_modes(sz, u, 1)
@@ -590,25 +724,24 @@
         grad = (nn(left, bb[:, cut]) + nn(matrix, d[:, cut])).astype(bf16).astype(f32)
         new[:, cut] = (grad * slope[:, cut]).astype(bf16)
     send_analysis(sz, bb, new[...], out, 0)
-    get_v.wait()
+    for get in get_v:
+        get.wait()
     first = point_sums(sz, field[...], new[...])
     half = sz.places // 2
     for place in range(half):
         parts[place] = first
         parts[half + place] = sums[...]
-    copies.send(parts, parts_hbm)
-    copies.finish()
-
-
-def back_call(sz, s, keep, recv, d, slope, u, bb, sums, own, other):
-    parts, line = (sz.places, sz.chans // 4 + 8, 128), (sz.modes, sz.rows)
+
+
+def back_call(sz, s, mine, other, d, slope, u, bb, sums, own_small, other_small):
+    parts, line, field = (sz.places, sz.chans // 4 + 8, 128), (sz.modes, sz.thin), (sz.thin, sz.wide)
     return run(
         "back",
         lambda *refs: back_kernel(sz, *refs),
-        [(shape(parts, f32), True), (kept(line), False)],
+        [(kept(parts, f32), False), (kept(line), False)],
         [smem] + [vmem] * 7 + [hbm, hbm],
-        (s, own, other, u, near(d), near(slope), near(bb), near(sums), keep, recv),
-        buffers(sz, "ff") + [pltpu.VMEM(parts, f32)],
+        (s, own_small, other_small, u, near(d), near(slope), near(bb), near(sums), mine, other),
+        [pltpu.VMEM(field, bf16), pltpu.VMEM(field, bf16)],
         2,
     )
 
@@ -632,7 +765,7 @@
     )(parts, far(after))
 
 
-def outer_kernel(sz, s_ref, sv0_ref, sv1_ref, su0_ref, su1_ref, theirs_ref, out_ref, left_ref, right_ref):
+def outer_kernel(sz, mine_ref, theirs_ref, out_ref, left_ref, right_ref):
     jk, groups, kk_count = sz.jk, sz.groups, sz.blk_k
     step = pl.program_id(0)
 
@@ -643,7 +776,7 @@
             rows = jnp.concatenate(
                 [sv[h * jk + jj * kk_count : h * jk + (jj + 1) * kk_count] for h in range(groups)], axis=0
             )
-            left_ref[place] = jnp.transpose(rows)
+            left_ref[place] = jnp.transpose(rows).astype(bf16)
         for lg in range(sz.lgs):
             flat = nn(to_blocks(sz, su, lg).astype(bf16), chan_lanes(sz))
             for at in range(jk):
@@ -652,40 +785,40 @@
 
     @pl.when(step == 0)
     def _():
-        first = s_ref[0] == 0
-        prepare(
-            0, jnp.where(first, sv0_ref[...], sv1_ref[...]), jnp.where(first, su0_ref[...], su1_ref[...])
-        )
+        prepare(0, mine_ref[0], mine_ref[1])
 
     @pl.when(step == 1)
     def _():
         prepare(1, theirs_ref[0], theirs_ref[1])
 
+    dims = (groups * kk_count, groups * kk_count * 128)
+    spread_lanes = (iota(dims, 0) == iota(dims, 1) // 128).astype(bf16)
+    columns = nn(left_ref[step], spread_lanes)
     for kk in range(kk_count):
-        for h in range(groups):
-            column = left_ref[step, :, h * kk_count + kk : h * kk_count + kk + 1]
-            for ll in range(sz.modes_y):
-                row = right_ref[step, kk, ll : ll + 1, :]
-                part = column[ll * sz.cpl : (ll + 1) * sz.cpl] * row
+        for ll in range(sz.modes_y):
+            row = right_ref[step, kk, ll : ll + 1, :]
+            for h in range(groups):
+                at = (h * kk_count + kk) * 128
+                part = columns[ll * sz.cpl : (ll + 1) * sz.cpl, at : at + sz.chans] * row
                 out_ref[0, 0, kk, ll, h * sz.cpl : (h + 1) * sz.cpl, :] = part
 
 
-def outer_call(sz, s, sv0, sv1, su0, su1, theirs):
+def outer_call(sz, mine, theirs):
     wide = sz.modes_y * sz.cpl
     return pl.pallas_call(
         lambda *refs: outer_kernel(sz, *refs),
         grid=(sz.blk_j,),
         out_shape=pltpu.HBM((1, sz.blk_j, sz.blk_k, sz.modes_y, sz.chans, sz.chans), f32),
-        in_specs=[smem] + [vmem] * 5,
+        in_specs=[vmem] * 2,
         out_specs=pl.BlockSpec((1, 1, sz.blk_k, sz.modes_y, sz.chans, sz.chans), lambda i: (0, i, 0, 0, 0, 0)),
         scratch_shapes=[
-            pltpu.VMEM((sz.blk_j, wide, sz.groups * sz.blk_k), f32),
+            pltpu.VMEM((sz.blk_j, wide, sz.groups * sz.blk_k), bf16),
             pltpu.VMEM((sz.blk_j, sz.blk_k, sz.modes_y, sz.chans), f32),
         ],
         compiler_params=pltpu.CompilerParams(vmem_limit_bytes=limit),
         cost_estimate=pl.CostEstimate(flops=0, transcendentals=0, bytes_accessed=20000000),
         name="outer",
-    )(s, sv0, sv1, su0, su1, theirs)
+    )(mine, theirs)
 
 
 def exchange(block):
@@ -694,6 +827,10 @@
 
 def swap(block):
     return lax.ppermute(block, "section", [(0, 1), (1, 0)])
+
+
+def swap_near(sz, block):
+    return lax.ppermute(block, "gx", [(i, i ^ 1) for i in range(sz.n_gx)])
 
 
 def local(ends, spectral_weight, point_weight, point_bias):
@@ -706,32 +843,36 @@
         part = lax.dynamic_slice_in_dim(field, which * sz.len_y, sz.len_y, axis=2)
         return jnp.swapaxes(part, 1, 2).reshape(sz.rows, sz.cells)
 
-    bx, bz, by = [jnp.asarray(t) for t in mode_tables(sz)]
+    bx, bz, by = [jnp.asarray(t.astype(ml_dtypes.bfloat16)) for t in mode_tables(sz)]
     send = half(ends[0], 1 - section)
     send, later = lax.optimization_barrier((send, ends[0]))
     recv = swap(send)
     keep = half(later, section)
-    gx = lax.axis_index("gx").astype(jnp.int32).reshape(1)
+    gx = lax.axis_index("gx").astype(jnp.int32)
+    gx = jnp.stack([gx, gx + 1 - 2 * (gx % 2)])
     bb = tables_call(sz, gx, bx, bz)
     own_small = jnp.concatenate([point_weight[0], jnp.broadcast_to(point_bias, (16, sz.chans))], axis=0)
     other_small = swap(own_small)
-
-    out = first_call(sz, s, keep, recv, other_small, bb)
-    out, weight = lax.optimization_barrier((out, spectral_weight))
+    mine_v, send_v, raw_g, out = first_call(sz, s, gx, keep, recv, bb)
+    next_v = swap_near(sz, send_v)
     r = exchange(out)
-    high = swap(pack_call(sz, weight, sz.half_j, 2))
-    low, ya = pack_call(sz, weight, 0, 6, by)
-    sv0, out, ya = mix_call(sz, 0, False, s, r, ya, low, high)
-    v1, slope0, bb, out = forward_call(sz, s, gx, keep, recv, exchange(out), bx, bz, own_small, other_small)
+    high = swap(pack_call(sz, mine_v, spectral_weight, sz.half_j))
+    mine_g, send_g = split_call(sz, gx, raw_g, mine_v)
+    next_g = swap_near(sz, send_g)
+    low, ya = pack_call(sz, mine_v, spectral_weight, 0, by)
+    sv0, out, ya = mix_call(sz, 0, False, s, r, ya, low, high, (other_small, mine_g, next_v))
+    bb = wide_call(sz, gx, bx, bz, sv0)
+    v1, slope0, bb, out = forward_call(sz, s, mine_v, next_v, exchange(out), bb, own_small, other_small, mine_g)
     sv1, out = mix_call(sz, 1, False, s, exchange(out), ya, low, high)
-    d1, sums, out = turn_call(sz, s, keep, recv, v1, exchange(out), bb, own_small, other_small)
+    out = gate_call(sz, out, next_g)
+    d1, sums, out = turn_call(sz, s, mine_g, next_g, v1, exchange(out), bb, own_small, other_small)
     su1, out = mix_call(sz, 1, True, s, exchange(out), ya, low, high)
-    parts, out = back_call(sz, s, keep, recv, d1, slope0, exchange(out), bb, sums, own_small, other_small)
+    parts, out = back_call(sz, s, mine_v, next_v, d1, slope0, exchange(out), bb, sums, own_small, other_small)
     r, parts = lax.optimization_barrier((exchange(out), parts))
-    su0, send = spec_call(sz, s, r, sv0, sv1, su1, ya)
+    mine, send = spec_call(sz, s, r, sv0, sv1, su1, ya)
     theirs = swap(send)
     parts = lax.all_to_all(parts, AXES, split_axis=0, concat_axis=0, tiled=True)
-    spectral_grad = outer_call(sz, s, sv0, sv1, su0, su1, theirs)
+    spectral_grad = outer_call(sz, mine, theirs)
     point_grad, bias_grad = finish_call(sz, parts, spectral_grad)
     return (spectral_grad, point_grad, bias_grad)
 

time: 154 us -> 138 us (0.90)
  blocking collectives: 78.2 us -> 50.1 us
  starting transfers between devices: 10.7 us -> 16.9 us
  Pallas kernels: 47.9 us -> 54 us
  waiting for transfers between devices: 7.64 us -> 10.5 us
  local copies, waits for them, and re-layouts: 7.44 us -> 5.2 us
    all_to_all x6 -> x5, blocking collectives: 78.2 us -> 50.1 us  [exchange(): return lax.all_to_all(block, AXES, split_axis=0, concat_axis=0, tiled=True)]
    pallas_call x9 -> x14, Pallas kernels: 28.2 us -> 45 us  [run(): pl.pallas_call(kernel, out_shape=tuple((pltpu.HBM(o.shape, o.dtype) if aw...]
    pallas_call x2 -> x0, Pallas kernels: 9.7 us -> none  [pack_call(): pl.pallas_call(lambda *refs: pack_kernel(sz, tables, *refs), grid=(half,)...]
    ppermute x0 -> x2, starting transfers between devices: none -> 4.58 us  [swap_near(): return lax.ppermute(block, 'gx', [(i, i ^ 1) for i in range(sz.n_gx)])]
    all_to_all x1 -> x2, waiting for transfers between devices: 6.28 us -> 9 us  [exchange(): return lax.all_to_all(block, AXES, split_axis=0, concat_axis=0, tiled=True)]
    all_to_all x1 -> x2, starting transfers between devices: 6.96 us -> 8.56 us  [exchange(): return lax.all_to_all(block, AXES, split_axis=0, concat_axis=0, tiled=True)]
    unnamed x20 -> x18, local copies, waits for them, and re-layouts: 5.27 us -> 4.04 us
  transfers between devices with their start and end apart: 6 -> 9, of which waited for: 2 -> 4; matrix products, arithmetic and copies ran while one was open for 1% -> 0% of each run, Pallas kernels for 11% -> 25%
where the time goes in v2:
time: 138 us
  Pallas kernels  54 us (39%)
  blocking collectives  50.1 us (36%)
  starting transfers between devices  16.9 us (12%)
  waiting for transfers between devices  10.5 us (8%)
  local copies, waits for them, and re-layouts  5.2 us (4%)
    all_to_all x5, blocking collectives, exchange(): return lax.all_to_all(block, AXES, split_axis=0, concat_axis=0, tiled=True)  50.1 us
    pallas_call x14, Pallas kernels, run(): pl.pallas_call(kernel, out_shape=tuple((pltpu.HBM(o.shape, o.dtype) if aw...  45 us
    all_to_all x2, waiting for transfers between devices, exchange(): return lax.all_to_all(block, AXES, split_axis=0, concat_axis=0, tiled=True)  9 us
    all_to_all x2, starting transfers between devices, exchange(): return lax.all_to_all(block, AXES, split_axis=0, concat_axis=0, tiled=True)  8.56 us
    pallas_call x1, Pallas kernels, outer_call(): pl.pallas_call(lambda *refs: outer_kernel(sz, *refs), grid=(sz.blk_j,), o...  8.27 us
    ppermute x2, starting transfers between devices, swap_near(): return lax.ppermute(block, 'gx', [(i, i ^ 1) for i in range(sz.n_gx)])  4.58 us
    unnamed x18, local copies, waits for them, and re-layouts  4.04 us
  transfers between devices with their start and end apart: 9, of which 4 were waited for; matrix products, arithmetic and copies ran while one was open for 0% of the time, Pallas kernels for 25%

profile of v2, /device:TPU:0, one launch (start us, length us, event | category | flops | bytes accessed | tf_op | source)
XLA Modules:
  0.0 137.6 jit_solution(13153516220879378239)
XLA Ops:
  0.7 1.6 %copy-done = bf16[1,32,16,16,128]{4,3,2,1,0:T(8,128)(2,1)S(1)} copy-done((bf16[1,32,16,16,128]{4,3,2,1,0:T(8,128)(2,1)S(1)}, bf16[1,32,16,16,128]{4,3,2,1,0:T(8,128)(2,1)}, u32[]{:S(2)}) %copy-start) | copy-done | bytes 2097176
  2.2 1.1 dynamic-slice_bitcast_fusion.1
  3.8 2.2 %tables.1.refs_4_ = bf16[512,2048]{1,0:T(8,128)(2,1)S(1)} custom-call(s32[2]{0:T(128)S(1)} %pad_add_fusion.refs_0_.refs_1_, bf16[4,512,16]{2,1,0:T(8,128)(2,1)} %constant.37.clone.refs_1_, bf16[512,128]{1,0:T(8,128)(2,1)} %constant.38.clone.refs_2_), custom_call_target="tpu_custom_call" | custom-call | bytes 3000000 | tf_op jit(solution)/shard_map/tables/pallas_call | solution.py:69
  6.2 2.6 %first.1 = (bf16[128,2048]{1,0:T(8,128)(2,1)}, bf16[128,2048]{1,0:T(8,128)(2,1)}, bf16[256,2048]{1,0:T(8,128)(2,1)}, bf16[512,256]{1,0:T(8,128)(2,1)}) custom-call(s32[1]{0:T(128)} %bitcast.refs_0_, s32[2]{0:T(128)S(1)} %pad_add_fusion.refs_0_.refs_1_, bf16[256,2048]{1,0:T(8,128)(2,1)S(1)} %dynamic-slice_bitcast_fusion.refs_2_, ...), custom_call_target="tpu_custom_call" | custom-call | bytes 3000000 | tf_op jit(solution)/shard_map/first/pallas_call | solution.py:69
  8.8 3.2 %pack.3 = bf16[4,4,256,128]{3,2,1,0:T(8,128)(2,1)} custom-call(bf16[128,2048]{1,0:T(8,128)(2,1)} %get-tuple-element.38.refs_0_.refs_2_.refs_4_.refs_8_, bf16[1,8,4,32,32,32]{5,4,3,2,1,0:T(8,128)(2,1)} %refs_1_.5), custom_call_target="tpu_custom_call" | custom-call | tf_op jit(solution)/shard_map/pack/pallas_call | solution.py:69
  12.5 2.7 %collective-permute-start.3 = (bf16[128,2048]{1,0:T(8,128)(2,1)}, bf16[128,2048]{1,0:T(8,128)(2,1)}, u32[]{:S(2)}, u32[]{:S(2)}) collective-permute-start(bf16[128,2048]{1,0:T(8,128)(2,1)} %get-tuple-element.43), channel_id=1, source_target_pairs={{0,4},{4,0},{8,12},{12,8},{1,5},{5,1},{9,13},{13,9},{2,6},{6,2},{1... | collective-permute-start | bytes 1572872 | tf_op jit(solution)/shard_map/ppermute | solution.py:833
  15.3 4.8 %all-to-all-start = ((bf16[32,16,256]{2,1,0:T(8,128)(2,1)}), bf16[32,16,256]{2,1,0:T(8,128)(2,1)S(1)}, u32[]{:S(2)}, u32[]{:S(2)}) async-start(bf16[32,16,256]{2,1,0:T(8,128)(2,1)} %bitcast.44), calls=%async_computation | async-start | bytes 524288 | tf_op jit(solution)/shard_map/all_to_all | solution.py:825
  20.1 3.2 %split.1 = (bf16[128,2048]{1,0:T(8,128)(2,1)}, bf16[128,2048]{1,0:T(8,128)(2,1)}) custom-call(s32[2]{0:T(128)S(1)} %pad_add_fusion.refs_0_.refs_1_, bf16[256,2048]{1,0:T(8,128)(2,1)} %get-tuple-element.41.refs_1_, bf16[128,2048]{1,0:T(8,128)(2,1)} %get-tuple-element.38.refs_0_.refs_2_.refs_4_.refs_8_), custom_call_target="tpu_custom_call" | custom-call | tf_op jit(solution)/shard_map/split/pallas_call | solution.py:69
  23.3 1.8 %collective-permute-start.4 = (bf16[128,2048]{1,0:T(8,128)(2,1)}, bf16[128,2048]{1,0:T(8,128)(2,1)}, u32[]{:S(2)}, u32[]{:S(2)}) collective-permute-start(bf16[128,2048]{1,0:T(8,128)(2,1)} %get-tuple-element.49), channel_id=1, source_target_pairs={{0,4},{4,0},{8,12},{12,8},{1,5},{5,1},{9,13},{13,9},{2,6},{6,2},{1... | collective-permute-start | bytes 1572872 | tf_op jit(solution)/shard_map/ppermute | solution.py:833
  25.3 3.8 %pack.2 = (bf16[4,4,256,128]{3,2,1,0:T(8,128)(2,1)}, bf16[1024,512]{1,0:T(8,128)(2,1)}) custom-call(bf16[128,2048]{1,0:T(8,128)(2,1)} %get-tuple-element.38.refs_0_.refs_2_.refs_4_.refs_8_, bf16[1,8,4,32,32,32]{5,4,3,2,1,0:T(8,128)(2,1)} %refs_1_.5, bf16[128,512]{1,0:T(8,128)(2,1)} %constant.39.clone.refs_2_), custom_call_target="tpu_custom_call" | custom-call | tf_op jit(solution)/shard_map/pack/pallas_call | solution.py:69
  29.1 5.8 %all-to-all-done = bf16[32,16,256]{2,1,0:T(8,128)(2,1)S(1)} async-done(((bf16[32,16,256]{2,1,0:T(8,128)(2,1)}), bf16[32,16,256]{2,1,0:T(8,128)(2,1)S(1)}, u32[]{:S(2)}, u32[]{:S(2)}) %all-to-all-start) | async-done | bytes 262176 | tf_op jit(solution)/shard_map/all_to_all | solution.py:825
  35.0 1.0 copy-done.6
  35.9 3.1 %mix.3 = (bf16[32,512]{1,0:T(8,128)(2,1)}, bf16[512,128]{1,0:T(8,128)(2,1)S(1)}, bf16[1024,512]{1,0:T(8,128)(2,1)S(1)}) custom-call(s32[1]{0:T(128)} %bitcast.refs_0_, bf16[512,256]{1,0:T(8,128)(2,1)S(1)} %bitcast.31, bf16[1024,512]{1,0:T(8,128)(2,1)} %get-tuple-element.39.refs_2_, bf16[4,4,256,128]{3,2,1,0:T(8,128)(2,1)} %get-tuple-element.40.refs_3_, ...), custom_call_target="tpu_custom_call" | custom-call | bytes 3000000 | tf_op jit(solution)/shard_map/mix/pallas_call | solution.py:69
  39.7 3.7 %all-to-all-start.1 = ((bf16[32,16,128]{2,1,0:T(8,128)(2,1)}), bf16[32,16,128]{2,1,0:T(8,128)(2,1)S(1)}, u32[]{:S(2)}, u32[]{:S(2)}) async-start(bf16[32,16,128]{2,1,0:T(8,128)(2,1)} %bitcast.39), calls=%async_computation.1 | async-start | bytes 262144 | tf_op jit(solution)/shard_map/all_to_all | solution.py:825
  43.5 4.7 %wide.1.refs_6_ = bf16[512,4096]{1,0:T(8,128)(2,1)} custom-call(s32[2]{0:T(128)S(1)} %pad_add_fusion.refs_0_.refs_1_, bf16[4,512,16]{2,1,0:T(8,128)(2,1)} %constant.37.clone.refs_1_, bf16[512,128]{1,0:T(8,128)(2,1)} %constant.38.clone.refs_2_, bf16[32,512]{1,0:T(8,128)(2,1)} %get-tuple-element.45.refs_3_), custom_call_target="tpu_custom_call" | custom-call | tf_op jit(solution)/shard_map/wide/pallas_call | solution.py:69
  48.2 3.2 %all-to-all-done.1 = bf16[32,16,128]{2,1,0:T(8,128)(2,1)S(1)} async-done(((bf16[32,16,128]{2,1,0:T(8,128)(2,1)}), bf16[32,16,128]{2,1,0:T(8,128)(2,1)S(1)}, u32[]{:S(2)}, u32[]{:S(2)}) %all-to-all-start.1) | async-done | bytes 131104 | tf_op jit(solution)/shard_map/all_to_all | solution.py:825
  51.4 5.0 %forward.1 = (bf16[128,4096]{1,0:T(8,128)(2,1)S(1)}, f32[128,4096]{1,0:T(8,128)S(1)}, bf16[512,4096]{1,0:T(8,128)(2,1)S(1)}, bf16[512,128]{1,0:T(8,128)(2,1)S(1)}) custom-call(s32[1]{0:T(128)} %bitcast.refs_0_, bf16[48,32]{1,0:T(8,128)(2,1)S(1)} %pad_maximum_fusion.refs_1_, bf16[48,32]{1,0:T(8,128)(2,1)S(1)} %copy-done.3, bf16[512,128]{1,0:T(8,128)(2,1)S(1)} %bitcast.33, ...), custom_call_target="tpu_custom_call" | custom-call | bytes 3000000 | tf_op jit(solution)/shard_map/forward/pallas_call | solution.py:69
  56.4 10.4 %all_to_all.83 = bf16[32,16,128]{2,1,0:T(8,128)(2,1)S(1)} all-to-all(bf16[32,16,128]{2,1,0:T(8,128)(2,1)S(1)} %bitcast.42), channel_id=1, replica_groups=mesh['section'=2,'gx'=4,'gy'=4] {'section','gx','gy'}, dimensions={0} | all-to-all | bytes 262144 | tf_op jit(solution)/shard_map/all_to_all | solution.py:825
  66.8 2.8 %mix.4 = (bf16[32,512]{1,0:T(8,128)(2,1)}, bf16[512,128]{1,0:T(8,128)(2,1)S(1)}) custom-call(s32[1]{0:T(128)} %bitcast.refs_0_, bf16[512,128]{1,0:T(8,128)(2,1)S(1)} %bitcast.37, bf16[1024,512]{1,0:T(8,128)(2,1)S(1)} %get-tuple-element.47.refs_2_, bf16[4,4,256,128]{3,2,1,0:T(8,128)(2,1)} %get-tuple-element.40.refs_3_, bf16[4,4,256,128]{3,2,1,0:T(8,128)(2,1)} %copy-done.6), custom_call_target="tpu_custom_call" | custom-call | bytes 3000000 | tf_op jit(solution)/shard_map/mix/pallas_call | solution.py:69
  69.6 9.9 %all_to_all.84 = bf16[32,16,128]{2,1,0:T(8,128)(2,1)S(1)} all-to-all(bf16[32,16,128]{2,1,0:T(8,128)(2,1)S(1)} %bitcast.38), channel_id=1, replica_groups=mesh['section'=2,'gx'=4,'gy'=4] {'section','gx','gy'}, dimensions={0} | all-to-all | bytes 262144 | tf_op jit(solution)/shard_map/all_to_all | solution.py:825
  79.5 4.6 %turn.1 = (bf16[128,4096]{1,0:T(8,128)(2,1)S(1)}, f32[16,128]{1,0:T(8,128)S(1)}, bf16[512,128]{1,0:T(8,128)(2,1)S(1)}) custom-call(s32[1]{0:T(128)} %bitcast.refs_0_, bf16[48,32]{1,0:T(8,128)(2,1)S(1)} %pad_maximum_fusion.refs_1_, bf16[48,32]{1,0:T(8,128)(2,1)S(1)} %copy-done.3, bf16[512,128]{1,0:T(8,128)(2,1)S(1)} %bitcast.35, ...), custom_call_target="tpu_custom_call" | custom-call | bytes 3000000 | tf_op jit(solution)/shard_map/turn/pallas_call | solution.py:69
  84.2 9.9 %all_to_all.85 = bf16[32,16,128]{2,1,0:T(8,128)(2,1)S(1)} all-to-all(bf16[32,16,128]{2,1,0:T(8,128)(2,1)S(1)} %bitcast.41), channel_id=1, replica_groups=mesh['section'=2,'gx'=4,'gy'=4] {'section','gx','gy'}, dimensions={0} | all-to-all | bytes 262144 | tf_op jit(solution)/shard_map/all_to_all | solution.py:825
  94.1 2.7 %mix.5 = (bf16[32,512]{1,0:T(8,128)(2,1)}, bf16[512,128]{1,0:T(8,128)(2,1)S(1)}) custom-call(s32[1]{0:T(128)} %bitcast.refs_0_, bf16[512,128]{1,0:T(8,128)(2,1)S(1)} %bitcast.36, bf16[1024,512]{1,0:T(8,128)(2,1)S(1)} %get-tuple-element.47.refs_2_, bf16[4,4,256,128]{3,2,1,0:T(8,128)(2,1)} %get-tuple-element.40.refs_3_, bf16[4,4,256,128]{3,2,1,0:T(8,128)(2,1)} %copy-done.6), custom_call_target="tpu_custom_call" | custom-call | bytes 3000000 | tf_op jit(solution)/shard_map/mix/pallas_call | solution.py:69
  96.8 9.9 %all_to_all.86 = bf16[32,16,128]{2,1,0:T(8,128)(2,1)S(1)} all-to-all(bf16[32,16,128]{2,1,0:T(8,128)(2,1)S(1)} %bitcast.43), channel_id=1, replica_groups=mesh['section'=2,'gx'=4,'gy'=4] {'section','gx','gy'}, dimensions={0} | all-to-all | bytes 262144 | tf_op jit(solution)/shard_map/all_to_all | solution.py:825
  106.7 5.3 %back.1 = (f32[32,16,128]{2,1,0:T(8,128)S(1)}, bf16[512,128]{1,0:T(8,128)(2,1)S(1)}) custom-call(s32[1]{0:T(128)} %bitcast.refs_0_, bf16[48,32]{1,0:T(8,128)(2,1)S(1)} %pad_maximum_fusion.refs_1_, bf16[48,32]{1,0:T(8,128)(2,1)S(1)} %copy-done.3, bf16[512,128]{1,0:T(8,128)(2,1)S(1)} %bitcast.32, bf16[128,4096]{1,0:T(8,128)(2,1)S(1)} %get-tuple-element.54.refs_4_, ...), custom_call_target="tpu_custom_call" | custom-call | bytes 3000000 | tf_op jit(solution)/shard_map/back/pallas_call | solution.py:69
  112.1 9.9 %all_to_all.87 = bf16[32,16,128]{2,1,0:T(8,128)(2,1)S(1)} all-to-all(bf16[32,16,128]{2,1,0:T(8,128)(2,1)S(1)} %bitcast.40), channel_id=1, replica_groups=mesh['section'=2,'gx'=4,'gy'=4] {'section','gx','gy'}, dimensions={0} | all-to-all | bytes 262144 | tf_op jit(solution)/shard_map/all_to_all | solution.py:825
  122.0 2.6 %all-to-all-start.7 = ((f32[32,16,128]{2,1,0:T(8,128)}), f32[32,16,128]{2,1,0:T(8,128)S(1)}, u32[]{:S(2)}, u32[]{:S(2)}) async-start(f32[32,16,128]{2,1,0:T(8,128)} %copy-done.1), calls=%async_computation.7 | async-start | bytes 524288 | tf_op jit(solution)/shard_map/all_to_all | solution.py:874
  124.6 1.7 %spec.1 = (bf16[2,32,512]{2,1,0:T(8,128)(2,1)}, bf16[2,32,512]{2,1,0:T(8,128)(2,1)}) custom-call(s32[1]{0:T(128)} %bitcast.refs_0_, bf16[512,128]{1,0:T(8,128)(2,1)S(1)} %bitcast.34, bf16[1024,512]{1,0:T(8,128)(2,1)S(1)} %get-tuple-element.47.refs_2_, bf16[32,512]{1,0:T(8,128)(2,1)} %get-tuple-element.45.refs_3_, bf16[32,512]{1,0:T(8,128)(2,1)} %get-tuple-element.60.refs_4_, ...), custom_call_target="tpu_custom_call" | custom-call | bytes 3000000 | tf_op jit(solution)/shard_map/spec/pallas_call | solution.py:69
  126.4 1.4 collective-permute-done.5.refs_1_
  127.8 0.8 copy-done.5
  128.6 8.3 %outer.1.refs_1_ = f32[1,8,4,32,32,32]{5,4,3,2,1,0:T(8,128)} custom-call(bf16[2,32,512]{2,1,0:T(8,128)(2,1)S(1)} %copy-done.5, bf16[2,32,512]{2,1,0:T(8,128)(2,1)S(1)} %collective-permute-done.5.refs_1_), custom_call_target="tpu_custom_call" | custom-call | bytes 20000000 | tf_op jit(solution)/shard_map/outer/pallas_call | solution.py:808
  136.9 0.7 finish.1
  (30 shorter events, 2.1 us)
Async XLA Ops:
  0.6 1.6 %copy-start = (bf16[1,32,16,16,128]{4,3,2,1,0:T(8,128)(2,1)S(1)}, bf16[1,32,16,16,128]{4,3,2,1,0:T(8,128)(2,1)}, u32[]{:S(2)}) copy-start(bf16[1,32,16,16,128]{4,3,2,1,0:T(8,128)(2,1)} %param.7) | copy-start | bytes 6291460
  3.3 3.0 %collective-permute-start.1 = (bf16[256,2048]{1,0:T(8,128)(2,1)}, bf16[256,2048]{1,0:T(8,128)(2,1)S(1)}, u32[]{:S(2)}, u32[]{:S(2)}) collective-permute-start(bf16[256,2048]{1,0:T(8,128)(2,1)} %dynamic-slice_bitcast_fusion.1), channel_id=1, source_target_pairs={{0,16},{16,0},{1,17},{17,1},{2,18},{18,2},{3,19},{19,3},{4,20},{20... | collective-permute-start | bytes 3145736 | tf_op jit(solution)/shard_map/ppermute | solution.py:829
  12.1 13.1 %copy-start.8 = (bf16[1,32]{1,0:T(2,128)(2,1)S(1)}, bf16[1,32]{1,0:T(2,128)(2,1)}, u32[]{:S(2)}) copy-start(bf16[1,32]{1,0:T(2,128)(2,1)} %param.10) | copy-start | bytes 196
  12.1 13.1 %copy-start.7 = (bf16[1,32,32]{2,1,0:T(8,128)(2,1)S(1)}, bf16[1,32,32]{2,1,0:T(8,128)(2,1)}, u32[]{:S(2)}) copy-start(bf16[1,32,32]{2,1,0:T(8,128)(2,1)} %param.9) | copy-start | bytes 6148
  12.1 22.9 %collective-permute-start.2 = (bf16[4,4,256,128]{3,2,1,0:T(8,128)(2,1)}, bf16[4,4,256,128]{3,2,1,0:T(8,128)(2,1)S(1)}, u32[]{:S(2)}, u32[]{:S(2)}) collective-permute-start(bf16[4,4,256,128]{3,2,1,0:T(8,128)(2,1)} %pack.3), channel_id=1, source_target_pairs={{0,16},{16,0},{1,17},{17,1},{2,18},{18,2},{3,19},{19,3},{4,20},{20... | collective-permute-start | bytes 3145736 | tf_op jit(solution)/shard_map/ppermute | solution.py:829
  12.5 22.4 %collective-permute-start.3 = (bf16[128,2048]{1,0:T(8,128)(2,1)}, bf16[128,2048]{1,0:T(8,128)(2,1)}, u32[]{:S(2)}, u32[]{:S(2)}) collective-permute-start(bf16[128,2048]{1,0:T(8,128)(2,1)} %get-tuple-element.43), channel_id=1, source_target_pairs={{0,4},{4,0},{8,12},{12,8},{1,5},{5,1},{9,13},{13,9},{2,6},{6,2},{1... | collective-permute-start | bytes 1572872 | tf_op jit(solution)/shard_map/ppermute | solution.py:833
  15.3 19.7 %all-to-all-start = ((bf16[32,16,256]{2,1,0:T(8,128)(2,1)}), bf16[32,16,256]{2,1,0:T(8,128)(2,1)S(1)}, u32[]{:S(2)}, u32[]{:S(2)}) async-start(bf16[32,16,256]{2,1,0:T(8,128)(2,1)} %bitcast.44), calls=%async_computation | async-start | bytes 524288 | tf_op jit(solution)/shard_map/all_to_all | solution.py:825
  23.3 46.3 %collective-permute-start.4 = (bf16[128,2048]{1,0:T(8,128)(2,1)}, bf16[128,2048]{1,0:T(8,128)(2,1)}, u32[]{:S(2)}, u32[]{:S(2)}) collective-permute-start(bf16[128,2048]{1,0:T(8,128)(2,1)} %get-tuple-element.49), channel_id=1, source_target_pairs={{0,4},{4,0},{8,12},{12,8},{1,5},{5,1},{9,13},{13,9},{2,6},{6,2},{1... | collective-permute-start | bytes 1572872 | tf_op jit(solution)/shard_map/ppermute | solution.py:833
  25.2 3.9 %collective-permute-start = (bf16[48,32]{1,0:T(8,128)(2,1)S(1)}, bf16[48,32]{1,0:T(8,128)(2,1)S(1)}, u32[]{:S(2)}, u32[]{:S(2)}) collective-permute-start(bf16[48,32]{1,0:T(8,128)(2,1)S(1)} %pad_maximum_fusion.refs_1_), channel_id=1, source_target_pairs={{0,16},{16,0},{1,17},{17,1},{2,18},{18,2},{3,19},{19,3},{4,20},{20... | collective-permute-start | bytes 9224 | tf_op jit(solution)/shard_map/ppermute | solution.py:829
  29.1 6.8 %copy-start.2 = (bf16[48,32]{1,0:T(8,128)(2,1)}, bf16[48,32]{1,0:T(8,128)(2,1)S(1)}, u32[]{:S(2)}) copy-start(bf16[48,32]{1,0:T(8,128)(2,1)S(1)} %collective-permute-done.refs_5_.refs_2_) | copy-start | bytes 9220
  35.0 1.0 copy-start.6
  39.1 0.6 copy-start.4
  39.7 11.7 %all-to-all-start.1 = ((bf16[32,16,128]{2,1,0:T(8,128)(2,1)}), bf16[32,16,128]{2,1,0:T(8,128)(2,1)S(1)}, u32[]{:S(2)}, u32[]{:S(2)}) async-start(bf16[32,16,128]{2,1,0:T(8,128)(2,1)} %bitcast.39), calls=%async_computation.1 | async-start | bytes 262144 | tf_op jit(solution)/shard_map/all_to_all | solution.py:825
  43.5 7.9 %copy-start.3 = (bf16[48,32]{1,0:T(8,128)(2,1)S(1)}, bf16[48,32]{1,0:T(8,128)(2,1)}, u32[]{:S(2)}) copy-start(bf16[48,32]{1,0:T(8,128)(2,1)} %copy-done.2) | copy-start | bytes 9220
  112.0 9.9 %copy-start.1 = (f32[32,16,128]{2,1,0:T(8,128)}, f32[32,16,128]{2,1,0:T(8,128)S(1)}, u32[]{:S(2)}) copy-start(f32[32,16,128]{2,1,0:T(8,128)S(1)} %get-tuple-element.64) | copy-start | bytes 786436
  122.0 14.9 %all-to-all-start.7 = ((f32[32,16,128]{2,1,0:T(8,128)}), f32[32,16,128]{2,1,0:T(8,128)S(1)}, u32[]{:S(2)}, u32[]{:S(2)}) async-start(f32[32,16,128]{2,1,0:T(8,128)} %copy-done.1), calls=%async_computation.7 | async-start | bytes 524288 | tf_op jit(solution)/shard_map/all_to_all | solution.py:874
  126.2 1.5 %collective-permute-start.5 = (bf16[2,32,512]{2,1,0:T(8,128)(2,1)}, bf16[2,32,512]{2,1,0:T(8,128)(2,1)S(1)}, u32[]{:S(2)}, u32[]{:S(2)}) collective-permute-start(bf16[2,32,512]{2,1,0:T(8,128)(2,1)} %get-tuple-element.63), channel_id=1, source_target_pairs={{0,16},{16,0},{1,17},{17,1},{2,18},{18,2},{3,19},{19,3},{4,20},{20... | collective-permute-start | bytes 196616 | tf_op jit(solution)/shard_map/ppermute | solution.py:829
  127.8 0.8 copy-start.5

commit v3 on v2

--- a/solution.py
+++ b/solution.py
@@ -473,18 +473,17 @@
     return iota(dims, 0) // (sz.jk * 8) == iota(dims, 1) // sz.chans
 
 
-def mix_kernel(sz, layer, turn, s_ref, r, ya_in, low_hbm, high_hbm, *rest):
+def mix_kernel(sz, layer, turn, s_ref, r, ya_in, *rest):
     if layer == 0:
-        rest = rest[3:]
-    spec_hbm, out, *rest = rest
-    if layer == 0:
-        ya, w, spec_b, blk, mix, sems = rest
+        low_hbm, high_hbm, *rest = rest
+        spec_hbm, out, ya, w, spec_b, blk, mix, sems = rest[3:]
     else:
         ya = ya_in
-        w, spec_b, blk, mix, sems = rest
+        w, spec_hbm, out, spec_b, blk, mix, sems = rest
     copies = Copies(sems)
     get_ya = copies.start(ya_in, ya) if layer == 0 else None
-    get_w = copies.choose(s_ref[0] == layer, [(low_hbm.at[jj], high_hbm.at[jj], w.at[jj]) for jj in range(sz.half_j)])
+    if layer == 0:
+        get_w = copies.choose(s_ref[0] == 0, [(low_hbm.at[jj], high_hbm.at[jj], w.at[jj]) for jj in range(sz.half_j)])
     spec = line_analysis(sz, r, ya, get_ya, layer > 0)
     spec_b[...] = spec
     copies.send(spec_b, spec_hbm)
@@ -502,7 +501,7 @@
         left_ref, right_ref, left_width = blk, mix, blk.shape[1]
     for jk in range(sz.jk):
         jj, kk = jk // sz.blk_k, jk % sz.blk_k
-        if kk == 0:
+        if kk == 0 and layer == 0:
             get_w[jj].wait()
         at = [slice((lg * sz.jk + jk) * 8, (lg * sz.jk + jk + 1) * 8) for lg in range(sz.lgs)]
         left = jnp.concatenate([left_ref[a, :left_width] for a in at], axis=0).astype(bf16)
@@ -519,27 +518,27 @@
     copies.finish()
 
 
-def mix_call(sz, layer, turn, s, r, ya, low, high, after=()):
+def mix_call(sz, layer, turn, s, r, ya, weights, after=()):
     count = sz.jk * 8 * sz.lgs
     spec = (sz.groups * sz.jk, sz.modes_y * sz.cpl)
     line = (sz.modes, sz.thin)
     outs = [(shape(spec), True), (kept(line), False)]
+    scratch = [pltpu.VMEM(spec, bf16)] + [pltpu.VMEM((count, sz.groups * 128), f32)] * 2
     if layer == 0:
         outs.append((kept(ya.shape), False))
+        scratch = [pltpu.VMEM(weights[0].shape, bf16)] + scratch
+        specs = [smem, vmem] + [hbm] * (3 + len(after))
     else:
         ya = near(ya)
+        weights = [near(weights)]
+        specs = [smem] + [vmem] * 3
     return run(
         "mix",
         lambda *refs: mix_kernel(sz, layer, turn, *refs),
         outs,
-        [smem, vmem, hbm if layer == 0 else vmem, hbm, hbm] + [hbm] * len(after),
-        (s, r, ya, low, high) + after,
-        [
-            pltpu.VMEM(low.shape, bf16),
-            pltpu.VMEM(spec, bf16),
-            pltpu.VMEM((count, sz.groups * 128), f32),
-            pltpu.VMEM((count, sz.groups * 128), f32),
-        ],
+        specs,
+        (s, r, ya, *weights, *after),
+        scratch,
         sz.half_j + 2,
     )
 
@@ -560,7 +559,7 @@
     return out
 
 
-def spec_kernel(sz, s_ref, r, ya, sv0_hbm, sv1_hbm, su1_hbm, mine_hbm, send_hbm, before, mine, sends, sems):
+def spec_kernel(sz, s_ref, r, ya, sv0_hbm, sv1_hbm, su1_hbm, mine, sends, before, sems):
     copies = Copies(sems)
     gets = [copies.start(src, before.at[at]) for at, src in enumerate((sv0_hbm, sv1_hbm, su1_hbm))]
     first = s_ref[0] == 0
@@ -570,11 +569,8 @@
     sv0, sv1, su1 = [before[at] for at in range(3)]
     sends[0] = jnp.where(first, sv1, sv0)
     sends[1] = jnp.where(first, su1, spec)
-    copies.send(sends, send_hbm)
     mine[0] = jnp.where(first, sv0, sv1)
     mine[1] = jnp.where(first, spec, su1)
-    copies.send(mine, mine_hbm)
-    copies.finish()
 
 
 def spec_call(sz, s, r, sv0, sv1, su1, ya):
@@ -582,11 +578,11 @@
     return run(
         "spec",
         lambda *refs: spec_kernel(sz, *refs),
-        [(shape((2,) + spec), True), (shape((2,) + spec), True)],
+        [(kept((2,) + spec), False), (kept((2,) + spec), False)],
         [smem, vmem, vmem, hbm, hbm, hbm],
         (s, r, near(ya), sv0, sv1, su1),
-        [pltpu.VMEM((3,) + spec, bf16), pltpu.VMEM((2,) + spec, bf16), pltpu.VMEM((2,) + spec, bf16)],
-        5,
+        [pltpu.VMEM((3,) + spec, bf16)],
+        3,
     )
 
 
@@ -645,7 +641,7 @@
 
 
 def forward_kernel(
-    sz, s_ref, own_ref, other_ref, u, mine_hbm, next_hbm, bb_hbm, after_hbm, v, slope, bb, out, field, sems
+    sz, s_ref, own_ref, other_ref, u, mine_hbm, next_hbm, bb_hbm, low_hbm, high_hbm, v, slope, bb, out, w, field, sems
 ):
     copies = Copies(sems)
     get_bb, get_v = [], []
@@ -653,6 +649,7 @@
         get_bb.append(copies.start(bb_hbm.at[:, cut], bb.at[:, cut]))
         if at == 0:
             get_v = field_copies(sz, copies, mine_hbm, next_hbm, field)
+    (get_w,) = copies.choose(s_ref[0] == 1, [(low_hbm, high_hbm, w)])
     weight, bias = small_parts(sz, s_ref, own_ref, other_ref, 0)
     matrix = point_matrix(sz, weight, True)
     column = nt(spread(sz), bias)[:, :1]
@@ -666,18 +663,25 @@
         v[:, cut] = value.astype(bf16)
         slope[:, cut] = rate
     send_analysis(sz, bb, v[...], out, 1)
-
-
-def forward_call(sz, s, mine, other, u, bb, own_small, other_small, after):
+    get_w.wait()
+
+
+def forward_call(sz, s, mine, other, u, bb, own_small, other_small, low, high):
     field, line = (sz.thin, sz.wide), (sz.modes, sz.thin)
     return run(
         "forward",
         lambda *refs: forward_kernel(sz, *refs),
-        [(kept(field), False), (kept(field, f32), False), (kept((sz.modes, sz.wide)), False), (kept(line), False)],
-        [smem, vmem, vmem, vmem, hbm, hbm, hbm, hbm],
-        (s, own_small, other_small, u, mine, other, bb, after),
+        [
+            (kept(field), False),
+            (kept(field, f32), False),
+            (kept((sz.modes, sz.wide)), False),
+            (kept(line), False),
+            (kept(low.shape), False),
+        ],
+        [smem, vmem, vmem, vmem, hbm, hbm, hbm, hbm, hbm],
+        (s, own_small, other_small, u, mine, other, bb, low, high),
         [pltpu.VMEM(field, bf16)],
-        2 + len(cuts(sz)),
+        3 + len(cuts(sz)),
     )
 
 
@@ -723,9 +727,9 @@
     for cut in cuts(sz):
         grad = (nn(left, bb[:, cut]) + nn(matrix, d[:, cut])).astype(bf16).astype(f32)
         new[:, cut] = (grad * slope[:, cut]).astype(bf16)
-    send_analysis(sz, bb, new[...], out, 0)
     for get in get_v:
         get.wait()
+    send_analysis(sz, bb, new[...], out, 0)
     first = point_sums(sz, field[...], new[...])
     half = sz.places // 2
     for place in range(half):
@@ -818,7 +822,7 @@
         compiler_params=pltpu.CompilerParams(vmem_limit_bytes=limit),
         cost_estimate=pl.CostEstimate(flops=0, transcendentals=0, bytes_accessed=20000000),
         name="outer",
-    )(mine, theirs)
+    )(near(mine), theirs)
 
 
 def exchange(block):
@@ -860,13 +864,13 @@
     mine_g, send_g = split_call(sz, gx, raw_g, mine_v)
     next_g = swap_near(sz, send_g)
     low, ya = pack_call(sz, mine_v, spectral_weight, 0, by)
-    sv0, out, ya = mix_call(sz, 0, False, s, r, ya, low, high, (other_small, mine_g, next_v))
+    sv0, out, ya = mix_call(sz, 0, False, s, r, ya, (low, high), (other_small, mine_g, next_v))
     bb = wide_call(sz, gx, bx, bz, sv0)
-    v1, slope0, bb, out = forward_call(sz, s, mine_v, next_v, exchange(out), bb, own_small, other_small, mine_g)
-    sv1, out = mix_call(sz, 1, False, s, exchange(out), ya, low, high)
+    v1, slope0, bb, out, w1 = forward_call(sz, s, mine_v, next_v, exchange(out), bb, own_small, other_small, low, high)
+    sv1, out = mix_call(sz, 1, False, s, exchange(out), ya, w1)
     out = gate_call(sz, out, next_g)
     d1, sums, out = turn_call(sz, s, mine_g, next_g, v1, exchange(out), bb, own_small, other_small)
-    su1, out = mix_call(sz, 1, True, s, exchange(out), ya, low, high)
+    su1, out = mix_call(sz, 1, True, s, exchange(out), ya, w1)
     parts, out = back_call(sz, s, mine_v, next_v, d1, slope0, exchange(out), bb, sums, own_small, other_small)
     r, parts = lax.optimization_barrier((exchange(out), parts))
     mine, send = spec_call(sz, s, r, sv0, sv1, su1, ya)

time: 138 us -> 133 us (0.964)
  Pallas kernels: 54 us -> 48.9 us
    pallas_call x14, Pallas kernels: 45 us -> 40 us  [run(): pl.pallas_call(kernel, out_shape=tuple((pltpu.HBM(o.shape, o.dtype) if aw...]
    unnamed x18 -> x16, local copies, waits for them, and re-layouts: 4.04 us -> 3.04 us
  transfers between devices with their start and end apart: 9 -> 9, of which waited for: 4 -> 5; matrix products, arithmetic and copies ran while one was open for 0% -> 0% of each run, Pallas kernels for 25% -> 25%
where the time goes in v3:
time: 133 us; the launch traced here: 132 us
  blocking collectives  50.1 us (38%)
  Pallas kernels  48.9 us (37%)
  starting transfers between devices  16.9 us (13%)
  waiting for transfers between devices  10.8 us (8%)
  local copies, waits for them, and re-layouts  4.19 us (3%)
    all_to_all x5, blocking collectives, exchange(): return lax.all_to_all(block, AXES, split_axis=0, concat_axis=0, tiled=True)  50.1 us
    pallas_call x14, Pallas kernels, run(): pl.pallas_call(kernel, out_shape=tuple((pltpu.HBM(o.shape, o.dtype) if aw...  40 us
    all_to_all x2, waiting for transfers between devices, exchange(): return lax.all_to_all(block, AXES, split_axis=0, concat_axis=0, tiled=True)  8.99 us
    all_to_all x2, starting transfers between devices, exchange(): return lax.all_to_all(block, AXES, split_axis=0, concat_axis=0, tiled=True)  8.56 us
    pallas_call x1, Pallas kernels, outer_call(): pl.pallas_call(lambda *refs: outer_kernel(sz, *refs), grid=(sz.blk_j,), o...  8.28 us
    ppermute x2, starting transfers between devices, swap_near(): return lax.ppermute(block, 'gx', [(i, i ^ 1) for i in range(sz.n_gx)])  4.58 us
    unnamed x16, local copies, waits for them, and re-layouts  3.04 us
  transfers between devices with their start and end apart: 9, of which 5 were waited for; matrix products, arithmetic and copies ran while one was open for 0% of the time, Pallas kernels for 25%

profile of v3, /device:TPU:0, one launch (start us, length us, event | category | flops | bytes accessed | tf_op | source)
XLA Modules:
  0.0 131.9 jit_solution(6039007465923683327)
XLA Ops:
  0.7 1.6 %copy-done = bf16[1,32,16,16,128]{4,3,2,1,0:T(8,128)(2,1)S(1)} copy-done((bf16[1,32,16,16,128]{4,3,2,1,0:T(8,128)(2,1)S(1)}, bf16[1,32,16,16,128]{4,3,2,1,0:T(8,128)(2,1)}, u32[]{:S(2)}) %copy-start) | copy-done | bytes 2097176
  2.2 1.1 dynamic-slice_bitcast_fusion.1
  3.8 2.2 %tables.1.refs_4_ = bf16[512,2048]{1,0:T(8,128)(2,1)S(1)} custom-call(s32[2]{0:T(128)S(1)} %pad_add_fusion.refs_0_.refs_1_, bf16[4,512,16]{2,1,0:T(8,128)(2,1)} %constant.37.clone.refs_1_, bf16[512,128]{1,0:T(8,128)(2,1)} %constant.38.clone.refs_2_), custom_call_target="tpu_custom_call" | custom-call | bytes 3000000 | tf_op jit(solution)/shard_map/tables/pallas_call | solution.py:69
  6.2 2.6 %first.1 = (bf16[128,2048]{1,0:T(8,128)(2,1)}, bf16[128,2048]{1,0:T(8,128)(2,1)}, bf16[256,2048]{1,0:T(8,128)(2,1)}, bf16[512,256]{1,0:T(8,128)(2,1)}) custom-call(s32[1]{0:T(128)} %bitcast.refs_0_, s32[2]{0:T(128)S(1)} %pad_add_fusion.refs_0_.refs_1_, bf16[256,2048]{1,0:T(8,128)(2,1)S(1)} %dynamic-slice_bitcast_fusion.refs_2_, ...), custom_call_target="tpu_custom_call" | custom-call | bytes 3000000 | tf_op jit(solution)/shard_map/first/pallas_call | solution.py:69
  8.8 3.2 %pack.3 = bf16[4,4,256,128]{3,2,1,0:T(8,128)(2,1)} custom-call(bf16[128,2048]{1,0:T(8,128)(2,1)} %get-tuple-element.39.refs_0_.refs_2_.refs_4_.refs_8_, bf16[1,8,4,32,32,32]{5,4,3,2,1,0:T(8,128)(2,1)} %refs_1_.5), custom_call_target="tpu_custom_call" | custom-call | tf_op jit(solution)/shard_map/pack/pallas_call | solution.py:69
  12.5 2.7 %collective-permute-start.3 = (bf16[128,2048]{1,0:T(8,128)(2,1)}, bf16[128,2048]{1,0:T(8,128)(2,1)S(1)}, u32[]{:S(2)}, u32[]{:S(2)}) collective-permute-start(bf16[128,2048]{1,0:T(8,128)(2,1)} %get-tuple-element.44), channel_id=1, source_target_pairs={{0,4},{4,0},{8,12},{12,8},{1,5},{5,1},{9,13},{13,9},{2,6},{6,2},{1... | collective-permute-start | bytes 1572872 | tf_op jit(solution)/shard_map/ppermute | solution.py:837
  15.3 4.8 %all-to-all-start = ((bf16[32,16,256]{2,1,0:T(8,128)(2,1)}), bf16[32,16,256]{2,1,0:T(8,128)(2,1)S(1)}, u32[]{:S(2)}, u32[]{:S(2)}) async-start(bf16[32,16,256]{2,1,0:T(8,128)(2,1)} %bitcast.11), calls=%async_computation | async-start | bytes 524288 | tf_op jit(solution)/shard_map/all_to_all | solution.py:829
  20.1 3.2 %split.1 = (bf16[128,2048]{1,0:T(8,128)(2,1)}, bf16[128,2048]{1,0:T(8,128)(2,1)}) custom-call(s32[2]{0:T(128)S(1)} %pad_add_fusion.refs_0_.refs_1_, bf16[256,2048]{1,0:T(8,128)(2,1)} %get-tuple-element.42.refs_1_, bf16[128,2048]{1,0:T(8,128)(2,1)} %get-tuple-element.39.refs_0_.refs_2_.refs_4_.refs_8_), custom_call_target="tpu_custom_call" | custom-call | tf_op jit(solution)/shard_map/split/pallas_call | solution.py:69
  23.3 1.8 %collective-permute-start.4 = (bf16[128,2048]{1,0:T(8,128)(2,1)}, bf16[128,2048]{1,0:T(8,128)(2,1)}, u32[]{:S(2)}, u32[]{:S(2)}) collective-permute-start(bf16[128,2048]{1,0:T(8,128)(2,1)} %get-tuple-element.51), channel_id=1, source_target_pairs={{0,4},{4,0},{8,12},{12,8},{1,5},{5,1},{9,13},{13,9},{2,6},{6,2},{1... | collective-permute-start | bytes 1572872 | tf_op jit(solution)/shard_map/ppermute | solution.py:837
  25.3 3.8 %pack.2 = (bf16[4,4,256,128]{3,2,1,0:T(8,128)(2,1)}, bf16[1024,512]{1,0:T(8,128)(2,1)}) custom-call(bf16[128,2048]{1,0:T(8,128)(2,1)} %get-tuple-element.39.refs_0_.refs_2_.refs_4_.refs_8_, bf16[1,8,4,32,32,32]{5,4,3,2,1,0:T(8,128)(2,1)} %refs_1_.5, bf16[128,512]{1,0:T(8,128)(2,1)} %constant.39.clone.refs_2_), custom_call_target="tpu_custom_call" | custom-call | tf_op jit(solution)/shard_map/pack/pallas_call | solution.py:69
  29.1 5.8 %all-to-all-done = bf16[32,16,256]{2,1,0:T(8,128)(2,1)S(1)} async-done(((bf16[32,16,256]{2,1,0:T(8,128)(2,1)}), bf16[32,16,256]{2,1,0:T(8,128)(2,1)S(1)}, u32[]{:S(2)}, u32[]{:S(2)}) %all-to-all-start) | async-done | bytes 262176 | tf_op jit(solution)/shard_map/all_to_all | solution.py:829
  35.0 0.8 copy-done.5
  35.8 3.2 %mix.3 = (bf16[32,512]{1,0:T(8,128)(2,1)}, bf16[512,128]{1,0:T(8,128)(2,1)S(1)}, bf16[1024,512]{1,0:T(8,128)(2,1)S(1)}) custom-call(s32[1]{0:T(128)} %bitcast.refs_0_, bf16[512,256]{1,0:T(8,128)(2,1)S(1)} %bitcast.31, bf16[1024,512]{1,0:T(8,128)(2,1)} %get-tuple-element.40.refs_2_, bf16[4,4,256,128]{3,2,1,0:T(8,128)(2,1)} %get-tuple-element.41.refs_3_.refs_7_, ...), custom_call_target="tpu_custom_call" | custom-call | bytes 3000000 | tf_op jit(solution)/shard_map/mix/pallas_call | solution.py:69
  38.9 0.6 copy-done.4
  39.6 3.7 %all-to-all-start.1 = ((bf16[32,16,128]{2,1,0:T(8,128)(2,1)}), bf16[32,16,128]{2,1,0:T(8,128)(2,1)S(1)}, u32[]{:S(2)}, u32[]{:S(2)}) async-start(bf16[32,16,128]{2,1,0:T(8,128)(2,1)} %bitcast.39), calls=%async_computation.1 | async-start | bytes 262144 | tf_op jit(solution)/shard_map/all_to_all | solution.py:829
  43.3 4.7 %wide.1.refs_6_ = bf16[512,4096]{1,0:T(8,128)(2,1)} custom-call(s32[2]{0:T(128)S(1)} %pad_add_fusion.refs_0_.refs_1_, bf16[4,512,16]{2,1,0:T(8,128)(2,1)} %constant.37.clone.refs_1_, bf16[512,128]{1,0:T(8,128)(2,1)} %constant.38.clone.refs_2_, bf16[32,512]{1,0:T(8,128)(2,1)} %get-tuple-element.46.refs_3_), custom_call_target="tpu_custom_call" | custom-call | tf_op jit(solution)/shard_map/wide/pallas_call | solution.py:69
  48.1 3.2 %all-to-all-done.1 = bf16[32,16,128]{2,1,0:T(8,128)(2,1)S(1)} async-done(((bf16[32,16,128]{2,1,0:T(8,128)(2,1)}), bf16[32,16,128]{2,1,0:T(8,128)(2,1)S(1)}, u32[]{:S(2)}, u32[]{:S(2)}) %all-to-all-start.1) | async-done | bytes 131104 | tf_op jit(solution)/shard_map/all_to_all | solution.py:829
  51.2 5.0 %forward.1 = (bf16[128,4096]{1,0:T(8,128)(2,1)S(1)}, f32[128,4096]{1,0:T(8,128)S(1)}, bf16[512,4096]{1,0:T(8,128)(2,1)S(1)}, bf16[512,128]{1,0:T(8,128)(2,1)S(1)}, bf16[4,4,256,128]{3,2,1,0:T(8,128)(2,1)S(1)}) custom-call(s32[1]{0:T(128)} %bitcast.refs_0_, bf16[48,32]{1,0:T(8,128)(2,1)S(1)} %pad_maximum_fusion.refs_1_, bf16[48,32]{1,0:T(8,128)(2,1)S(1)} %copy-done.3, ...), custom_call_target="tpu_custom_call" | custom-call | bytes 3000000 | tf_op jit(solution)/shard_map/forward/pallas_call | solution.py:69
  56.2 10.4 %all_to_all.83 = bf16[32,16,128]{2,1,0:T(8,128)(2,1)S(1)} all-to-all(bf16[32,16,128]{2,1,0:T(8,128)(2,1)S(1)} %bitcast.41), channel_id=1, replica_groups=mesh['section'=2,'gx'=4,'gy'=4] {'section','gx','gy'}, dimensions={0} | all-to-all | bytes 262144 | tf_op jit(solution)/shard_map/all_to_all | solution.py:829
  66.7 1.5 %mix.4 = (bf16[32,512]{1,0:T(8,128)(2,1)}, bf16[512,128]{1,0:T(8,128)(2,1)S(1)}) custom-call(s32[1]{0:T(128)} %bitcast.refs_0_, bf16[512,128]{1,0:T(8,128)(2,1)S(1)} %bitcast.36, bf16[1024,512]{1,0:T(8,128)(2,1)S(1)} %get-tuple-element.48.refs_2_, bf16[4,4,256,128]{3,2,1,0:T(8,128)(2,1)S(1)} %get-tuple-element.49.refs_3_), custom_call_target="tpu_custom_call" | custom-call | bytes 3000000 | tf_op jit(solution)/shard_map/mix/pallas_call | solution.py:69
  68.2 9.9 %all_to_all.84 = bf16[32,16,128]{2,1,0:T(8,128)(2,1)S(1)} all-to-all(bf16[32,16,128]{2,1,0:T(8,128)(2,1)S(1)} %bitcast.38), channel_id=1, replica_groups=mesh['section'=2,'gx'=4,'gy'=4] {'section','gx','gy'}, dimensions={0} | all-to-all | bytes 262144 | tf_op jit(solution)/shard_map/all_to_all | solution.py:829
  78.1 4.6 %turn.1 = (bf16[128,4096]{1,0:T(8,128)(2,1)S(1)}, f32[16,128]{1,0:T(8,128)S(1)}, bf16[512,128]{1,0:T(8,128)(2,1)S(1)}) custom-call(s32[1]{0:T(128)} %bitcast.refs_0_, bf16[48,32]{1,0:T(8,128)(2,1)S(1)} %pad_maximum_fusion.refs_1_, bf16[48,32]{1,0:T(8,128)(2,1)S(1)} %copy-done.3, bf16[512,128]{1,0:T(8,128)(2,1)S(1)} %bitcast.35, ...), custom_call_target="tpu_custom_call" | custom-call | bytes 3000000 | tf_op jit(solution)/shard_map/turn/pallas_call | solution.py:69
  82.8 9.9 %all_to_all.85 = bf16[32,16,128]{2,1,0:T(8,128)(2,1)S(1)} all-to-all(bf16[32,16,128]{2,1,0:T(8,128)(2,1)S(1)} %bitcast.42), channel_id=1, replica_groups=mesh['section'=2,'gx'=4,'gy'=4] {'section','gx','gy'}, dimensions={0} | all-to-all | bytes 262144 | tf_op jit(solution)/shard_map/all_to_all | solution.py:829
  92.7 1.7 %mix.5 = (bf16[32,512]{1,0:T(8,128)(2,1)}, bf16[512,128]{1,0:T(8,128)(2,1)S(1)}) custom-call(s32[1]{0:T(128)} %bitcast.refs_0_, bf16[512,128]{1,0:T(8,128)(2,1)S(1)} %bitcast.37, bf16[1024,512]{1,0:T(8,128)(2,1)S(1)} %get-tuple-element.48.refs_2_, bf16[4,4,256,128]{3,2,1,0:T(8,128)(2,1)S(1)} %get-tuple-element.49.refs_3_), custom_call_target="tpu_custom_call" | custom-call | bytes 3000000 | tf_op jit(solution)/shard_map/mix/pallas_call | solution.py:69
  94.4 9.9 %all_to_all.86 = bf16[32,16,128]{2,1,0:T(8,128)(2,1)S(1)} all-to-all(bf16[32,16,128]{2,1,0:T(8,128)(2,1)S(1)} %bitcast.43), channel_id=1, replica_groups=mesh['section'=2,'gx'=4,'gy'=4] {'section','gx','gy'}, dimensions={0} | all-to-all | bytes 262144 | tf_op jit(solution)/shard_map/all_to_all | solution.py:829
  104.3 3.1 %back.1 = (f32[32,16,128]{2,1,0:T(8,128)S(1)}, bf16[512,128]{1,0:T(8,128)(2,1)S(1)}) custom-call(s32[1]{0:T(128)} %bitcast.refs_0_, bf16[48,32]{1,0:T(8,128)(2,1)S(1)} %pad_maximum_fusion.refs_1_, bf16[48,32]{1,0:T(8,128)(2,1)S(1)} %copy-done.3, bf16[512,128]{1,0:T(8,128)(2,1)S(1)} %bitcast.33, bf16[128,4096]{1,0:T(8,128)(2,1)S(1)} %get-tuple-element.56.refs_4_, ...), custom_call_target="tpu_custom_call" | custom-call | bytes 3000000 | tf_op jit(solution)/shard_map/back/pallas_call | solution.py:69
  107.5 9.9 %all_to_all.87 = bf16[32,16,128]{2,1,0:T(8,128)(2,1)S(1)} all-to-all(bf16[32,16,128]{2,1,0:T(8,128)(2,1)S(1)} %bitcast.40), channel_id=1, replica_groups=mesh['section'=2,'gx'=4,'gy'=4] {'section','gx','gy'}, dimensions={0} | all-to-all | bytes 262144 | tf_op jit(solution)/shard_map/all_to_all | solution.py:829
  117.4 2.6 %all-to-all-start.7 = ((f32[32,16,128]{2,1,0:T(8,128)}), f32[32,16,128]{2,1,0:T(8,128)S(1)}, u32[]{:S(2)}, u32[]{:S(2)}) async-start(f32[32,16,128]{2,1,0:T(8,128)} %copy-done.1), calls=%async_computation.7 | async-start | bytes 524288 | tf_op jit(solution)/shard_map/all_to_all | solution.py:878
  120.0 1.0 spec.1
  121.2 1.1 collective-permute-done.5.refs_1_
  122.3 8.3 %outer.1.refs_1_ = f32[1,8,4,32,32,32]{5,4,3,2,1,0:T(8,128)} custom-call(bf16[2,32,512]{2,1,0:T(8,128)(2,1)S(1)} %get-tuple-element.64.refs_0_, bf16[2,32,512]{2,1,0:T(8,128)(2,1)S(1)} %collective-permute-done.5.refs_1_), custom_call_target="tpu_custom_call" | custom-call | bytes 20000000 | tf_op jit(solution)/shard_map/outer/pallas_call | solution.py:812
  131.2 0.7 finish.1
  (28 shorter events, 2.1 us)
Async XLA Ops:
  0.6 1.6 %copy-start = (bf16[1,32,16,16,128]{4,3,2,1,0:T(8,128)(2,1)S(1)}, bf16[1,32,16,16,128]{4,3,2,1,0:T(8,128)(2,1)}, u32[]{:S(2)}) copy-start(bf16[1,32,16,16,128]{4,3,2,1,0:T(8,128)(2,1)} %param.7) | copy-start | bytes 6291460
  3.3 3.0 %collective-permute-start.1 = (bf16[256,2048]{1,0:T(8,128)(2,1)}, bf16[256,2048]{1,0:T(8,128)(2,1)S(1)}, u32[]{:S(2)}, u32[]{:S(2)}) collective-permute-start(bf16[256,2048]{1,0:T(8,128)(2,1)} %dynamic-slice_bitcast_fusion.1), channel_id=1, source_target_pairs={{0,16},{16,0},{1,17},{17,1},{2,18},{18,2},{3,19},{19,3},{4,20},{20... | collective-permute-start | bytes 3145736 | tf_op jit(solution)/shard_map/ppermute | solution.py:833
  12.1 13.1 %copy-start.7 = (bf16[1,32]{1,0:T(2,128)(2,1)S(1)}, bf16[1,32]{1,0:T(2,128)(2,1)}, u32[]{:S(2)}) copy-start(bf16[1,32]{1,0:T(2,128)(2,1)} %param.10) | copy-start | bytes 196
  12.1 13.1 %copy-start.6 = (bf16[1,32,32]{2,1,0:T(8,128)(2,1)S(1)}, bf16[1,32,32]{2,1,0:T(8,128)(2,1)}, u32[]{:S(2)}) copy-start(bf16[1,32,32]{2,1,0:T(8,128)(2,1)} %param.9) | copy-start | bytes 6148
  12.1 22.9 %collective-permute-start.2 = (bf16[4,4,256,128]{3,2,1,0:T(8,128)(2,1)}, bf16[4,4,256,128]{3,2,1,0:T(8,128)(2,1)}, u32[]{:S(2)}, u32[]{:S(2)}) collective-permute-start(bf16[4,4,256,128]{3,2,1,0:T(8,128)(2,1)} %pack.3), channel_id=1, source_target_pairs={{0,16},{16,0},{1,17},{17,1},{2,18},{18,2},{3,19},{19,3},{4,20},{20... | collective-permute-start | bytes 3145736 | tf_op jit(solution)/shard_map/ppermute | solution.py:833
  12.5 22.4 %collective-permute-start.3 = (bf16[128,2048]{1,0:T(8,128)(2,1)}, bf16[128,2048]{1,0:T(8,128)(2,1)S(1)}, u32[]{:S(2)}, u32[]{:S(2)}) collective-permute-start(bf16[128,2048]{1,0:T(8,128)(2,1)} %get-tuple-element.44), channel_id=1, source_target_pairs={{0,4},{4,0},{8,12},{12,8},{1,5},{5,1},{9,13},{13,9},{2,6},{6,2},{1... | collective-permute-start | bytes 1572872 | tf_op jit(solution)/shard_map/ppermute | solution.py:837
  15.3 19.7 %all-to-all-start = ((bf16[32,16,256]{2,1,0:T(8,128)(2,1)}), bf16[32,16,256]{2,1,0:T(8,128)(2,1)S(1)}, u32[]{:S(2)}, u32[]{:S(2)}) async-start(bf16[32,16,256]{2,1,0:T(8,128)(2,1)} %bitcast.11), calls=%async_computation | async-start | bytes 524288 | tf_op jit(solution)/shard_map/all_to_all | solution.py:829
  23.3 44.8 %collective-permute-start.4 = (bf16[128,2048]{1,0:T(8,128)(2,1)}, bf16[128,2048]{1,0:T(8,128)(2,1)}, u32[]{:S(2)}, u32[]{:S(2)}) collective-permute-start(bf16[128,2048]{1,0:T(8,128)(2,1)} %get-tuple-element.51), channel_id=1, source_target_pairs={{0,4},{4,0},{8,12},{12,8},{1,5},{5,1},{9,13},{13,9},{2,6},{6,2},{1... | collective-permute-start | bytes 1572872 | tf_op jit(solution)/shard_map/ppermute | solution.py:837
  25.2 3.9 %collective-permute-start = (bf16[48,32]{1,0:T(8,128)(2,1)S(1)}, bf16[48,32]{1,0:T(8,128)(2,1)S(1)}, u32[]{:S(2)}, u32[]{:S(2)}) collective-permute-start(bf16[48,32]{1,0:T(8,128)(2,1)S(1)} %pad_maximum_fusion.refs_1_), channel_id=1, source_target_pairs={{0,16},{16,0},{1,17},{17,1},{2,18},{18,2},{3,19},{19,3},{4,20},{20... | collective-permute-start | bytes 9224 | tf_op jit(solution)/shard_map/ppermute | solution.py:833
  29.1 6.7 %copy-start.2 = (bf16[48,32]{1,0:T(8,128)(2,1)}, bf16[48,32]{1,0:T(8,128)(2,1)S(1)}, u32[]{:S(2)}) copy-start(bf16[48,32]{1,0:T(8,128)(2,1)S(1)} %collective-permute-done.refs_5_.refs_2_) | copy-start | bytes 9220
  35.0 0.8 copy-start.5
  38.9 0.6 copy-start.4
  39.6 11.7 %all-to-all-start.1 = ((bf16[32,16,128]{2,1,0:T(8,128)(2,1)}), bf16[32,16,128]{2,1,0:T(8,128)(2,1)S(1)}, u32[]{:S(2)}, u32[]{:S(2)}) async-start(bf16[32,16,128]{2,1,0:T(8,128)(2,1)} %bitcast.39), calls=%async_computation.1 | async-start | bytes 262144 | tf_op jit(solution)/shard_map/all_to_all | solution.py:829
  43.3 7.9 %copy-start.3 = (bf16[48,32]{1,0:T(8,128)(2,1)S(1)}, bf16[48,32]{1,0:T(8,128)(2,1)}, u32[]{:S(2)}) copy-start(bf16[48,32]{1,0:T(8,128)(2,1)} %copy-done.2) | copy-start | bytes 9220
  107.5 9.9 %copy-start.1 = (f32[32,16,128]{2,1,0:T(8,128)}, f32[32,16,128]{2,1,0:T(8,128)S(1)}, u32[]{:S(2)}) copy-start(f32[32,16,128]{2,1,0:T(8,128)S(1)} %get-tuple-element.66) | copy-start | bytes 786436
  117.4 13.8 %all-to-all-start.7 = ((f32[32,16,128]{2,1,0:T(8,128)}), f32[32,16,128]{2,1,0:T(8,128)S(1)}, u32[]{:S(2)}, u32[]{:S(2)}) async-start(f32[32,16,128]{2,1,0:T(8,128)} %copy-done.1), calls=%async_computation.7 | async-start | bytes 524288 | tf_op jit(solution)/shard_map/all_to_all | solution.py:878
  121.0 1.3 %collective-permute-start.5 = (bf16[2,32,512]{2,1,0:T(8,128)(2,1)S(1)}, bf16[2,32,512]{2,1,0:T(8,128)(2,1)S(1)}, u32[]{:S(2)}, u32[]{:S(2)}) collective-permute-start(bf16[2,32,512]{2,1,0:T(8,128)(2,1)S(1)} %get-tuple-element.65), channel_id=1, source_target_pairs={{0,16},{16,0},{1,17},{17,1},{2,18},{18,2},{3,19},{19,3},{4,20},{20... | collective-permute-start | bytes 196616 | tf_op jit(solution)/shard_map/ppermute | solution.py:833

commit v4 on v3

--- a/solution.py
+++ b/solution.py
@@ -162,12 +162,11 @@
 
 
 def activate(pre):
-    inner = gelu_coef * (pre + 0.044715 * pre * pre * pre)
-    tanh_val = jnp.tanh(inner)
-    value = 0.5 * pre * (1.0 + tanh_val)
-    slope = 0.5 * (1.0 + tanh_val) + 0.5 * pre * (1.0 - tanh_val * tanh_val) * gelu_coef * (
-        1.0 + 3.0 * 0.044715 * pre * pre
-    )
+    square = pre * pre
+    tanh_val = jnp.tanh(pre * (gelu_coef + (gelu_coef * 0.044715) * square))
+    half = 0.5 + 0.5 * tanh_val
+    value = pre * half
+    slope = half + value * (1.0 - tanh_val) * (gelu_coef + (3.0 * gelu_coef * 0.044715) * square)
     return value, slope
 
 
@@ -716,6 +715,14 @@
     )
 
 
+def pieces(sz, value):
+    part = sz.chans // 4
+    high = value.astype(bf16).astype(f32)
+    low = value - high
+    bias = jnp.where(iota((8, 128), 0) < 4, high[part:], low[part:])
+    return jnp.concatenate([high[:part], low[:part], bias], axis=0).astype(bf16)
+
+
 def back_kernel(
     sz, s_ref, own_ref, other_ref, u, d, slope, bb, sums, mine_hbm, next_hbm, parts, out, new, field, sems
 ):
@@ -732,17 +739,18 @@
     send_analysis(sz, bb, new[...], out, 0)
     first = point_sums(sz, field[...], new[...])
     half = sz.places // 2
-    for place in range(half):
-        parts[place] = first
-        parts[half + place] = sums[...]
+    for layer, value in enumerate((first, sums[...])):
+        block = pieces(sz, value)
+        for place in range(half):
+            parts[layer * half + place] = block
 
 
 def back_call(sz, s, mine, other, d, slope, u, bb, sums, own_small, other_small):
-    parts, line, field = (sz.places, sz.chans // 4 + 8, 128), (sz.modes, sz.thin), (sz.thin, sz.wide)
+    parts, line, field = (sz.places, sz.chans // 2 + 8, 128), (sz.modes, sz.thin), (sz.thin, sz.wide)
     return run(
         "back",
         lambda *refs: back_kernel(sz, *refs),
-        [(kept(parts, f32), False), (kept(line), False)],
+        [(kept(parts), False), (kept(line), False)],
         [smem] + [vmem] * 7 + [hbm, hbm],
         (s, own_small, other_small, u, near(d), near(slope), near(bb), near(sums), mine, other),
         [pltpu.VMEM(field, bf16), pltpu.VMEM(field, bf16)],
@@ -751,11 +759,12 @@
 
 
 def finish_kernel(sz, parts_ref, after_ref, point_ref, bias_ref):
-    total = jnp.sum(parts_ref[...], axis=0)
+    total = jnp.sum(parts_ref[...].astype(f32), axis=0)
     part = sz.chans // 4
+    bias_ref[...] = (total[2 * part : 2 * part + 1] + total[2 * part + 4 : 2 * part + 5])[:, : sz.chans]
+    total = total[:part] + total[part : 2 * part]
     for t in range(4):
         point_ref[0, t * part : (t + 1) * part, :] = total[:part, t * sz.chans : (t + 1) * sz.chans]
-    bias_ref[...] = total[part : part + 1, : sz.chans]
 
 
 def finish_call(sz, parts, after):
@@ -797,24 +806,27 @@
 
     dims = (groups * kk_count, groups * kk_count * 128)
     spread_lanes = (iota(dims, 0) == iota(dims, 1) // 128).astype(bf16)
-    columns = nn(left_ref[step], spread_lanes)
-    for kk in range(kk_count):
-        for ll in range(sz.modes_y):
-            row = right_ref[step, kk, ll : ll + 1, :]
-            for h in range(groups):
-                at = (h * kk_count + kk) * 128
-                part = columns[ll * sz.cpl : (ll + 1) * sz.cpl, at : at + sz.chans] * row
-                out_ref[0, 0, kk, ll, h * sz.cpl : (h + 1) * sz.cpl, :] = part
+    each = out_ref.shape[1]
+    for sub in range(each):
+        columns = nn(left_ref[step * each + sub], spread_lanes)
+        for kk in range(kk_count):
+            for ll in range(sz.modes_y):
+                row = right_ref[step * each + sub, kk, ll : ll + 1, :]
+                for h in range(groups):
+                    at = (h * kk_count + kk) * 128
+                    part = columns[ll * sz.cpl : (ll + 1) * sz.cpl, at : at + sz.chans] * row
+                    out_ref[0, sub, kk, ll, h * sz.cpl : (h + 1) * sz.cpl, :] = part
 
 
 def outer_call(sz, mine, theirs):
+    each = max(1, sz.half_j // 2)
     wide = sz.modes_y * sz.cpl
     return pl.pallas_call(
         lambda *refs: outer_kernel(sz, *refs),
-        grid=(sz.blk_j,),
+        grid=(sz.blk_j // each,),
         out_shape=pltpu.HBM((1, sz.blk_j, sz.blk_k, sz.modes_y, sz.chans, sz.chans), f32),
         in_specs=[vmem] * 2,
-        out_specs=pl.BlockSpec((1, 1, sz.blk_k, sz.modes_y, sz.chans, sz.chans), lambda i: (0, i, 0, 0, 0, 0)),
+        out_specs=pl.BlockSpec((1, each, sz.blk_k, sz.modes_y, sz.chans, sz.chans), lambda i: (0, i, 0, 0, 0, 0)),
         scratch_shapes=[
             pltpu.VMEM((sz.blk_j, wide, sz.groups * sz.blk_k), bf16),
             pltpu.VMEM((sz.blk_j, sz.blk_k, sz.modes_y, sz.chans), f32),
@@ -864,8 +876,8 @@
     mine_g, send_g = split_call(sz, gx, raw_g, mine_v)
     next_g = swap_near(sz, send_g)
     low, ya = pack_call(sz, mine_v, spectral_weight, 0, by)
-    sv0, out, ya = mix_call(sz, 0, False, s, r, ya, (low, high), (other_small, mine_g, next_v))
-    bb = wide_call(sz, gx, bx, bz, sv0)
+    bb = wide_call(sz, gx, bx, bz, mine_v)
+    sv0, out, ya = mix_call(sz, 0, False, s, r, ya, (low, high), (other_small, bb, next_v))
     v1, slope0, bb, out, w1 = forward_call(sz, s, mine_v, next_v, exchange(out), bb, own_small, other_small, low, high)
     sv1, out = mix_call(sz, 1, False, s, exchange(out), ya, w1)
     out = gate_call(sz, out, next_g)

time: 133 us -> 130 us (0.977)
  blocking collectives: 50.1 us -> 61.1 us
  waiting for transfers between devices: 10.8 us -> 2.54 us
  starting transfers between devices: 16.9 us -> 13.1 us
  Pallas kernels: 48.9 us -> 47.3 us
    all_to_all x5 -> x6, blocking collectives: 50.1 us -> 61.1 us  [exchange(): return lax.all_to_all(block, AXES, split_axis=0, concat_axis=0, tiled=True)]
    all_to_all x2 -> x1, waiting for transfers between devices: 8.99 us -> 1.06 us  [exchange(): return lax.all_to_all(block, AXES, split_axis=0, concat_axis=0, tiled=True)]
    all_to_all x2 -> x1, starting transfers between devices: 8.56 us -> 4.82 us  [exchange(): return lax.all_to_all(block, AXES, split_axis=0, concat_axis=0, tiled=True)]
  transfers between devices with their start and end apart: 9 -> 8, of which waited for: 5 -> 4; matrix products, arithmetic and copies ran while one was open for 0% -> 0% of each run, Pallas kernels for 25% -> 24%
where the time goes in v4:
time: 130 us; the launch traced here: 129 us
  blocking collectives  61.1 us (47%)
  Pallas kernels  47.3 us (36%)
  starting transfers between devices  13.1 us (10%)
  local copies, waits for them, and re-layouts  4.28 us (3%)
  waiting for transfers between devices  2.54 us (2%)
    all_to_all x6, blocking collectives, exchange(): return lax.all_to_all(block, AXES, split_axis=0, concat_axis=0, tiled=True)  61.1 us
    pallas_call x14, Pallas kernels, run(): pl.pallas_call(kernel, out_shape=tuple((pltpu.HBM(o.shape, o.dtype) if aw...  39.3 us
    pallas_call x1, Pallas kernels, outer_call(): pl.pallas_call(lambda *refs: outer_kernel(sz, *refs), grid=(sz.blk_j // e...  7.24 us
    all_to_all x1, starting transfers between devices, exchange(): return lax.all_to_all(block, AXES, split_axis=0, concat_axis=0, tiled=True)  4.82 us
    ppermute x2, starting transfers between devices, swap_near(): return lax.ppermute(block, 'gx', [(i, i ^ 1) for i in range(sz.n_gx)])  4.58 us
    unnamed x16, local copies, waits for them, and re-layouts  3.13 us
  transfers between devices with their start and end apart: 8, of which 4 were waited for; matrix products, arithmetic and copies ran while one was open for 0% of the time, Pallas kernels for 24%

profile of v4, /device:TPU:0, one launch (start us, length us, event | category | flops | bytes accessed | tf_op | source)
XLA Modules:
  0.0 129.2 jit_solution(13021193812945047915)
XLA Ops:
  0.7 1.6 %copy-done = bf16[1,32,16,16,128]{4,3,2,1,0:T(8,128)(2,1)S(1)} copy-done((bf16[1,32,16,16,128]{4,3,2,1,0:T(8,128)(2,1)S(1)}, bf16[1,32,16,16,128]{4,3,2,1,0:T(8,128)(2,1)}, u32[]{:S(2)}) %copy-start) | copy-done | bytes 2097176
  2.2 1.1 dynamic-slice_bitcast_fusion.1
  3.3 0.5 collective-permute-start.1
  3.8 2.2 %tables.1.refs_4_ = bf16[512,2048]{1,0:T(8,128)(2,1)S(1)} custom-call(s32[2]{0:T(128)S(1)} %pad_add_fusion.refs_0_.refs_1_, bf16[4,512,16]{2,1,0:T(8,128)(2,1)} %constant.37.clone.refs_1_, bf16[512,128]{1,0:T(8,128)(2,1)} %constant.38.clone.refs_2_), custom_call_target="tpu_custom_call" | custom-call | bytes 3000000 | tf_op jit(solution)/shard_map/tables/pallas_call | solution.py:69
  6.2 2.6 %first.1 = (bf16[128,2048]{1,0:T(8,128)(2,1)}, bf16[128,2048]{1,0:T(8,128)(2,1)}, bf16[256,2048]{1,0:T(8,128)(2,1)}, bf16[512,256]{1,0:T(8,128)(2,1)}) custom-call(s32[1]{0:T(128)} %bitcast.refs_0_, s32[2]{0:T(128)S(1)} %pad_add_fusion.refs_0_.refs_1_, bf16[256,2048]{1,0:T(8,128)(2,1)S(1)} %dynamic-slice_bitcast_fusion.refs_2_, ...), custom_call_target="tpu_custom_call" | custom-call | bytes 3000000 | tf_op jit(solution)/shard_map/first/pallas_call | solution.py:69
  8.8 3.2 %pack.3 = bf16[4,4,256,128]{3,2,1,0:T(8,128)(2,1)} custom-call(bf16[128,2048]{1,0:T(8,128)(2,1)} %get-tuple-element.39.refs_0_.refs_3_.refs_4_.refs_2_.refs_8_, bf16[1,8,4,32,32,32]{5,4,3,2,1,0:T(8,128)(2,1)} %refs_1_.5), custom_call_target="tpu_custom_call" | custom-call | tf_op jit(solution)/shard_map/pack/pallas_call | solution.py:69
  12.5 2.7 %collective-permute-start.3 = (bf16[128,2048]{1,0:T(8,128)(2,1)}, bf16[128,2048]{1,0:T(8,128)(2,1)S(1)}, u32[]{:S(2)}, u32[]{:S(2)}) collective-permute-start(bf16[128,2048]{1,0:T(8,128)(2,1)} %get-tuple-element.42), channel_id=1, source_target_pairs={{0,4},{4,0},{8,12},{12,8},{1,5},{5,1},{9,13},{13,9},{2,6},{6,2},{1... | collective-permute-start | bytes 1572872 | tf_op jit(solution)/shard_map/ppermute | solution.py:849
  15.3 4.8 %all-to-all-start = ((bf16[32,16,256]{2,1,0:T(8,128)(2,1)}), bf16[32,16,256]{2,1,0:T(8,128)(2,1)S(1)}, u32[]{:S(2)}, u32[]{:S(2)}) async-start(bf16[32,16,256]{2,1,0:T(8,128)(2,1)} %bitcast.11), calls=%async_computation | async-start | bytes 524288 | tf_op jit(solution)/shard_map/all_to_all | solution.py:841
  20.1 3.3 %split.1 = (bf16[128,2048]{1,0:T(8,128)(2,1)}, bf16[128,2048]{1,0:T(8,128)(2,1)}) custom-call(s32[2]{0:T(128)S(1)} %pad_add_fusion.refs_0_.refs_1_, bf16[256,2048]{1,0:T(8,128)(2,1)} %get-tuple-element.48.refs_1_, bf16[128,2048]{1,0:T(8,128)(2,1)} %get-tuple-element.39.refs_0_.refs_3_.refs_4_.refs_2_.refs_8_), custom_call_target="tpu_custom_call" | custom-call | tf_op jit(solution)/shard_map/split/pallas_call | solution.py:69
  23.4 1.8 %collective-permute-start.4 = (bf16[128,2048]{1,0:T(8,128)(2,1)}, bf16[128,2048]{1,0:T(8,128)(2,1)}, u32[]{:S(2)}, u32[]{:S(2)}) collective-permute-start(bf16[128,2048]{1,0:T(8,128)(2,1)} %get-tuple-element.49), channel_id=1, source_target_pairs={{0,4},{4,0},{8,12},{12,8},{1,5},{5,1},{9,13},{13,9},{2,6},{6,2},{1... | collective-permute-start | bytes 1572872 | tf_op jit(solution)/shard_map/ppermute | solution.py:849
  25.3 4.7 %wide.1.refs_6_ = bf16[512,4096]{1,0:T(8,128)(2,1)} custom-call(s32[2]{0:T(128)S(1)} %pad_add_fusion.refs_0_.refs_1_, bf16[4,512,16]{2,1,0:T(8,128)(2,1)} %constant.37.clone.refs_1_, bf16[512,128]{1,0:T(8,128)(2,1)} %constant.38.clone.refs_2_, bf16[128,2048]{1,0:T(8,128)(2,1)} %get-tuple-element.39.refs_0_.refs_3_.refs_4_.refs_2_.refs_8_), custom_call_target="tpu_custom_call" | custom-call | tf_op jit(solution)/shard_map/wide/pallas_call | solution.py:69
  30.1 3.8 %pack.2 = (bf16[4,4,256,128]{3,2,1,0:T(8,128)(2,1)}, bf16[1024,512]{1,0:T(8,128)(2,1)}) custom-call(bf16[128,2048]{1,0:T(8,128)(2,1)} %get-tuple-element.39.refs_0_.refs_3_.refs_4_.refs_2_.refs_8_, bf16[1,8,4,32,32,32]{5,4,3,2,1,0:T(8,128)(2,1)} %refs_1_.5, bf16[128,512]{1,0:T(8,128)(2,1)} %constant.39.clone.refs_2_), custom_call_target="tpu_custom_call" | custom-call | tf_op jit(solution)/shard_map/pack/pallas_call | solution.py:69
  33.9 1.1 all-to-all-done
  34.9 0.8 copy-done.5
  35.8 3.1 %mix.3 = (bf16[32,512]{1,0:T(8,128)(2,1)}, bf16[512,128]{1,0:T(8,128)(2,1)S(1)}, bf16[1024,512]{1,0:T(8,128)(2,1)S(1)}) custom-call(s32[1]{0:T(128)} %bitcast.refs_0_, bf16[512,256]{1,0:T(8,128)(2,1)S(1)} %bitcast.31, bf16[1024,512]{1,0:T(8,128)(2,1)} %get-tuple-element.40.refs_2_, bf16[4,4,256,128]{3,2,1,0:T(8,128)(2,1)} %get-tuple-element.41.refs_3_.refs_7_, ...), custom_call_target="tpu_custom_call" | custom-call | bytes 3000000 | tf_op jit(solution)/shard_map/mix/pallas_call | solution.py:69
  38.9 11.5 %all_to_all.83 = bf16[32,16,128]{2,1,0:T(8,128)(2,1)S(1)} all-to-all(bf16[32,16,128]{2,1,0:T(8,128)(2,1)S(1)} %bitcast.42), channel_id=1, replica_groups=mesh['section'=2,'gx'=4,'gy'=4] {'section','gx','gy'}, dimensions={0} | all-to-all | bytes 262144 | tf_op jit(solution)/shard_map/all_to_all | solution.py:841
  50.4 0.7 copy-done.2
  51.1 4.7 %forward.1 = (bf16[128,4096]{1,0:T(8,128)(2,1)S(1)}, f32[128,4096]{1,0:T(8,128)S(1)}, bf16[512,4096]{1,0:T(8,128)(2,1)S(1)}, bf16[512,128]{1,0:T(8,128)(2,1)S(1)}, bf16[4,4,256,128]{3,2,1,0:T(8,128)(2,1)S(1)}) custom-call(s32[1]{0:T(128)} %bitcast.refs_0_, bf16[48,32]{1,0:T(8,128)(2,1)S(1)} %pad_maximum_fusion.refs_1_, bf16[48,32]{1,0:T(8,128)(2,1)S(1)} %copy-done.2, ...), custom_call_target="tpu_custom_call" | custom-call | bytes 3000000 | tf_op jit(solution)/shard_map/forward/pallas_call | solution.py:69
  55.8 9.9 %all_to_all.84 = bf16[32,16,128]{2,1,0:T(8,128)(2,1)S(1)} all-to-all(bf16[32,16,128]{2,1,0:T(8,128)(2,1)S(1)} %bitcast.40), channel_id=1, replica_groups=mesh['section'=2,'gx'=4,'gy'=4] {'section','gx','gy'}, dimensions={0} | all-to-all | bytes 262144 | tf_op jit(solution)/shard_map/all_to_all | solution.py:841
  65.7 1.5 %mix.4 = (bf16[32,512]{1,0:T(8,128)(2,1)}, bf16[512,128]{1,0:T(8,128)(2,1)S(1)}) custom-call(s32[1]{0:T(128)} %bitcast.refs_0_, bf16[512,128]{1,0:T(8,128)(2,1)S(1)} %bitcast.37, bf16[1024,512]{1,0:T(8,128)(2,1)S(1)} %get-tuple-element.45.refs_2_, bf16[4,4,256,128]{3,2,1,0:T(8,128)(2,1)S(1)} %get-tuple-element.46.refs_3_), custom_call_target="tpu_custom_call" | custom-call | bytes 3000000 | tf_op jit(solution)/shard_map/mix/pallas_call | solution.py:69
  67.2 9.9 %all_to_all.85 = bf16[32,16,128]{2,1,0:T(8,128)(2,1)S(1)} all-to-all(bf16[32,16,128]{2,1,0:T(8,128)(2,1)S(1)} %bitcast.38), channel_id=1, replica_groups=mesh['section'=2,'gx'=4,'gy'=4] {'section','gx','gy'}, dimensions={0} | all-to-all | bytes 262144 | tf_op jit(solution)/shard_map/all_to_all | solution.py:841
  77.2 4.3 %turn.1 = (bf16[128,4096]{1,0:T(8,128)(2,1)S(1)}, f32[16,128]{1,0:T(8,128)S(1)}, bf16[512,128]{1,0:T(8,128)(2,1)S(1)}) custom-call(s32[1]{0:T(128)} %bitcast.refs_0_, bf16[48,32]{1,0:T(8,128)(2,1)S(1)} %pad_maximum_fusion.refs_1_, bf16[48,32]{1,0:T(8,128)(2,1)S(1)} %copy-done.3, bf16[512,128]{1,0:T(8,128)(2,1)S(1)} %bitcast.35, ...), custom_call_target="tpu_custom_call" | custom-call | bytes 3000000 | tf_op jit(solution)/shard_map/turn/pallas_call | solution.py:69
  81.5 9.9 %all_to_all.86 = bf16[32,16,128]{2,1,0:T(8,128)(2,1)S(1)} all-to-all(bf16[32,16,128]{2,1,0:T(8,128)(2,1)S(1)} %bitcast.41), channel_id=1, replica_groups=mesh['section'=2,'gx'=4,'gy'=4] {'section','gx','gy'}, dimensions={0} | all-to-all | bytes 262144 | tf_op jit(solution)/shard_map/all_to_all | solution.py:841
  91.4 1.7 %mix.5 = (bf16[32,512]{1,0:T(8,128)(2,1)}, bf16[512,128]{1,0:T(8,128)(2,1)S(1)}) custom-call(s32[1]{0:T(128)} %bitcast.refs_0_, bf16[512,128]{1,0:T(8,128)(2,1)S(1)} %bitcast.36, bf16[1024,512]{1,0:T(8,128)(2,1)S(1)} %get-tuple-element.45.refs_2_, bf16[4,4,256,128]{3,2,1,0:T(8,128)(2,1)S(1)} %get-tuple-element.46.refs_3_), custom_call_target="tpu_custom_call" | custom-call | bytes 3000000 | tf_op jit(solution)/shard_map/mix/pallas_call | solution.py:69
  93.1 9.9 %all_to_all.87 = bf16[32,16,128]{2,1,0:T(8,128)(2,1)S(1)} all-to-all(bf16[32,16,128]{2,1,0:T(8,128)(2,1)S(1)} %bitcast.43), channel_id=1, replica_groups=mesh['section'=2,'gx'=4,'gy'=4] {'section','gx','gy'}, dimensions={0} | all-to-all | bytes 262144 | tf_op jit(solution)/shard_map/all_to_all | solution.py:841
  103.0 3.1 %back.1 = (bf16[32,24,128]{2,1,0:T(8,128)(2,1)S(1)}, bf16[512,128]{1,0:T(8,128)(2,1)S(1)}) custom-call(s32[1]{0:T(128)} %bitcast.refs_0_, bf16[48,32]{1,0:T(8,128)(2,1)S(1)} %pad_maximum_fusion.refs_1_, bf16[48,32]{1,0:T(8,128)(2,1)S(1)} %copy-done.3, bf16[512,128]{1,0:T(8,128)(2,1)S(1)} %bitcast.32, bf16[128,4096]{1,0:T(8,128)(2,1)S(1)} %get-tuple-element.55.refs_4_, ...), custom_call_target="tpu_custom_call" | custom-call | bytes 3000000 | tf_op jit(solution)/shard_map/back/pallas_call | solution.py:69
  106.2 9.9 %all_to_all.88 = bf16[32,16,128]{2,1,0:T(8,128)(2,1)S(1)} all-to-all(bf16[32,16,128]{2,1,0:T(8,128)(2,1)S(1)} %bitcast.39), channel_id=1, replica_groups=mesh['section'=2,'gx'=4,'gy'=4] {'section','gx','gy'}, dimensions={0} | all-to-all | bytes 262144 | tf_op jit(solution)/shard_map/all_to_all | solution.py:841
  116.1 2.6 %all-to-all-start.7 = ((bf16[32,24,128]{2,1,0:T(8,128)(2,1)}), bf16[32,24,128]{2,1,0:T(8,128)(2,1)S(1)}, u32[]{:S(2)}, u32[]{:S(2)}) async-start(bf16[32,24,128]{2,1,0:T(8,128)(2,1)} %copy-done.4), calls=%async_computation.7 | async-start | bytes 393216 | tf_op jit(solution)/shard_map/all_to_all | solution.py:890
  118.7 1.0 spec.1
  119.9 1.1 collective-permute-done.5.refs_1_
  121.0 7.2 %outer.1.refs_1_ = f32[1,8,4,32,32,32]{5,4,3,2,1,0:T(8,128)} custom-call(bf16[2,32,512]{2,1,0:T(8,128)(2,1)S(1)} %get-tuple-element.64.refs_0_, bf16[2,32,512]{2,1,0:T(8,128)(2,1)S(1)} %collective-permute-done.5.refs_1_), custom_call_target="tpu_custom_call" | custom-call | bytes 20000000 | tf_op jit(solution)/shard_map/outer/pallas_call | solution.py:824
  128.5 0.7 finish.1
  (27 shorter events, 1.3 us)
Async XLA Ops:
  0.6 1.6 %copy-start = (bf16[1,32,16,16,128]{4,3,2,1,0:T(8,128)(2,1)S(1)}, bf16[1,32,16,16,128]{4,3,2,1,0:T(8,128)(2,1)}, u32[]{:S(2)}) copy-start(bf16[1,32,16,16,128]{4,3,2,1,0:T(8,128)(2,1)} %param.7) | copy-start | bytes 6291460
  3.3 3.0 %collective-permute-start.1 = (bf16[256,2048]{1,0:T(8,128)(2,1)}, bf16[256,2048]{1,0:T(8,128)(2,1)S(1)}, u32[]{:S(2)}, u32[]{:S(2)}) collective-permute-start(bf16[256,2048]{1,0:T(8,128)(2,1)} %dynamic-slice_bitcast_fusion.1), channel_id=1, source_target_pairs={{0,16},{16,0},{1,17},{17,1},{2,18},{18,2},{3,19},{19,3},{4,20},{20... | collective-permute-start | bytes 3145736 | tf_op jit(solution)/shard_map/ppermute | solution.py:845
  12.1 13.2 %copy-start.7 = (bf16[1,32]{1,0:T(2,128)(2,1)S(1)}, bf16[1,32]{1,0:T(2,128)(2,1)}, u32[]{:S(2)}) copy-start(bf16[1,32]{1,0:T(2,128)(2,1)} %param.10) | copy-start | bytes 196
  12.1 13.1 %copy-start.6 = (bf16[1,32,32]{2,1,0:T(8,128)(2,1)S(1)}, bf16[1,32,32]{2,1,0:T(8,128)(2,1)}, u32[]{:S(2)}) copy-start(bf16[1,32,32]{2,1,0:T(8,128)(2,1)} %param.9) | copy-start | bytes 6148
  12.1 22.9 %collective-permute-start.2 = (bf16[4,4,256,128]{3,2,1,0:T(8,128)(2,1)}, bf16[4,4,256,128]{3,2,1,0:T(8,128)(2,1)}, u32[]{:S(2)}, u32[]{:S(2)}) collective-permute-start(bf16[4,4,256,128]{3,2,1,0:T(8,128)(2,1)} %pack.3), channel_id=1, source_target_pairs={{0,16},{16,0},{1,17},{17,1},{2,18},{18,2},{3,19},{19,3},{4,20},{20... | collective-permute-start | bytes 3145736 | tf_op jit(solution)/shard_map/ppermute | solution.py:845
  12.5 22.4 %collective-permute-start.3 = (bf16[128,2048]{1,0:T(8,128)(2,1)}, bf16[128,2048]{1,0:T(8,128)(2,1)S(1)}, u32[]{:S(2)}, u32[]{:S(2)}) collective-permute-start(bf16[128,2048]{1,0:T(8,128)(2,1)} %get-tuple-element.42), channel_id=1, source_target_pairs={{0,4},{4,0},{8,12},{12,8},{1,5},{5,1},{9,13},{13,9},{2,6},{6,2},{1... | collective-permute-start | bytes 1572872 | tf_op jit(solution)/shard_map/ppermute | solution.py:849
  15.3 19.7 %all-to-all-start = ((bf16[32,16,256]{2,1,0:T(8,128)(2,1)}), bf16[32,16,256]{2,1,0:T(8,128)(2,1)S(1)}, u32[]{:S(2)}, u32[]{:S(2)}) async-start(bf16[32,16,256]{2,1,0:T(8,128)(2,1)} %bitcast.11), calls=%async_computation | async-start | bytes 524288 | tf_op jit(solution)/shard_map/all_to_all | solution.py:841
  23.4 43.9 %collective-permute-start.4 = (bf16[128,2048]{1,0:T(8,128)(2,1)}, bf16[128,2048]{1,0:T(8,128)(2,1)}, u32[]{:S(2)}, u32[]{:S(2)}) collective-permute-start(bf16[128,2048]{1,0:T(8,128)(2,1)} %get-tuple-element.49), channel_id=1, source_target_pairs={{0,4},{4,0},{8,12},{12,8},{1,5},{5,1},{9,13},{13,9},{2,6},{6,2},{1... | collective-permute-start | bytes 1572872 | tf_op jit(solution)/shard_map/ppermute | solution.py:849
  25.2 8.6 %collective-permute-start = (bf16[48,32]{1,0:T(8,128)(2,1)S(1)}, bf16[48,32]{1,0:T(8,128)(2,1)S(1)}, u32[]{:S(2)}, u32[]{:S(2)}) collective-permute-start(bf16[48,32]{1,0:T(8,128)(2,1)S(1)} %pad_maximum_fusion.refs_1_), channel_id=1, source_target_pairs={{0,16},{16,0},{1,17},{17,1},{2,18},{18,2},{3,19},{19,3},{4,20},{20... | collective-permute-start | bytes 9224 | tf_op jit(solution)/shard_map/ppermute | solution.py:845
  33.9 1.9 %copy-start.1 = (bf16[48,32]{1,0:T(8,128)(2,1)}, bf16[48,32]{1,0:T(8,128)(2,1)S(1)}, u32[]{:S(2)}) copy-start(bf16[48,32]{1,0:T(8,128)(2,1)S(1)} %collective-permute-done.refs_5_.refs_2_) | copy-start | bytes 9220
  34.9 0.8 copy-start.5
  50.4 0.7 copy-start.2
  55.8 21.4 %copy-start.3 = (bf16[48,32]{1,0:T(8,128)(2,1)S(1)}, bf16[48,32]{1,0:T(8,128)(2,1)}, u32[]{:S(2)}) copy-start(bf16[48,32]{1,0:T(8,128)(2,1)} %copy-done.1) | copy-start | bytes 9220
  106.2 9.9 %copy-start.4 = (bf16[32,24,128]{2,1,0:T(8,128)(2,1)}, bf16[32,24,128]{2,1,0:T(8,128)(2,1)S(1)}, u32[]{:S(2)}) copy-start(bf16[32,24,128]{2,1,0:T(8,128)(2,1)S(1)} %get-tuple-element.66) | copy-start | bytes 589828
  116.1 12.4 %all-to-all-start.7 = ((bf16[32,24,128]{2,1,0:T(8,128)(2,1)}), bf16[32,24,128]{2,1,0:T(8,128)(2,1)S(1)}, u32[]{:S(2)}, u32[]{:S(2)}) async-start(bf16[32,24,128]{2,1,0:T(8,128)(2,1)} %copy-done.4), calls=%async_computation.7 | async-start | bytes 393216 | tf_op jit(solution)/shard_map/all_to_all | solution.py:890
  119.7 1.3 %collective-permute-start.5 = (bf16[2,32,512]{2,1,0:T(8,128)(2,1)S(1)}, bf16[2,32,512]{2,1,0:T(8,128)(2,1)S(1)}, u32[]{:S(2)}, u32[]{:S(2)}) collective-permute-start(bf16[2,32,512]{2,1,0:T(8,128)(2,1)S(1)} %get-tuple-element.65), channel_id=1, source_target_pairs={{0,16},{16,0},{1,17},{17,1},{2,18},{18,2},{3,19},{19,3},{4,20},{20... | collective-permute-start | bytes 196616 | tf_op jit(solution)/shard_map/ppermute | solution.py:845

commit v5 on v4

--- a/solution.py
+++ b/solution.py
@@ -203,6 +203,19 @@
         bb[:, x * depth : (x + 1) * depth] = (across[:, x : x + 1] * along).astype(bf16)
 
 
+def pack_rows(sz, copies, gets, w, out, out_hbm):
+    for jj in range(sz.half_j):
+        gets[jj].wait()
+        for kk in range(sz.blk_k):
+            for h in range(sz.groups):
+                lanes = [
+                    w[jj, kk, lg * 8 : (lg + 1) * 8, h * sz.cpl : (h + 1) * sz.cpl, :].reshape(128, sz.chans)
+                    for lg in range(sz.lgs)
+                ]
+                out[jj, kk, h * 128 : (h + 1) * 128, :] = jnp.concatenate(lanes, axis=1)
+        copies.send(out.at[jj], out_hbm.at[jj])
+
+
 def tables_kernel(sz, gx_ref, bx_hbm, bz_hbm, bb, bx, bz, sems):
     copies = Copies(sems)
     get_bx = copies.start(bx_hbm.at[gx_ref[0]], bx)
@@ -268,28 +281,38 @@
     return bb
 
 
-def first_kernel(sz, s_ref, gx_ref, keep, recv, bb, mine_hbm, send_hbm, raw_hbm, out_hbm, v, out, sems):
+def first_kernel(
+    sz, s_ref, gx_ref, keep, recv, bb, w_hbm, mine_hbm, send_hbm, raw_hbm, out_hbm, high_hbm, v, out, w, high, sems
+):
     copies = Copies(sems)
     first = s_ref[0] == 0
-    (put_raw,) = copies.choose(first, [(recv, keep, raw_hbm)])
+    gets = [copies.start(w_hbm.at[0, sz.half_j + jj], w.at[jj]) for jj in range(sz.half_j)]
     v[...] = nn(reorder(sz), jnp.where(first, keep[...], recv[...])).astype(bf16)
     send_quarters(sz, gx_ref, v, mine_hbm, send_hbm, copies)
     send_analysis(sz, bb, v[...], out, 0)
     copies.send(out, out_hbm)
+    (put_raw,) = copies.choose(first, [(recv, keep, raw_hbm)])
+    pack_rows(sz, copies, gets, w, high, high_hbm)
     put_raw.wait()
     copies.finish()
 
 
-def first_call(sz, s, gx, keep, recv, bb):
+def first_call(sz, s, gx, keep, recv, bb, weight):
     line, field, part = (sz.modes, sz.rows), (sz.rows, sz.cells), (sz.thin, sz.cells)
+    packed = (sz.half_j, sz.blk_k, sz.groups * 128, sz.lgs * sz.chans)
     return run(
         "first",
         lambda *refs: first_kernel(sz, *refs),
-        [(shape(part), True), (shape(part), True), (shape(field), True), (shape(line), True)],
-        [smem, smem, vmem, vmem, vmem],
-        (s, gx, keep, recv, near(bb)),
-        [pltpu.VMEM(field, bf16), pltpu.VMEM(line, bf16)],
-        2 + 2 * sz.groups,
+        [(shape(part), True), (shape(part), True), (shape(field), True), (shape(line), True), (shape(packed), True)],
+        [smem, smem, vmem, vmem, vmem, hbm],
+        (s, gx, keep, recv, near(bb), weight),
+        [
+            pltpu.VMEM(field, bf16),
+            pltpu.VMEM(line, bf16),
+            pltpu.VMEM((sz.half_j,) + weight.shape[2:], bf16),
+            pltpu.VMEM(packed, bf16),
+        ],
+        2 + 2 * sz.groups + 2 * sz.half_j,
     )
 
 
@@ -339,16 +362,7 @@
                 pieces += [jnp.where(lane_c == c + row_c, part, 0.0) for c in range(0, sz.cpl, each)]
             ya[g * 128 : (g + 1) * 128, :] = jnp.concatenate(pieces, axis=0).astype(bf16)
         copies.send(ya, ya_hbm)
-    for jj in range(sz.half_j):
-        gets[jj].wait()
-        for kk in range(sz.blk_k):
-            for h in range(sz.groups):
-                lanes = [
-                    w[jj, kk, lg * 8 : (lg + 1) * 8, h * sz.cpl : (h + 1) * sz.cpl, :].reshape(128, sz.chans)
-                    for lg in range(sz.lgs)
-                ]
-                out[jj, kk, h * 128 : (h + 1) * 128, :] = jnp.concatenate(lanes, axis=1)
-        copies.send(out.at[jj], out_hbm.at[jj])
+    pack_rows(sz, copies, gets, w, out, out_hbm)
     copies.finish()
 
 
@@ -640,15 +654,18 @@
 
 
 def forward_kernel(
-    sz, s_ref, own_ref, other_ref, u, mine_hbm, next_hbm, bb_hbm, low_hbm, high_hbm, v, slope, bb, out, w, field, sems
+    sz, s_ref, own_hbm, other_hbm, u, mine_hbm, next_hbm, bb_hbm, low_hbm, high_hbm, v, slope, bb, out, w, field, own_ref, other_ref, sems
 ):
     copies = Copies(sems)
+    get_small = [copies.start(own_hbm, own_ref), copies.start(other_hbm, other_ref)]
     get_bb, get_v = [], []
     for at, cut in enumerate(cuts(sz)):
         get_bb.append(copies.start(bb_hbm.at[:, cut], bb.at[:, cut]))
         if at == 0:
             get_v = field_copies(sz, copies, mine_hbm, next_hbm, field)
     (get_w,) = copies.choose(s_ref[0] == 1, [(low_hbm, high_hbm, w)])
+    for get in get_small:
+        get.wait()
     weight, bias = small_parts(sz, s_ref, own_ref, other_ref, 0)
     matrix = point_matrix(sz, weight, True)
     column = nt(spread(sz), bias)[:, :1]
@@ -677,10 +694,10 @@
             (kept(line), False),
             (kept(low.shape), False),
         ],
-        [smem, vmem, vmem, vmem, hbm, hbm, hbm, hbm, hbm],
+        [smem, hbm, hbm, vmem, hbm, hbm, hbm, hbm, hbm],
         (s, own_small, other_small, u, mine, other, bb, low, high),
-        [pltpu.VMEM(field, bf16)],
-        3 + len(cuts(sz)),
+        [pltpu.VMEM(field, bf16), pltpu.VMEM(own_small.shape, bf16), pltpu.VMEM(own_small.shape, bf16)],
+        5 + len(cuts(sz)),
     )
 
 
@@ -869,10 +886,10 @@
     bb = tables_call(sz, gx, bx, bz)
     own_small = jnp.concatenate([point_weight[0], jnp.broadcast_to(point_bias, (16, sz.chans))], axis=0)
     other_small = swap(own_small)
-    mine_v, send_v, raw_g, out = first_call(sz, s, gx, keep, recv, bb)
+    mine_v, send_v, raw_g, out, high = first_call(sz, s, gx, keep, recv, bb, spectral_weight)
+    high = swap(high)
     next_v = swap_near(sz, send_v)
     r = exchange(out)
-    high = swap(pack_call(sz, mine_v, spectral_weight, sz.half_j))
     mine_g, send_g = split_call(sz, gx, raw_g, mine_v)
     next_g = swap_near(sz, send_g)
     low, ya = pack_call(sz, mine_v, spectral_weight, 0, by)

time: 130 us -> 129 us (level)
    unnamed x16 -> x18, local copies, waits for them, and re-layouts: 3.13 us -> 2.43 us
    pallas_call x14 -> x13, Pallas kernels: 39.3 us -> 38.9 us  [run(): pl.pallas_call(kernel, out_shape=tuple((pltpu.HBM(o.shape, o.dtype) if aw...]
  transfers between devices with their start and end apart: 8 -> 8, of which waited for: 4 -> 4; matrix products, arithmetic and copies ran while one was open for 0% -> 0% of each run, Pallas kernels for 24% -> 25%
where the time goes in v5:
time: 129 us; the launch traced here: 128 us
  blocking collectives  61 us (47%)
  Pallas kernels  46.8 us (36%)
  starting transfers between devices  13.1 us (10%)
  local copies, waits for them, and re-layouts  3.58 us (3%)
  waiting for transfers between devices  2.53 us (2%)
    all_to_all x6, blocking collectives, exchange(): return lax.all_to_all(block, AXES, split_axis=0, concat_axis=0, tiled=True)  61 us
    pallas_call x13, Pallas kernels, run(): pl.pallas_call(kernel, out_shape=tuple((pltpu.HBM(o.shape, o.dtype) if aw...  38.9 us
    pallas_call x1, Pallas kernels, outer_call(): pl.pallas_call(lambda *refs: outer_kernel(sz, *refs), grid=(sz.blk_j // e...  7.25 us
    all_to_all x1, starting transfers between devices, exchange(): return lax.all_to_all(block, AXES, split_axis=0, concat_axis=0, tiled=True)  4.82 us
    ppermute x2, starting transfers between devices, swap_near(): return lax.ppermute(block, 'gx', [(i, i ^ 1) for i in range(sz.n_gx)])  4.57 us
    all_to_all x1, starting transfers between devices, local(): parts = lax.all_to_all(parts, AXES, split_axis=0, concat_axis=0, tiled=True)  2.58 us
  transfers between devices with their start and end apart: 8, of which 4 were waited for; matrix products, arithmetic and copies ran while one was open for 0% of the time, Pallas kernels for 25%

profile of v5, /device:TPU:0, one launch (start us, length us, event | category | flops | bytes accessed | tf_op | source)
XLA Modules:
  0.0 128.1 jit_solution(6584090403476652957)
XLA Ops:
  0.7 1.6 %copy-done = bf16[1,32,16,16,128]{4,3,2,1,0:T(8,128)(2,1)S(1)} copy-done((bf16[1,32,16,16,128]{4,3,2,1,0:T(8,128)(2,1)S(1)}, bf16[1,32,16,16,128]{4,3,2,1,0:T(8,128)(2,1)}, u32[]{:S(2)}) %copy-start) | copy-done | bytes 2097176
  2.2 1.1 dynamic-slice_bitcast_fusion.1
  3.3 0.5 collective-permute-start.1
  3.8 2.2 %tables.1.refs_4_ = bf16[512,2048]{1,0:T(8,128)(2,1)S(1)} custom-call(s32[2]{0:T(128)S(1)} %pad_add_fusion.refs_0_.refs_1_, bf16[4,512,16]{2,1,0:T(8,128)(2,1)} %constant.37.clone.refs_1_, bf16[512,128]{1,0:T(8,128)(2,1)} %constant.38.clone.refs_2_), custom_call_target="tpu_custom_call" | custom-call | bytes 3000000 | tf_op jit(solution)/shard_map/tables/pallas_call | solution.py:69
  6.2 5.3 %first.1 = (bf16[128,2048]{1,0:T(8,128)(2,1)}, bf16[128,2048]{1,0:T(8,128)(2,1)}, bf16[256,2048]{1,0:T(8,128)(2,1)}, bf16[512,256]{1,0:T(8,128)(2,1)}, bf16[4,4,256,128]{3,2,1,0:T(8,128)(2,1)}) custom-call(s32[1]{0:T(128)} %bitcast.refs_0_, s32[2]{0:T(128)S(1)} %pad_add_fusion.refs_0_.refs_1_, bf16[256,2048]{1,0:T(8,128)(2,1)S(1)} %dynamic-slice_bitcast_fusion.refs_2_, ...), custom_call_target="tpu_custom_call" | custom-call | bytes 3000000 | tf_op jit(solution)/shard_map/first/pallas_call | solution.py:69
  11.6 0.4 collective-permute-start.2
  12.0 2.7 %collective-permute-start.3 = (bf16[128,2048]{1,0:T(8,128)(2,1)}, bf16[128,2048]{1,0:T(8,128)(2,1)S(1)}, u32[]{:S(2)}, u32[]{:S(2)}) collective-permute-start(bf16[128,2048]{1,0:T(8,128)(2,1)} %get-tuple-element.44), channel_id=1, source_target_pairs={{0,4},{4,0},{8,12},{12,8},{1,5},{5,1},{9,13},{13,9},{2,6},{6,2},{1... | collective-permute-start | bytes 1572872 | tf_op jit(solution)/shard_map/ppermute | solution.py:866
  14.7 4.8 %all-to-all-start = ((bf16[32,16,256]{2,1,0:T(8,128)(2,1)}), bf16[32,16,256]{2,1,0:T(8,128)(2,1)S(1)}, u32[]{:S(2)}, u32[]{:S(2)}) async-start(bf16[32,16,256]{2,1,0:T(8,128)(2,1)} %bitcast.44), calls=%async_computation | async-start | bytes 524288 | tf_op jit(solution)/shard_map/all_to_all | solution.py:858
  19.6 3.3 %split.1 = (bf16[128,2048]{1,0:T(8,128)(2,1)}, bf16[128,2048]{1,0:T(8,128)(2,1)}) custom-call(s32[2]{0:T(128)S(1)} %pad_add_fusion.refs_0_.refs_1_, bf16[256,2048]{1,0:T(8,128)(2,1)} %get-tuple-element.50.refs_1_, bf16[128,2048]{1,0:T(8,128)(2,1)} %get-tuple-element.40.refs_0_.refs_3_.refs_4_.refs_2_.refs_8_), custom_call_target="tpu_custom_call" | custom-call | tf_op jit(solution)/shard_map/split/pallas_call | solution.py:69
  22.9 1.8 %collective-permute-start.4 = (bf16[128,2048]{1,0:T(8,128)(2,1)}, bf16[128,2048]{1,0:T(8,128)(2,1)}, u32[]{:S(2)}, u32[]{:S(2)}) collective-permute-start(bf16[128,2048]{1,0:T(8,128)(2,1)} %get-tuple-element.51), channel_id=1, source_target_pairs={{0,4},{4,0},{8,12},{12,8},{1,5},{5,1},{9,13},{13,9},{2,6},{6,2},{1... | collective-permute-start | bytes 1572872 | tf_op jit(solution)/shard_map/ppermute | solution.py:866
  24.8 4.7 %wide.1.refs_6_ = bf16[512,4096]{1,0:T(8,128)(2,1)} custom-call(s32[2]{0:T(128)S(1)} %pad_add_fusion.refs_0_.refs_1_, bf16[4,512,16]{2,1,0:T(8,128)(2,1)} %constant.37.clone.refs_1_, bf16[512,128]{1,0:T(8,128)(2,1)} %constant.38.clone.refs_2_, bf16[128,2048]{1,0:T(8,128)(2,1)} %get-tuple-element.40.refs_0_.refs_3_.refs_4_.refs_2_.refs_8_), custom_call_target="tpu_custom_call" | custom-call | tf_op jit(solution)/shard_map/wide/pallas_call | solution.py:69
  29.6 3.8 %pack.1 = (bf16[4,4,256,128]{3,2,1,0:T(8,128)(2,1)}, bf16[1024,512]{1,0:T(8,128)(2,1)}) custom-call(bf16[128,2048]{1,0:T(8,128)(2,1)} %get-tuple-element.40.refs_0_.refs_3_.refs_4_.refs_2_.refs_8_, bf16[1,8,4,32,32,32]{5,4,3,2,1,0:T(8,128)(2,1)} %refs_1_.3, bf16[128,512]{1,0:T(8,128)(2,1)} %constant.39.clone.refs_2_), custom_call_target="tpu_custom_call" | custom-call | tf_op jit(solution)/shard_map/pack/pallas_call | solution.py:69
  33.4 1.0 all-to-all-done
  34.4 0.8 copy-done.6
  35.2 3.2 %mix.3 = (bf16[32,512]{1,0:T(8,128)(2,1)}, bf16[512,128]{1,0:T(8,128)(2,1)S(1)}, bf16[1024,512]{1,0:T(8,128)(2,1)S(1)}) custom-call(s32[1]{0:T(128)} %bitcast.refs_0_, bf16[512,256]{1,0:T(8,128)(2,1)S(1)} %bitcast.31, bf16[1024,512]{1,0:T(8,128)(2,1)} %get-tuple-element.41.refs_2_, bf16[4,4,256,128]{3,2,1,0:T(8,128)(2,1)} %get-tuple-element.42.refs_3_.refs_7_, ...), custom_call_target="tpu_custom_call" | custom-call | bytes 3000000 | tf_op jit(solution)/shard_map/mix/pallas_call | solution.py:69
  38.4 11.5 %all_to_all.83 = bf16[32,16,128]{2,1,0:T(8,128)(2,1)S(1)} all-to-all(bf16[32,16,128]{2,1,0:T(8,128)(2,1)S(1)} %bitcast.42), channel_id=1, replica_groups=mesh['section'=2,'gx'=4,'gy'=4] {'section','gx','gy'}, dimensions={0} | all-to-all | bytes 262144 | tf_op jit(solution)/shard_map/all_to_all | solution.py:858
  49.9 4.7 %forward.1 = (bf16[128,4096]{1,0:T(8,128)(2,1)S(1)}, f32[128,4096]{1,0:T(8,128)S(1)}, bf16[512,4096]{1,0:T(8,128)(2,1)S(1)}, bf16[512,128]{1,0:T(8,128)(2,1)S(1)}, bf16[4,4,256,128]{3,2,1,0:T(8,128)(2,1)S(1)}) custom-call(s32[1]{0:T(128)} %bitcast.refs_0_, bf16[48,32]{1,0:T(8,128)(2,1)} %copy-done.3, bf16[48,32]{1,0:T(8,128)(2,1)} %copy-done.1, ...), custom_call_target="tpu_custom_call" | custom-call | bytes 3000000 | tf_op jit(solution)/shard_map/forward/pallas_call | solution.py:69
  54.6 9.9 %all_to_all.84 = bf16[32,16,128]{2,1,0:T(8,128)(2,1)S(1)} all-to-all(bf16[32,16,128]{2,1,0:T(8,128)(2,1)S(1)} %bitcast.40), channel_id=1, replica_groups=mesh['section'=2,'gx'=4,'gy'=4] {'section','gx','gy'}, dimensions={0} | all-to-all | bytes 262144 | tf_op jit(solution)/shard_map/all_to_all | solution.py:858
  64.5 1.5 %mix.4 = (bf16[32,512]{1,0:T(8,128)(2,1)}, bf16[512,128]{1,0:T(8,128)(2,1)S(1)}) custom-call(s32[1]{0:T(128)} %bitcast.refs_0_, bf16[512,128]{1,0:T(8,128)(2,1)S(1)} %bitcast.37, bf16[1024,512]{1,0:T(8,128)(2,1)S(1)} %get-tuple-element.47.refs_2_, bf16[4,4,256,128]{3,2,1,0:T(8,128)(2,1)S(1)} %get-tuple-element.48.refs_3_), custom_call_target="tpu_custom_call" | custom-call | bytes 3000000 | tf_op jit(solution)/shard_map/mix/pallas_call | solution.py:69
  66.1 9.9 %all_to_all.85 = bf16[32,16,128]{2,1,0:T(8,128)(2,1)S(1)} all-to-all(bf16[32,16,128]{2,1,0:T(8,128)(2,1)S(1)} %bitcast.38), channel_id=1, replica_groups=mesh['section'=2,'gx'=4,'gy'=4] {'section','gx','gy'}, dimensions={0} | all-to-all | bytes 262144 | tf_op jit(solution)/shard_map/all_to_all | solution.py:858
  76.0 4.3 %turn.1 = (bf16[128,4096]{1,0:T(8,128)(2,1)S(1)}, f32[16,128]{1,0:T(8,128)S(1)}, bf16[512,128]{1,0:T(8,128)(2,1)S(1)}) custom-call(s32[1]{0:T(128)} %bitcast.refs_0_, bf16[48,32]{1,0:T(8,128)(2,1)S(1)} %copy-done.4, bf16[48,32]{1,0:T(8,128)(2,1)S(1)} %copy-done.2, bf16[512,128]{1,0:T(8,128)(2,1)S(1)} %bitcast.35, ...), custom_call_target="tpu_custom_call" | custom-call | bytes 3000000 | tf_op jit(solution)/shard_map/turn/pallas_call | solution.py:69
  80.3 9.9 %all_to_all.86 = bf16[32,16,128]{2,1,0:T(8,128)(2,1)S(1)} all-to-all(bf16[32,16,128]{2,1,0:T(8,128)(2,1)S(1)} %bitcast.41), channel_id=1, replica_groups=mesh['section'=2,'gx'=4,'gy'=4] {'section','gx','gy'}, dimensions={0} | all-to-all | bytes 262144 | tf_op jit(solution)/shard_map/all_to_all | solution.py:858
  90.3 1.7 %mix.5 = (bf16[32,512]{1,0:T(8,128)(2,1)}, bf16[512,128]{1,0:T(8,128)(2,1)S(1)}) custom-call(s32[1]{0:T(128)} %bitcast.refs_0_, bf16[512,128]{1,0:T(8,128)(2,1)S(1)} %bitcast.36, bf16[1024,512]{1,0:T(8,128)(2,1)S(1)} %get-tuple-element.47.refs_2_, bf16[4,4,256,128]{3,2,1,0:T(8,128)(2,1)S(1)} %get-tuple-element.48.refs_3_), custom_call_target="tpu_custom_call" | custom-call | bytes 3000000 | tf_op jit(solution)/shard_map/mix/pallas_call | solution.py:69
  92.0 9.9 %all_to_all.87 = bf16[32,16,128]{2,1,0:T(8,128)(2,1)S(1)} all-to-all(bf16[32,16,128]{2,1,0:T(8,128)(2,1)S(1)} %bitcast.43), channel_id=1, replica_groups=mesh['section'=2,'gx'=4,'gy'=4] {'section','gx','gy'}, dimensions={0} | all-to-all | bytes 262144 | tf_op jit(solution)/shard_map/all_to_all | solution.py:858
  101.9 3.1 %back.1 = (bf16[32,24,128]{2,1,0:T(8,128)(2,1)S(1)}, bf16[512,128]{1,0:T(8,128)(2,1)S(1)}) custom-call(s32[1]{0:T(128)} %bitcast.refs_0_, bf16[48,32]{1,0:T(8,128)(2,1)S(1)} %copy-done.4, bf16[48,32]{1,0:T(8,128)(2,1)S(1)} %copy-done.2, bf16[512,128]{1,0:T(8,128)(2,1)S(1)} %bitcast.32, bf16[128,4096]{1,0:T(8,128)(2,1)S(1)} %get-tuple-element.57.refs_4_, ...), custom_call_target="tpu_custom_call" | custom-call | bytes 3000000 | tf_op jit(solution)/shard_map/back/pallas_call | solution.py:69
  105.1 9.9 %all_to_all.88 = bf16[32,16,128]{2,1,0:T(8,128)(2,1)S(1)} all-to-all(bf16[32,16,128]{2,1,0:T(8,128)(2,1)S(1)} %bitcast.39), channel_id=1, replica_groups=mesh['section'=2,'gx'=4,'gy'=4] {'section','gx','gy'}, dimensions={0} | all-to-all | bytes 262144 | tf_op jit(solution)/shard_map/all_to_all | solution.py:858
  115.0 2.6 %all-to-all-start.7 = ((bf16[32,24,128]{2,1,0:T(8,128)(2,1)}), bf16[32,24,128]{2,1,0:T(8,128)(2,1)S(1)}, u32[]{:S(2)}, u32[]{:S(2)}) async-start(bf16[32,24,128]{2,1,0:T(8,128)(2,1)} %copy-done.5), calls=%async_computation.7 | async-start | bytes 393216 | tf_op jit(solution)/shard_map/all_to_all | solution.py:907
  117.6 1.0 spec.1
  118.7 1.1 collective-permute-done.5.refs_1_
  119.9 7.2 %outer.1.refs_1_ = f32[1,8,4,32,32,32]{5,4,3,2,1,0:T(8,128)} custom-call(bf16[2,32,512]{2,1,0:T(8,128)(2,1)S(1)} %get-tuple-element.66.refs_0_, bf16[2,32,512]{2,1,0:T(8,128)(2,1)S(1)} %collective-permute-done.5.refs_1_), custom_call_target="tpu_custom_call" | custom-call | bytes 20000000 | tf_op jit(solution)/shard_map/outer/pallas_call | solution.py:841
  127.1 0.2 all-to-all-done.7.refs_0_
  127.4 0.7 finish.1
  (28 shorter events, 0.6 us)
Async XLA Ops:
  0.6 1.6 %copy-start = (bf16[1,32,16,16,128]{4,3,2,1,0:T(8,128)(2,1)S(1)}, bf16[1,32,16,16,128]{4,3,2,1,0:T(8,128)(2,1)}, u32[]{:S(2)}) copy-start(bf16[1,32,16,16,128]{4,3,2,1,0:T(8,128)(2,1)} %param.7) | copy-start | bytes 6291460
  3.3 3.0 %collective-permute-start.1 = (bf16[256,2048]{1,0:T(8,128)(2,1)}, bf16[256,2048]{1,0:T(8,128)(2,1)S(1)}, u32[]{:S(2)}, u32[]{:S(2)}) collective-permute-start(bf16[256,2048]{1,0:T(8,128)(2,1)} %dynamic-slice_bitcast_fusion.1), channel_id=1, source_target_pairs={{0,16},{16,0},{1,17},{17,1},{2,18},{18,2},{3,19},{19,3},{4,20},{20... | collective-permute-start | bytes 3145736 | tf_op jit(solution)/shard_map/ppermute | solution.py:862
  11.5 13.2 %copy-start.8 = (bf16[1,32]{1,0:T(2,128)(2,1)S(1)}, bf16[1,32]{1,0:T(2,128)(2,1)}, u32[]{:S(2)}) copy-start(bf16[1,32]{1,0:T(2,128)(2,1)} %param.10) | copy-start | bytes 196
  11.6 13.1 %copy-start.7 = (bf16[1,32,32]{2,1,0:T(8,128)(2,1)S(1)}, bf16[1,32,32]{2,1,0:T(8,128)(2,1)}, u32[]{:S(2)}) copy-start(bf16[1,32,32]{2,1,0:T(8,128)(2,1)} %param.9) | copy-start | bytes 6148
  11.6 22.9 %collective-permute-start.2 = (bf16[4,4,256,128]{3,2,1,0:T(8,128)(2,1)}, bf16[4,4,256,128]{3,2,1,0:T(8,128)(2,1)}, u32[]{:S(2)}, u32[]{:S(2)}) collective-permute-start(bf16[4,4,256,128]{3,2,1,0:T(8,128)(2,1)} %get-tuple-element.43), channel_id=1, source_target_pairs={{0,16},{16,0},{1,17},{17,1},{2,18},{18,2},{3,19},{19,3},{4,20},{20... | collective-permute-start | bytes 3145736 | tf_op jit(solution)/shard_map/ppermute | solution.py:862
  12.0 22.4 %collective-permute-start.3 = (bf16[128,2048]{1,0:T(8,128)(2,1)}, bf16[128,2048]{1,0:T(8,128)(2,1)S(1)}, u32[]{:S(2)}, u32[]{:S(2)}) collective-permute-start(bf16[128,2048]{1,0:T(8,128)(2,1)} %get-tuple-element.44), channel_id=1, source_target_pairs={{0,4},{4,0},{8,12},{12,8},{1,5},{5,1},{9,13},{13,9},{2,6},{6,2},{1... | collective-permute-start | bytes 1572872 | tf_op jit(solution)/shard_map/ppermute | solution.py:866
  14.7 19.7 %all-to-all-start = ((bf16[32,16,256]{2,1,0:T(8,128)(2,1)}), bf16[32,16,256]{2,1,0:T(8,128)(2,1)S(1)}, u32[]{:S(2)}, u32[]{:S(2)}) async-start(bf16[32,16,256]{2,1,0:T(8,128)(2,1)} %bitcast.44), calls=%async_computation | async-start | bytes 524288 | tf_op jit(solution)/shard_map/all_to_all | solution.py:858
  22.9 43.2 %collective-permute-start.4 = (bf16[128,2048]{1,0:T(8,128)(2,1)}, bf16[128,2048]{1,0:T(8,128)(2,1)}, u32[]{:S(2)}, u32[]{:S(2)}) collective-permute-start(bf16[128,2048]{1,0:T(8,128)(2,1)} %get-tuple-element.51), channel_id=1, source_target_pairs={{0,4},{4,0},{8,12},{12,8},{1,5},{5,1},{9,13},{13,9},{2,6},{6,2},{1... | collective-permute-start | bytes 1572872 | tf_op jit(solution)/shard_map/ppermute | solution.py:866
  24.7 4.8 %copy-start.3 = (bf16[48,32]{1,0:T(8,128)(2,1)}, bf16[48,32]{1,0:T(8,128)(2,1)S(1)}, u32[]{:S(2)}) copy-start(bf16[48,32]{1,0:T(8,128)(2,1)S(1)} %pad_maximum_fusion.refs_1_) | copy-start | bytes 9220
  24.7 8.6 %collective-permute-start = (bf16[48,32]{1,0:T(8,128)(2,1)S(1)}, bf16[48,32]{1,0:T(8,128)(2,1)S(1)}, u32[]{:S(2)}, u32[]{:S(2)}) collective-permute-start(bf16[48,32]{1,0:T(8,128)(2,1)S(1)} %pad_maximum_fusion.refs_1_), channel_id=1, source_target_pairs={{0,16},{16,0},{1,17},{17,1},{2,18},{18,2},{3,19},{19,3},{4,20},{20... | collective-permute-start | bytes 9224 | tf_op jit(solution)/shard_map/ppermute | solution.py:862
  33.4 1.9 %copy-start.1 = (bf16[48,32]{1,0:T(8,128)(2,1)}, bf16[48,32]{1,0:T(8,128)(2,1)S(1)}, u32[]{:S(2)}) copy-start(bf16[48,32]{1,0:T(8,128)(2,1)S(1)} %collective-permute-done.refs_5_.refs_2_) | copy-start | bytes 9220
  34.4 0.8 copy-start.6
  54.6 21.4 %copy-start.2 = (bf16[48,32]{1,0:T(8,128)(2,1)S(1)}, bf16[48,32]{1,0:T(8,128)(2,1)}, u32[]{:S(2)}) copy-start(bf16[48,32]{1,0:T(8,128)(2,1)} %copy-done.1) | copy-start | bytes 9220
  54.6 21.4 %copy-start.4 = (bf16[48,32]{1,0:T(8,128)(2,1)S(1)}, bf16[48,32]{1,0:T(8,128)(2,1)}, u32[]{:S(2)}) copy-start(bf16[48,32]{1,0:T(8,128)(2,1)} %copy-done.3) | copy-start | bytes 9220
  105.0 9.9 %copy-start.5 = (bf16[32,24,128]{2,1,0:T(8,128)(2,1)}, bf16[32,24,128]{2,1,0:T(8,128)(2,1)S(1)}, u32[]{:S(2)}) copy-start(bf16[32,24,128]{2,1,0:T(8,128)(2,1)S(1)} %get-tuple-element.68) | copy-start | bytes 589828
  115.0 12.4 %all-to-all-start.7 = ((bf16[32,24,128]{2,1,0:T(8,128)(2,1)}), bf16[32,24,128]{2,1,0:T(8,128)(2,1)S(1)}, u32[]{:S(2)}, u32[]{:S(2)}) async-start(bf16[32,24,128]{2,1,0:T(8,128)(2,1)} %copy-done.5), calls=%async_computation.7 | async-start | bytes 393216 | tf_op jit(solution)/shard_map/all_to_all | solution.py:907
  118.6 1.3 %collective-permute-start.5 = (bf16[2,32,512]{2,1,0:T(8,128)(2,1)S(1)}, bf16[2,32,512]{2,1,0:T(8,128)(2,1)S(1)}, u32[]{:S(2)}, u32[]{:S(2)}) collective-permute-start(bf16[2,32,512]{2,1,0:T(8,128)(2,1)S(1)} %get-tuple-element.67), channel_id=1, source_target_pairs={{0,16},{16,0},{1,17},{17,1},{2,18},{18,2},{3,19},{19,3},{4,20},{20... | collective-permute-start | bytes 196616 | tf_op jit(solution)/shard_map/ppermute | solution.py:862

commit v6 on v5

--- a/solution.py
+++ b/solution.py
@@ -260,10 +260,16 @@
     gets.append(copies.start(bz_hbm, bz))
     for get in gets:
         get.wait()
+    depth = sz.depth
+    along = bz[...].astype(f32)
     for side in range(2):
-        at = slice(side * sz.cells, (side + 1) * sz.cells)
-        fill_table(sz, bx.at[side], bz, bb.at[:, at])
-        copies.send(bb.at[:, at], bb_hbm.at[:, at])
+        across = bx[side].astype(f32)
+        for x in range(sz.len_x):
+            at = side * sz.cells + x * depth
+            bb[:, at : at + depth] = (across[:, x : x + 1] * along).astype(bf16)
+            if x % 4 == 3:
+                part = slice(at - 3 * depth, at + depth)
+                copies.send(bb.at[:, part], bb_hbm.at[:, part])
     copies.finish()
 
 
@@ -275,7 +281,7 @@
         [smem, hbm, hbm, hbm],
         (gx, bx, bz, after),
         [pltpu.VMEM((2,) + bx.shape[1:], bf16), pltpu.VMEM(bz.shape, bf16), pltpu.VMEM((sz.modes, sz.wide), bf16)],
-        5,
+        3 + sz.len_x // 2,
         0,
     )
     return bb
@@ -318,9 +324,16 @@
 
 def split_kernel(sz, gx_ref, raw_hbm, after_hbm, mine_hbm, send_hbm, raw, field, sems):
     copies = Copies(sems)
-    copies.start(raw_hbm, raw).wait()
-    field[...] = nn(reorder(sz), raw[...]).astype(bf16)
-    send_quarters(sz, gx_ref, field, mine_hbm, send_hbm, copies)
+    half = sz.cells // 2
+    halves = [slice(0, half), slice(half, sz.cells)]
+    gets = [copies.start(raw_hbm.at[:, cut], raw.at[:, cut]) for cut in halves]
+    matrix = reorder(sz)
+    for get, cut in zip(gets, halves):
+        get.wait()
+        field[:, cut] = nn(matrix, raw[:, cut]).astype(bf16)
+        send_quarters(
+            sz, gx_ref, field.at[:, cut], mine_hbm.at[:, cut], send_hbm.at[:, cut], copies
+        )
     copies.finish()
 
 
@@ -333,7 +346,7 @@
         [smem, hbm, hbm],
         (gx, raw, after),
         [pltpu.VMEM(field, bf16), pltpu.VMEM(field, bf16)],
-        1 + 2 * sz.groups,
+        2 + 4 * sz.groups,
         0,
     )
 

time: 129 us -> 129 us (level)
  transfers between devices with their start and end apart: 8 -> 8, of which waited for: 4 -> 4; matrix products, arithmetic and copies ran while one was open for 0% -> 0% of each run, Pallas kernels for 25% -> 24%
where the time goes in v6:
time: 129 us; the launch traced here: 128 us
  blocking collectives  61 us (47%)
  Pallas kernels  46.4 us (36%)
  starting transfers between devices  13.1 us (10%)
  local copies, waits for them, and re-layouts  3.58 us (3%)
  waiting for transfers between devices  2.99 us (2%)
    all_to_all x6, blocking collectives, exchange(): return lax.all_to_all(block, AXES, split_axis=0, concat_axis=0, tiled=True)  61 us
    pallas_call x13, Pallas kernels, run(): pl.pallas_call(kernel, out_shape=tuple((pltpu.HBM(o.shape, o.dtype) if aw...  38.4 us
    pallas_call x1, Pallas kernels, outer_call(): pl.pallas_call(lambda *refs: outer_kernel(sz, *refs), grid=(sz.blk_j // e...  7.25 us
    all_to_all x1, starting transfers between devices, exchange(): return lax.all_to_all(block, AXES, split_axis=0, concat_axis=0, tiled=True)  4.82 us
    ppermute x2, starting transfers between devices, swap_near(): return lax.ppermute(block, 'gx', [(i, i ^ 1) for i in range(sz.n_gx)])  4.58 us
    all_to_all x1, starting transfers between devices, local(): parts = lax.all_to_all(parts, AXES, split_axis=0, concat_axis=0, tiled=True)  2.58 us
  transfers between devices with their start and end apart: 8, of which 4 were waited for; matrix products, arithmetic and copies ran while one was open for 0% of the time, Pallas kernels for 24%

profile of v6, /device:TPU:0, one launch (start us, length us, event | category | flops | bytes accessed | tf_op | source)
XLA Modules:
  0.0 128.1 jit_solution(13787108147635703612)
XLA Ops:
  0.7 1.6 %copy-done = bf16[1,32,16,16,128]{4,3,2,1,0:T(8,128)(2,1)S(1)} copy-done((bf16[1,32,16,16,128]{4,3,2,1,0:T(8,128)(2,1)S(1)}, bf16[1,32,16,16,128]{4,3,2,1,0:T(8,128)(2,1)}, u32[]{:S(2)}) %copy-start) | copy-done | bytes 2097176
  2.2 1.1 dynamic-slice_bitcast_fusion.1
  3.3 0.5 collective-permute-start.1
  3.8 2.2 %tables.1.refs_4_ = bf16[512,2048]{1,0:T(8,128)(2,1)S(1)} custom-call(s32[2]{0:T(128)S(1)} %pad_add_fusion.refs_0_.refs_1_, bf16[4,512,16]{2,1,0:T(8,128)(2,1)} %constant.37.clone.refs_1_, bf16[512,128]{1,0:T(8,128)(2,1)} %constant.38.clone.refs_2_), custom_call_target="tpu_custom_call" | custom-call | bytes 3000000 | tf_op jit(solution)/shard_map/tables/pallas_call | solution.py:69
  6.2 5.3 %first.1 = (bf16[128,2048]{1,0:T(8,128)(2,1)}, bf16[128,2048]{1,0:T(8,128)(2,1)}, bf16[256,2048]{1,0:T(8,128)(2,1)}, bf16[512,256]{1,0:T(8,128)(2,1)}, bf16[4,4,256,128]{3,2,1,0:T(8,128)(2,1)}) custom-call(s32[1]{0:T(128)} %bitcast.refs_0_, s32[2]{0:T(128)S(1)} %pad_add_fusion.refs_0_.refs_1_, bf16[256,2048]{1,0:T(8,128)(2,1)S(1)} %dynamic-slice_bitcast_fusion.refs_2_, ...), custom_call_target="tpu_custom_call" | custom-call | bytes 3000000 | tf_op jit(solution)/shard_map/first/pallas_call | solution.py:69
  11.6 0.4 collective-permute-start.2
  12.0 2.7 %collective-permute-start.3 = (bf16[128,2048]{1,0:T(8,128)(2,1)}, bf16[128,2048]{1,0:T(8,128)(2,1)S(1)}, u32[]{:S(2)}, u32[]{:S(2)}) collective-permute-start(bf16[128,2048]{1,0:T(8,128)(2,1)} %get-tuple-element.44), channel_id=1, source_target_pairs={{0,4},{4,0},{8,12},{12,8},{1,5},{5,1},{9,13},{13,9},{2,6},{6,2},{1... | collective-permute-start | bytes 1572872 | tf_op jit(solution)/shard_map/ppermute | solution.py:879
  14.7 4.8 %all-to-all-start = ((bf16[32,16,256]{2,1,0:T(8,128)(2,1)}), bf16[32,16,256]{2,1,0:T(8,128)(2,1)S(1)}, u32[]{:S(2)}, u32[]{:S(2)}) async-start(bf16[32,16,256]{2,1,0:T(8,128)(2,1)} %bitcast.44), calls=%async_computation | async-start | bytes 524288 | tf_op jit(solution)/shard_map/all_to_all | solution.py:871
  19.6 3.1 %split.1 = (bf16[128,2048]{1,0:T(8,128)(2,1)}, bf16[128,2048]{1,0:T(8,128)(2,1)}) custom-call(s32[2]{0:T(128)S(1)} %pad_add_fusion.refs_0_.refs_1_, bf16[256,2048]{1,0:T(8,128)(2,1)} %get-tuple-element.50.refs_1_, bf16[128,2048]{1,0:T(8,128)(2,1)} %get-tuple-element.40.refs_0_.refs_3_.refs_4_.refs_2_.refs_8_), custom_call_target="tpu_custom_call" | custom-call | tf_op jit(solution)/shard_map/split/pallas_call | solution.py:69
  22.7 1.8 %collective-permute-start.4 = (bf16[128,2048]{1,0:T(8,128)(2,1)}, bf16[128,2048]{1,0:T(8,128)(2,1)}, u32[]{:S(2)}, u32[]{:S(2)}) collective-permute-start(bf16[128,2048]{1,0:T(8,128)(2,1)} %get-tuple-element.51), channel_id=1, source_target_pairs={{0,4},{4,0},{8,12},{12,8},{1,5},{5,1},{9,13},{13,9},{2,6},{6,2},{1... | collective-permute-start | bytes 1572872 | tf_op jit(solution)/shard_map/ppermute | solution.py:879
  24.6 4.4 %wide.1.refs_6_ = bf16[512,4096]{1,0:T(8,128)(2,1)} custom-call(s32[2]{0:T(128)S(1)} %pad_add_fusion.refs_0_.refs_1_, bf16[4,512,16]{2,1,0:T(8,128)(2,1)} %constant.37.clone.refs_1_, bf16[512,128]{1,0:T(8,128)(2,1)} %constant.38.clone.refs_2_, bf16[128,2048]{1,0:T(8,128)(2,1)} %get-tuple-element.40.refs_0_.refs_3_.refs_4_.refs_2_.refs_8_), custom_call_target="tpu_custom_call" | custom-call | tf_op jit(solution)/shard_map/wide/pallas_call | solution.py:69
  29.1 3.8 %pack.1 = (bf16[4,4,256,128]{3,2,1,0:T(8,128)(2,1)}, bf16[1024,512]{1,0:T(8,128)(2,1)}) custom-call(bf16[128,2048]{1,0:T(8,128)(2,1)} %get-tuple-element.40.refs_0_.refs_3_.refs_4_.refs_2_.refs_8_, bf16[1,8,4,32,32,32]{5,4,3,2,1,0:T(8,128)(2,1)} %refs_1_.3, bf16[128,512]{1,0:T(8,128)(2,1)} %constant.39.clone.refs_2_), custom_call_target="tpu_custom_call" | custom-call | tf_op jit(solution)/shard_map/pack/pallas_call | solution.py:69
  32.9 1.5 %all-to-all-done = bf16[32,16,256]{2,1,0:T(8,128)(2,1)S(1)} async-done(((bf16[32,16,256]{2,1,0:T(8,128)(2,1)}), bf16[32,16,256]{2,1,0:T(8,128)(2,1)S(1)}, u32[]{:S(2)}, u32[]{:S(2)}) %all-to-all-start) | async-done | bytes 262176 | tf_op jit(solution)/shard_map/all_to_all | solution.py:871
  34.4 0.8 copy-done.6
  35.2 3.2 %mix.3 = (bf16[32,512]{1,0:T(8,128)(2,1)}, bf16[512,128]{1,0:T(8,128)(2,1)S(1)}, bf16[1024,512]{1,0:T(8,128)(2,1)S(1)}) custom-call(s32[1]{0:T(128)} %bitcast.refs_0_, bf16[512,256]{1,0:T(8,128)(2,1)S(1)} %bitcast.31, bf16[1024,512]{1,0:T(8,128)(2,1)} %get-tuple-element.41.refs_2_, bf16[4,4,256,128]{3,2,1,0:T(8,128)(2,1)} %get-tuple-element.42.refs_3_.refs_7_, ...), custom_call_target="tpu_custom_call" | custom-call | bytes 3000000 | tf_op jit(solution)/shard_map/mix/pallas_call | solution.py:69
  38.4 11.5 %all_to_all.83 = bf16[32,16,128]{2,1,0:T(8,128)(2,1)S(1)} all-to-all(bf16[32,16,128]{2,1,0:T(8,128)(2,1)S(1)} %bitcast.42), channel_id=1, replica_groups=mesh['section'=2,'gx'=4,'gy'=4] {'section','gx','gy'}, dimensions={0} | all-to-all | bytes 262144 | tf_op jit(solution)/shard_map/all_to_all | solution.py:871
  49.9 4.7 %forward.1 = (bf16[128,4096]{1,0:T(8,128)(2,1)S(1)}, f32[128,4096]{1,0:T(8,128)S(1)}, bf16[512,4096]{1,0:T(8,128)(2,1)S(1)}, bf16[512,128]{1,0:T(8,128)(2,1)S(1)}, bf16[4,4,256,128]{3,2,1,0:T(8,128)(2,1)S(1)}) custom-call(s32[1]{0:T(128)} %bitcast.refs_0_, bf16[48,32]{1,0:T(8,128)(2,1)} %copy-done.3, bf16[48,32]{1,0:T(8,128)(2,1)} %copy-done.1, ...), custom_call_target="tpu_custom_call" | custom-call | bytes 3000000 | tf_op jit(solution)/shard_map/forward/pallas_call | solution.py:69
  54.6 9.9 %all_to_all.84 = bf16[32,16,128]{2,1,0:T(8,128)(2,1)S(1)} all-to-all(bf16[32,16,128]{2,1,0:T(8,128)(2,1)S(1)} %bitcast.40), channel_id=1, replica_groups=mesh['section'=2,'gx'=4,'gy'=4] {'section','gx','gy'}, dimensions={0} | all-to-all | bytes 262144 | tf_op jit(solution)/shard_map/all_to_all | solution.py:871
  64.5 1.5 %mix.4 = (bf16[32,512]{1,0:T(8,128)(2,1)}, bf16[512,128]{1,0:T(8,128)(2,1)S(1)}) custom-call(s32[1]{0:T(128)} %bitcast.refs_0_, bf16[512,128]{1,0:T(8,128)(2,1)S(1)} %bitcast.37, bf16[1024,512]{1,0:T(8,128)(2,1)S(1)} %get-tuple-element.47.refs_2_, bf16[4,4,256,128]{3,2,1,0:T(8,128)(2,1)S(1)} %get-tuple-element.48.refs_3_), custom_call_target="tpu_custom_call" | custom-call | bytes 3000000 | tf_op jit(solution)/shard_map/mix/pallas_call | solution.py:69
  66.1 9.9 %all_to_all.85 = bf16[32,16,128]{2,1,0:T(8,128)(2,1)S(1)} all-to-all(bf16[32,16,128]{2,1,0:T(8,128)(2,1)S(1)} %bitcast.38), channel_id=1, replica_groups=mesh['section'=2,'gx'=4,'gy'=4] {'section','gx','gy'}, dimensions={0} | all-to-all | bytes 262144 | tf_op jit(solution)/shard_map/all_to_all | solution.py:871
  76.0 4.3 %turn.1 = (bf16[128,4096]{1,0:T(8,128)(2,1)S(1)}, f32[16,128]{1,0:T(8,128)S(1)}, bf16[512,128]{1,0:T(8,128)(2,1)S(1)}) custom-call(s32[1]{0:T(128)} %bitcast.refs_0_, bf16[48,32]{1,0:T(8,128)(2,1)S(1)} %copy-done.4, bf16[48,32]{1,0:T(8,128)(2,1)S(1)} %copy-done.2, bf16[512,128]{1,0:T(8,128)(2,1)S(1)} %bitcast.35, ...), custom_call_target="tpu_custom_call" | custom-call | bytes 3000000 | tf_op jit(solution)/shard_map/turn/pallas_call | solution.py:69
  80.3 9.9 %all_to_all.86 = bf16[32,16,128]{2,1,0:T(8,128)(2,1)S(1)} all-to-all(bf16[32,16,128]{2,1,0:T(8,128)(2,1)S(1)} %bitcast.41), channel_id=1, replica_groups=mesh['section'=2,'gx'=4,'gy'=4] {'section','gx','gy'}, dimensions={0} | all-to-all | bytes 262144 | tf_op jit(solution)/shard_map/all_to_all | solution.py:871
  90.3 1.7 %mix.5 = (bf16[32,512]{1,0:T(8,128)(2,1)}, bf16[512,128]{1,0:T(8,128)(2,1)S(1)}) custom-call(s32[1]{0:T(128)} %bitcast.refs_0_, bf16[512,128]{1,0:T(8,128)(2,1)S(1)} %bitcast.36, bf16[1024,512]{1,0:T(8,128)(2,1)S(1)} %get-tuple-element.47.refs_2_, bf16[4,4,256,128]{3,2,1,0:T(8,128)(2,1)S(1)} %get-tuple-element.48.refs_3_), custom_call_target="tpu_custom_call" | custom-call | bytes 3000000 | tf_op jit(solution)/shard_map/mix/pallas_call | solution.py:69
  92.0 9.9 %all_to_all.87 = bf16[32,16,128]{2,1,0:T(8,128)(2,1)S(1)} all-to-all(bf16[32,16,128]{2,1,0:T(8,128)(2,1)S(1)} %bitcast.43), channel_id=1, replica_groups=mesh['section'=2,'gx'=4,'gy'=4] {'section','gx','gy'}, dimensions={0} | all-to-all | bytes 262144 | tf_op jit(solution)/shard_map/all_to_all | solution.py:871
  101.9 3.1 %back.1 = (bf16[32,24,128]{2,1,0:T(8,128)(2,1)S(1)}, bf16[512,128]{1,0:T(8,128)(2,1)S(1)}) custom-call(s32[1]{0:T(128)} %bitcast.refs_0_, bf16[48,32]{1,0:T(8,128)(2,1)S(1)} %copy-done.4, bf16[48,32]{1,0:T(8,128)(2,1)S(1)} %copy-done.2, bf16[512,128]{1,0:T(8,128)(2,1)S(1)} %bitcast.32, bf16[128,4096]{1,0:T(8,128)(2,1)S(1)} %get-tuple-element.57.refs_4_, ...), custom_call_target="tpu_custom_call" | custom-call | bytes 3000000 | tf_op jit(solution)/shard_map/back/pallas_call | solution.py:69
  105.1 9.9 %all_to_all.88 = bf16[32,16,128]{2,1,0:T(8,128)(2,1)S(1)} all-to-all(bf16[32,16,128]{2,1,0:T(8,128)(2,1)S(1)} %bitcast.39), channel_id=1, replica_groups=mesh['section'=2,'gx'=4,'gy'=4] {'section','gx','gy'}, dimensions={0} | all-to-all | bytes 262144 | tf_op jit(solution)/shard_map/all_to_all | solution.py:871
  115.0 2.6 %all-to-all-start.7 = ((bf16[32,24,128]{2,1,0:T(8,128)(2,1)}), bf16[32,24,128]{2,1,0:T(8,128)(2,1)S(1)}, u32[]{:S(2)}, u32[]{:S(2)}) async-start(bf16[32,24,128]{2,1,0:T(8,128)(2,1)} %copy-done.5), calls=%async_computation.7 | async-start | bytes 393216 | tf_op jit(solution)/shard_map/all_to_all | solution.py:920
  117.6 1.0 spec.1
  118.7 1.1 collective-permute-done.5.refs_1_
  119.9 7.2 %outer.1.refs_1_ = f32[1,8,4,32,32,32]{5,4,3,2,1,0:T(8,128)} custom-call(bf16[2,32,512]{2,1,0:T(8,128)(2,1)S(1)} %get-tuple-element.66.refs_0_, bf16[2,32,512]{2,1,0:T(8,128)(2,1)S(1)} %collective-permute-done.5.refs_1_), custom_call_target="tpu_custom_call" | custom-call | bytes 20000000 | tf_op jit(solution)/shard_map/outer/pallas_call | solution.py:854
  127.1 0.2 all-to-all-done.7.refs_0_
  127.4 0.7 finish.1
  (28 shorter events, 0.6 us)
Async XLA Ops:
  0.6 1.6 %copy-start = (bf16[1,32,16,16,128]{4,3,2,1,0:T(8,128)(2,1)S(1)}, bf16[1,32,16,16,128]{4,3,2,1,0:T(8,128)(2,1)}, u32[]{:S(2)}) copy-start(bf16[1,32,16,16,128]{4,3,2,1,0:T(8,128)(2,1)} %param.7) | copy-start | bytes 6291460
  3.3 3.0 %collective-permute-start.1 = (bf16[256,2048]{1,0:T(8,128)(2,1)}, bf16[256,2048]{1,0:T(8,128)(2,1)S(1)}, u32[]{:S(2)}, u32[]{:S(2)}) collective-permute-start(bf16[256,2048]{1,0:T(8,128)(2,1)} %dynamic-slice_bitcast_fusion.1), channel_id=1, source_target_pairs={{0,16},{16,0},{1,17},{17,1},{2,18},{18,2},{3,19},{19,3},{4,20},{20... | collective-permute-start | bytes 3145736 | tf_op jit(solution)/shard_map/ppermute | solution.py:875
  11.5 13.0 %copy-start.8 = (bf16[1,32]{1,0:T(2,128)(2,1)S(1)}, bf16[1,32]{1,0:T(2,128)(2,1)}, u32[]{:S(2)}) copy-start(bf16[1,32]{1,0:T(2,128)(2,1)} %param.10) | copy-start | bytes 196
  11.6 13.0 %copy-start.7 = (bf16[1,32,32]{2,1,0:T(8,128)(2,1)S(1)}, bf16[1,32,32]{2,1,0:T(8,128)(2,1)}, u32[]{:S(2)}) copy-start(bf16[1,32,32]{2,1,0:T(8,128)(2,1)} %param.9) | copy-start | bytes 6148
  11.6 22.9 %collective-permute-start.2 = (bf16[4,4,256,128]{3,2,1,0:T(8,128)(2,1)}, bf16[4,4,256,128]{3,2,1,0:T(8,128)(2,1)}, u32[]{:S(2)}, u32[]{:S(2)}) collective-permute-start(bf16[4,4,256,128]{3,2,1,0:T(8,128)(2,1)} %get-tuple-element.43), channel_id=1, source_target_pairs={{0,16},{16,0},{1,17},{17,1},{2,18},{18,2},{3,19},{19,3},{4,20},{20... | collective-permute-start | bytes 3145736 | tf_op jit(solution)/shard_map/ppermute | solution.py:875
  12.0 22.4 %collective-permute-start.3 = (bf16[128,2048]{1,0:T(8,128)(2,1)}, bf16[128,2048]{1,0:T(8,128)(2,1)S(1)}, u32[]{:S(2)}, u32[]{:S(2)}) collective-permute-start(bf16[128,2048]{1,0:T(8,128)(2,1)} %get-tuple-element.44), channel_id=1, source_target_pairs={{0,4},{4,0},{8,12},{12,8},{1,5},{5,1},{9,13},{13,9},{2,6},{6,2},{1... | collective-permute-start | bytes 1572872 | tf_op jit(solution)/shard_map/ppermute | solution.py:879
  14.7 19.7 %all-to-all-start = ((bf16[32,16,256]{2,1,0:T(8,128)(2,1)}), bf16[32,16,256]{2,1,0:T(8,128)(2,1)S(1)}, u32[]{:S(2)}, u32[]{:S(2)}) async-start(bf16[32,16,256]{2,1,0:T(8,128)(2,1)} %bitcast.44), calls=%async_computation | async-start | bytes 524288 | tf_op jit(solution)/shard_map/all_to_all | solution.py:871
  22.7 43.4 %collective-permute-start.4 = (bf16[128,2048]{1,0:T(8,128)(2,1)}, bf16[128,2048]{1,0:T(8,128)(2,1)}, u32[]{:S(2)}, u32[]{:S(2)}) collective-permute-start(bf16[128,2048]{1,0:T(8,128)(2,1)} %get-tuple-element.51), channel_id=1, source_target_pairs={{0,4},{4,0},{8,12},{12,8},{1,5},{5,1},{9,13},{13,9},{2,6},{6,2},{1... | collective-permute-start | bytes 1572872 | tf_op jit(solution)/shard_map/ppermute | solution.py:879
  24.6 4.5 %copy-start.3 = (bf16[48,32]{1,0:T(8,128)(2,1)}, bf16[48,32]{1,0:T(8,128)(2,1)S(1)}, u32[]{:S(2)}) copy-start(bf16[48,32]{1,0:T(8,128)(2,1)S(1)} %pad_maximum_fusion.refs_1_) | copy-start | bytes 9220
  24.6 8.3 %collective-permute-start = (bf16[48,32]{1,0:T(8,128)(2,1)S(1)}, bf16[48,32]{1,0:T(8,128)(2,1)S(1)}, u32[]{:S(2)}, u32[]{:S(2)}) collective-permute-start(bf16[48,32]{1,0:T(8,128)(2,1)S(1)} %pad_maximum_fusion.refs_1_), channel_id=1, source_target_pairs={{0,16},{16,0},{1,17},{17,1},{2,18},{18,2},{3,19},{19,3},{4,20},{20... | collective-permute-start | bytes 9224 | tf_op jit(solution)/shard_map/ppermute | solution.py:875
  32.9 2.3 %copy-start.1 = (bf16[48,32]{1,0:T(8,128)(2,1)}, bf16[48,32]{1,0:T(8,128)(2,1)S(1)}, u32[]{:S(2)}) copy-start(bf16[48,32]{1,0:T(8,128)(2,1)S(1)} %collective-permute-done.refs_5_.refs_2_) | copy-start | bytes 9220
  34.4 0.8 copy-start.6
  54.6 21.4 %copy-start.2 = (bf16[48,32]{1,0:T(8,128)(2,1)S(1)}, bf16[48,32]{1,0:T(8,128)(2,1)}, u32[]{:S(2)}) copy-start(bf16[48,32]{1,0:T(8,128)(2,1)} %copy-done.1) | copy-start | bytes 9220
  54.6 21.4 %copy-start.4 = (bf16[48,32]{1,0:T(8,128)(2,1)S(1)}, bf16[48,32]{1,0:T(8,128)(2,1)}, u32[]{:S(2)}) copy-start(bf16[48,32]{1,0:T(8,128)(2,1)} %copy-done.3) | copy-start | bytes 9220
  105.0 9.9 %copy-start.5 = (bf16[32,24,128]{2,1,0:T(8,128)(2,1)}, bf16[32,24,128]{2,1,0:T(8,128)(2,1)S(1)}, u32[]{:S(2)}) copy-start(bf16[32,24,128]{2,1,0:T(8,128)(2,1)S(1)} %get-tuple-element.68) | copy-start | bytes 589828
  115.0 12.4 %all-to-all-start.7 = ((bf16[32,24,128]{2,1,0:T(8,128)(2,1)}), bf16[32,24,128]{2,1,0:T(8,128)(2,1)S(1)}, u32[]{:S(2)}, u32[]{:S(2)}) async-start(bf16[32,24,128]{2,1,0:T(8,128)(2,1)} %copy-done.5), calls=%async_computation.7 | async-start | bytes 393216 | tf_op jit(solution)/shard_map/all_to_all | solution.py:920
  118.6 1.3 %collective-permute-start.5 = (bf16[2,32,512]{2,1,0:T(8,128)(2,1)S(1)}, bf16[2,32,512]{2,1,0:T(8,128)(2,1)S(1)}, u32[]{:S(2)}, u32[]{:S(2)}) collective-permute-start(bf16[2,32,512]{2,1,0:T(8,128)(2,1)S(1)} %get-tuple-element.67), channel_id=1, source_target_pairs={{0,16},{16,0},{1,17},{17,1},{2,18},{18,2},{3,19},{19,3},{4,20},{20... | collective-permute-start | bytes 196616 | tf_op jit(solution)/shard_map/ppermute | solution.py:875
